TPU v7x, 256 devices: a whole 4x4x8 slice. The times are simulated.
256 devices in a mesh: seq: 32 (over z_hi, x, core), head: 8 (over y, z_lo).
Axes of the slice: x: 4, y: 4, z: 8 (z_hi: 4, z_lo: 2; z = z_hi * 2 + z_lo), core: 2. Of those that a mesh axis runs over, the one named last changes fastest.
Arguments:
- queries: bfloat16 [24576, 4096], P('seq', 'head'), may hold values from -100 to 100
- keys: bfloat16 [24576, 4096], P('seq', 'head'), may hold values from -7 to 7
- values: bfloat16 [24576, 4096], P('seq', 'head'), may hold values from -6 to 6
- targets: bfloat16 [24576, 4096], P('seq', 'head'), may hold values from -6 to 6
- token_rate: float32 [24576, 8], P('seq', 'head'), may hold values from 0.1 to 1
- window: int32 [8], P('head'), may hold values from 256 to 512, as said below
- split: int32 [1], replicated, may hold values from 9216 to 15359
- fast_init: float32 [8, 3, 512, 512], P('head'), may hold values from -0.25 to 0.25
Outputs:
- mixed: bfloat16 [24576, 4096], P('seq', 'head')
- fast_final: float32 [8, 3, 512, 512], P('head')
Inputs may be any that keep to these rules, and one draw needn't show every extreme that they name: Some head has a window of exactly 512.
All inputs are finite; a program needn't handle non-finite values.
Results may differ from a plain program's by a relative error of at most 0.0073.
Values may be sent and summed in bfloat16 or wider, within the bound.
No kernel may reach another device: no remote copies, remote signals or barrier semaphores. Data moves between devices by JAX's collectives and lax.ppermute only.
A program may use at most 64 MiB of HBM per device.

v0:
```python
import functools
import math

import jax
import jax.numpy as jnp
from jax import lax
from jax.experimental import pallas as pl
from jax.experimental.pallas import tpu as pltpu
from jax.sharding import Mesh
from jax.sharding import PartitionSpec as P

HEADS = 8
HD = 512
HID = 512
WIN = 512
ROWS = 3 * HD
SEQ = ("z", "x", "core")
TILE = 256
CHUNKS = 2
SHARES = 64

fast_rate = 0.01
epsilon = 1e-06
bf16 = jnp.bfloat16
f32 = jnp.float32
VMEM_SPEC = pl.BlockSpec(memory_space=pltpu.VMEM)
SMEM_SPEC = pl.BlockSpec(memory_space=pltpu.SMEM)
ANY_SPEC = pl.BlockSpec(memory_space=pl.ANY)
HBM_SPEC = pl.BlockSpec(memory_space=pltpu.HBM)


def dot(a, b, over_a, over_b):
    return lax.dot_general(a, b, (((over_a,), (over_b,)), ((), ())), preferred_element_type=f32)


def exchange(value, mesh_axes, partner):
    count = math.prod(lax.axis_size(a) for a in mesh_axes)
    return lax.ppermute(value, mesh_axes, [(i, partner(i)) for i in range(count)])


def ring_pair(step):
    def partner(i):
        place, core = divmod(i, 2)
        return (place ^ (1 if core == step else 3)) * 2 + core

    return partner


def swap_x(value, step):
    return exchange(value, ("x", "core"), ring_pair(step))


def swap_z(value, step):
    return exchange(value, ("z", "core"), ring_pair(step))


def swap_core(value):
    return exchange(value, ("core",), lambda i: i ^ 1)


def spread(squares):
    return lax.all_to_all(squares, ("x", "core", "head"), 0, 0, tiled=True)


def rows_of(value, start, count):
    return lax.dynamic_slice_in_dim(value, start, count, 0)


def halves():
    core = lax.axis_index("core")
    place = lax.axis_index("x")
    low, high = place & 1, place >> 1
    first = jnp.where(core == 0, low ^ high, high)
    second = jnp.where(core == 0, high, low ^ high)
    return core, first, second


def piece_starts():
    core, a, b = halves()
    here = [(a, b), (a, 1 - b), (1 - a, b), (1 - a, 1 - b)]
    there = [(b, a), (b, 1 - a), (1 - b, a), (1 - b, 1 - a)]
    places = [core * 4 + i * 2 + j for i, j in here] + [(1 - core) * 4 + i * 2 + j for i, j in there]
    return (jnp.stack(places) * (ROWS // 8)).astype(jnp.int32)


def reduced(sent, own, before_z=None, beside_first=None, beside_second=None):
    _, first, second = halves()
    half, rows = ROWS // 4, ROWS // 8
    chunks = range(len(sent))
    got = [swap_core(s) for s in sent]

    def two(c, start, count):
        return rows_of(own[c], start, count) + rows_of(got[c], start, count).astype(f32)

    got_x = [swap_x(two(c, (1 - first) * half, half).astype(bf16), 0) for c in chunks]
    away = (1 - second) * rows
    send = [(two(c, first * half + away, rows) + rows_of(got_x[c], away, rows).astype(f32)).astype(bf16) for c in chunks]
    got_x2 = [swap_x(s, 1) for s in send]
    near = second * rows
    mine = [two(c, first * half + near, rows) + rows_of(got_x[c], near, rows).astype(f32) + got_x2[c].astype(f32) for c in chunks]
    mine = [m.astype(bf16) for m in mine]
    if before_z is not None:
        mine = before_z(mine)
    other = [swap_z(m, 0) for m in mine]
    if beside_first is not None:
        other = beside_first(mine, other)
    mine = [(m.astype(f32) + o.astype(f32)).astype(bf16) for m, o in zip(mine, other)]
    other = [swap_z(m, 1) for m in mine]
    if beside_second is not None:
        other = beside_second(mine, other)
    return mine, other


def gathered(own):
    near = swap_x(own, 1)
    pair = jnp.concatenate([own, near], axis=0)
    far = swap_x(pair, 0)
    return [pair, far, swap_core(pair), swap_core(far)]


def finish_kernel(*refs):
    total_ref, square_ref = refs[2 * CHUNKS :]
    wide = HID // CHUNKS
    for c in range(CHUNKS):
        total = refs[c][...].astype(f32) + refs[CHUNKS + c][...].astype(f32)
        total_ref[:, c * wide : (c + 1) * wide] = total.astype(bf16)
        square = jnp.sum(total * total, axis=0, keepdims=True)
        square = square if c == 0 else before + square
        before = square
    square_ref[...] = jnp.broadcast_to(jnp.sum(square, axis=1, keepdims=True), (8, 128))[None] + jnp.zeros(square_ref.shape, f32)


def fetch(sources, targets, sem):
    copies = [pltpu.make_async_copy(a, b, sem.at[i]) for i, (a, b) in enumerate(zip(sources, targets))]
    for copy in copies:
        copy.start()
    return copies


def grads(place, keys_ref, targets_ref, rate_ref, wb_ref, grad_ref, outs):
    keys = keys_ref[...]
    d_out = (-rate_ref[...] * targets_ref[...].astype(f32)).astype(bf16)
    half, wide = ROWS // 2, HID // CHUNKS
    for c in range(CHUNKS):
        cols = slice(c * wide, (c + 1) * wide)
        first = dot(keys, wb_ref[0:HD, cols], 1, 0)
        third = dot(keys, wb_ref[HD : 2 * HD, cols], 1, 0)
        d_act = dot(d_out, wb_ref[2 * HD :, cols], 1, 0)
        sigma = jax.nn.sigmoid(first)
        swish = first * sigma
        act = (swish * third).astype(bf16)
        d_first = (d_act * third * sigma * (1.0 + first * (1.0 - sigma))).astype(bf16)
        d_third = (d_act * swish).astype(bf16)
        grad_ref[0:HD] = dot(keys, d_first, 0, 0)
        grad_ref[HD : 2 * HD] = dot(keys, d_third, 0, 0)
        grad_ref[2 * HD :] = dot(d_out, act, 0, 0)
        outs[c][...] = grad_ref[pl.ds(pl.multiple_of((1 - place) * half, half), half)].astype(bf16)
        outs[CHUNKS + c][...] = grad_ref[pl.ds(pl.multiple_of(place * half, half), half)]


def first_kernel(place_ref, keys_hbm, targets_hbm, rate_ref, w_hbm, wb_hbm, *rest):
    outs, (grad_ref, keys_ref, targets_ref, w_ref, wb_ref, sem) = rest[: 2 * CHUNKS], rest[2 * CHUNKS :]
    thirds = [pl.ds(i * HD, HD) for i in range(3)]
    copies = fetch(
        [w_hbm.at[t] for t in thirds] + [keys_hbm, targets_hbm],
        [w_ref.at[t] for t in thirds] + [keys_ref, targets_ref],
        sem,
    )
    for copy, third in zip(copies, thirds):
        copy.wait()
        wb_ref[third] = w_ref[third].astype(bf16)
    leave = pltpu.make_async_copy(wb_ref, wb_hbm, sem.at[5])
    leave.start()
    copies[3].wait()
    copies[4].wait()
    grads(place_ref[0], keys_ref, targets_ref, rate_ref, wb_ref, grad_ref, outs)
    leave.wait()


def piece_rows(starts_ref):
    rows = ROWS // 8
    return [pl.ds(pl.multiple_of(starts_ref[i], rows), rows) for i in range(8)]


def renew(starts_ref, square_ref, w_ref, pieces, new_ref, out_ref, sem, wb_ref=None, arrive=None):
    mean = jnp.sum(square_ref[...], axis=0)[0:1, 0:1] / float(HEADS * ROWS * HID)
    factor = fast_rate / jnp.sqrt(mean + epsilon)
    rows = ROWS // 8
    copies = []
    for i, at in enumerate(piece_rows(starts_ref)):
        if arrive is not None:
            arrive[i].wait()
        new = w_ref[at] - factor * pieces[i // 2][i % 2 * rows : (i % 2 + 1) * rows].astype(f32)
        new_ref[at] = new
        copies.append(pltpu.make_async_copy(new_ref.at[at], out_ref.at[at], sem.at[i]))
        copies[-1].start()
        if wb_ref is not None:
            wb_ref[at] = new.astype(bf16)
    return copies


def second_kernel(place_ref, starts_ref, square_ref, keys_hbm, targets_hbm, rate_ref, w_hbm, *rest):
    pieces, (out_ref, wb_ref, *outs) = rest[:4], rest[4 : 6 + 2 * CHUNKS]
    grad_ref, new_ref, sem, keys_ref, targets_ref, w_ref, fetched = rest[6 + 2 * CHUNKS :]
    spans = piece_rows(starts_ref)
    arrive = fetch(
        [w_hbm.at[at] for at in spans] + [keys_hbm, targets_hbm],
        [w_ref.at[at] for at in spans] + [keys_ref, targets_ref],
        fetched,
    )
    copies = renew(starts_ref, square_ref, w_ref, pieces, new_ref, out_ref, sem, wb_ref, arrive)
    for copy in arrive[8:]:
        copy.wait()
    grads(place_ref[0], keys_ref, targets_ref, rate_ref, wb_ref, grad_ref, outs)
    for copy in copies:
        copy.wait()


def last_kernel(starts_ref, square_ref, w_ref, *rest):
    pieces, (out_ref, new_ref, sem) = rest[:4], rest[4:]
    for copy in renew(starts_ref, square_ref, w_ref, pieces, new_ref, out_ref, sem):
        copy.wait()


def attend_kernel(meta_ref, q_ref, halo_k_ref, k_ref, halo_v_ref, v_ref, out_ref):
    local = q_ref.shape[0]
    anchor, width = meta_ref[0], meta_ref[1]
    scale = HD ** (-0.5)
    held = [(halo_k_ref, halo_v_ref, -WIN, WIN), (k_ref, v_ref, 0, local)]
    for start in range(0, local, TILE):
        spans = []
        for keys, values, base, count in held:
            low, high = max(base, start - WIN), min(base + count, start + TILE)
            if low < high:
                spans.append((keys, values, low - base, high - base, low))
        query = q_ref[start : start + TILE]
        scores = []
        for keys, _, low, high, position in spans:
            s = dot(query, keys[low:high], 1, 1) * scale
            row = lax.broadcasted_iota(jnp.int32, s.shape, 0) + start
            col = lax.broadcasted_iota(jnp.int32, s.shape, 1) + position
            live = (col <= row) & (col > row - width) & (col >= -anchor)
            scores.append(jnp.where(live, s, -1e30))
        peak = functools.reduce(jnp.maximum, [jnp.max(s, axis=1, keepdims=True) for s in scores])
        expo = [jnp.exp(s - peak) for s in scores]
        total = sum(jnp.sum(e, axis=1, keepdims=True) for e in expo)
        inverse = 1.0 / total
        attn = 0.0
        for e, (_, values, low, high, _) in zip(expo, spans):
            attn = attn + dot((e * inverse).astype(bf16), values[low:high], 1, 0)
        out_ref[start : start + TILE] = attn


def apply_kernel(meta_ref, q_ref, attn_ref, early_ref, late_ref, out_ref, y_ref):
    anchor, split = meta_ref[0], meta_ref[2]

    def fast(query, wb_ref):
        first = dot(query, wb_ref[0:HD], 1, 0)
        third = dot(query, wb_ref[HD : 2 * HD], 1, 0)
        act = (first * jax.nn.sigmoid(first) * third).astype(bf16)
        return dot(act, wb_ref[2 * HD :], 1, 1)

    def tile(i, carry):
        start = pl.multiple_of(i * TILE, TILE)
        rows = pl.ds(start, TILE)

        @pl.when(anchor + start < split)
        def _():
            y_ref[...] = fast(q_ref[rows], early_ref)

        @pl.when(anchor + start + TILE > split)
        def _():
            late = fast(q_ref[rows], late_ref)
            position = anchor + start + lax.broadcasted_iota(jnp.int32, late.shape, 0)
            y_ref[...] = jnp.where(position < split, y_ref[...], late)

        y = y_ref[...]
        norm = y / jnp.sqrt(jnp.mean(y * y, axis=1, keepdims=True) + epsilon)
        out_ref[rows] = (attn_ref[rows] + norm).astype(bf16)
        return carry

    lax.fori_loop(0, q_ref.shape[0] // TILE, tile, 0)


def call(kernel, specs, outs, args, megabytes, scratch=(), out_specs=None):
    return pl.pallas_call(
        kernel,
        out_shape=outs,
        in_specs=specs,
        out_specs=jax.tree.map(lambda _: VMEM_SPEC, outs) if out_specs is None else out_specs,
        scratch_shapes=list(scratch),
        compiler_params=pltpu.CompilerParams(vmem_limit_bytes=megabytes << 20),
    )(*args)


def in_hbm(value):
    return pltpu.with_memory_space_constraint(value, pltpu.HBM)


def array(shape, dtype):
    return jax.ShapeDtypeStruct(shape, dtype)


def per_device(queries, keys, values, targets, token_rate, window, split, fast_init):
    local = queries.shape[0]
    anchor = lax.axis_index(SEQ) * local
    count = lax.axis_size(SEQ)
    onward = [(i, i + 1) for i in range(count - 1)]
    halo_k = lax.ppermute(keys[local - WIN :], SEQ, onward)
    halo_v = lax.ppermute(values[local - WIN :], SEQ, onward)
    positions = anchor + jnp.arange(local, dtype=jnp.int32)[:, None]
    first_block = (positions < split[0]).astype(f32)
    rate_zero = token_rate * first_block
    rate_one = token_rate * (1.0 - first_block)
    core = lax.axis_index("core").astype(jnp.int32).reshape(1)
    starts = piece_starts()
    meta = jnp.stack([anchor, window[0], split[0]]).astype(jnp.int32)
    weights_zero = fast_init.reshape(ROWS, HID)
    half = ROWS // 2
    wide = [array((half, HID // CHUNKS), kind) for kind in (bf16, f32) for _ in range(CHUNKS)]
    grad = pltpu.VMEM((ROWS, HID // CHUNKS), f32)
    renewal = [pltpu.VMEM((ROWS, HID), f32), pltpu.SemaphoreType.DMA((8,))]

    fetched = [pltpu.VMEM((local, HD), bf16)] * 2

    wb_zero, *halved = call(
        first_kernel,
        [SMEM_SPEC, HBM_SPEC, HBM_SPEC, VMEM_SPEC, HBM_SPEC],
        [pltpu.HBM((ROWS, HID), bf16)] + wide,
        (core, in_hbm(keys), in_hbm(targets), rate_zero, in_hbm(weights_zero)),
        24,
        [grad] + fetched + [pltpu.VMEM((ROWS, HID), f32), pltpu.VMEM((ROWS, HID), bf16), pltpu.SemaphoreType.DMA((6,))],
        [HBM_SPEC] + [VMEM_SPEC] * (2 * CHUNKS),
    )

    def finished(mine, other):
        total, square = call(
            finish_kernel,
            [VMEM_SPEC] * (2 * CHUNKS),
            [array((ROWS // 8, HID), bf16), array((SHARES, 8, 128), f32)],
            (*mine, *other),
            8,
        )
        return spread(square), gathered(total)

    kept = {}

    def have_keys(mine):
        kept["halo"], mine = lax.optimization_barrier((halo_k, mine))
        return mine

    square, pieces = finished(*reduced(halved[:CHUNKS], halved[CHUNKS:], have_keys))
    weights_one, wb_one, *halved = call(
        second_kernel,
        [SMEM_SPEC] * 2 + [VMEM_SPEC, HBM_SPEC, HBM_SPEC, VMEM_SPEC, HBM_SPEC] + [VMEM_SPEC] * 4,
        [pltpu.HBM((ROWS, HID), f32), array((ROWS, HID), bf16)] + wide,
        (core, starts, square, in_hbm(keys), in_hbm(targets), rate_one, in_hbm(weights_zero), *pieces),
        24,
        [grad] + renewal + fetched + [pltpu.VMEM((ROWS, HID), f32), pltpu.SemaphoreType.DMA((10,))],
        [HBM_SPEC] + [VMEM_SPEC] * (1 + 2 * CHUNKS),
    )
    def attend(before, after):
        query, _ = lax.optimization_barrier((queries, before))
        attn = call(
            attend_kernel,
            [SMEM_SPEC] + [VMEM_SPEC] * 5,
            array((local, HD), f32),
            (meta, query, kept["halo"], keys, halo_v, values),
            20,
        )
        kept["attn"], after = lax.optimization_barrier((attn, after))
        return after

    def apply(before, after):
        query, _ = lax.optimization_barrier((queries, before))
        outputs = call(
            apply_kernel,
            [SMEM_SPEC] + [VMEM_SPEC] * 4,
            array((local, HD), bf16),
            (meta, query, kept["attn"], wb_zero, wb_one),
            20,
            [pltpu.VMEM((TILE, HD), f32)],
        )
        kept["outputs"], after = lax.optimization_barrier((outputs, after))
        return after

    square, pieces = finished(*reduced(halved[:CHUNKS], halved[CHUNKS:], None, attend, apply))
    weights_two = call(
        last_kernel,
        [SMEM_SPEC] + [VMEM_SPEC] * 6,
        array((ROWS, HID), f32),
        (starts, square, weights_one, *pieces),
        20,
        renewal,
        ANY_SPEC,
    )
    return (kept["outputs"], weights_two.reshape(1, 3, HD, HID))


def solution(mesh):
    finer = Mesh(mesh.devices.reshape(4, 4, 2, mesh.shape["head"]), ("z", "x", "core", "head"))
    tokens = P(SEQ, "head")
    weights = P("head", None, None, None)
    return jax.shard_map(
        per_device,
        mesh=finer,
        in_specs=(tokens,) * 5 + (P("head"), P(), weights),
        out_specs=(tokens, weights),
        check_vma=False,
    )
```

profile of v0, /device:TPU:1, one launch (start us, length us, event | category | flops | bytes accessed | tf_op | source)
XLA Modules:
  0.0 160.9 jit_solution(17660663697776447134)
XLA Ops:
  2.3 5.9 %shard_map.95 = (bf16[1536,512]{1,0:T(8,128)(2,1)}, bf16[768,256]{1,0:T(8,128)(2,1)S(1)}, bf16[768,256]{1,0:T(8,128)(2,1)S(1)}, f32[768,256]{1,0:T(8,128)S(1)}, f32[768,256]{1,0:T(8,128)S(1)}) custom-call(s32[1]{0:T(128)} %bitcast.1.place_ref, bf16[768,512]{1,0:T(8,128)(2,1)} %k_ref.1, bf16[768,512]{1,0:T(8,128)(2,1)} %targets_hbm.3, ...), custom_call_target="tpu_custom_call" | custom-call | tf_op jit(solution)/shard_map/pallas_call | solution.py:286
  8.1 3.3 %collective-permute-start.1 = (bf16[768,256]{1,0:T(8,128)(2,1)S(1)}, bf16[768,256]{1,0:T(8,128)(2,1)}, u32[]{:S(2)}, u32[]{:S(2)}) collective-permute-start(bf16[768,256]{1,0:T(8,128)(2,1)S(1)} %get-tuple-element.29), channel_id=1, source_target_pairs={{0,8},{8,0},{1,9},{9,1},{2,10},{10,2},{3,11},{11,3},{4,12},{12,4},... | collective-permute-start | bytes 1179656 | tf_op jit(solution)/shard_map/ppermute | solution.py:38
  13.0 1.6 %add_convert_fusion.3 = bf16[384,256]{1,0:T(8,128)(2,1)} fusion(f32[768,256]{1,0:T(8,128)S(1)} %get-tuple-element.28, s32[]{:T(128)S(6)} %select_n.24, bf16[768,256]{1,0:T(8,128)(2,1)} %collective-permute-done.1), kind=kLoop, calls=%fused_computation.4 | loop fusion | flops 294912 | bytes 786436 | tf_op jit(solution)/shard_map/convert_element_type | solution.py:95
  15.4 1.6 %add_convert_fusion.2 = bf16[384,256]{1,0:T(8,128)(2,1)} fusion(f32[768,256]{1,0:T(8,128)S(1)} %get-tuple-element.30, s32[]{:T(128)S(6)} %select_n.24, bf16[768,256]{1,0:T(8,128)(2,1)} %collective-permute-done.4), kind=kLoop, calls=%fused_computation.3 | loop fusion | flops 294912 | bytes 786436 | tf_op jit(solution)/shard_map/convert_element_type | solution.py:95
  17.0 1.9 %collective-permute-start.5 = (bf16[384,256]{1,0:T(8,128)(2,1)}, bf16[384,256]{1,0:T(8,128)(2,1)}, u32[]{:S(2)}, u32[]{:S(2)}) collective-permute-start(bf16[384,256]{1,0:T(8,128)(2,1)} %add_convert_fusion.2), channel_id=1, source_target_pairs={{0,16},{8,56},{16,0},{24,40},{32,48},{40,24},{48,32},{56,8},{1,17}... | collective-permute-start | bytes 589832 | tf_op jit(solution)/shard_map/ppermute | solution.py:38
  19.8 1.9 %collective-permute-start = (bf16[512,512]{1,0:T(8,128)(2,1)}, bf16[512,512]{1,0:T(8,128)(2,1)S(1)}, u32[]{:S(2)}, u32[]{:S(2)}) collective-permute-start(bf16[512,512]{1,0:T(8,128)(2,1)} %slice.6), channel_id=1, source_target_pairs={{0,8},{8,16},{16,24},{24,32},{32,40},{40,48},{48,56},{56,64},{64,7... | collective-permute-start | bytes 1572872 | tf_op jit(solution)/shard_map/ppermute | solution.py:309
  25.3 3.8 %collective-permute-done.3 = bf16[192,256]{1,0:T(8,128)(2,1)S(1)} collective-permute-done((bf16[192,256]{1,0:T(8,128)(2,1)S(1)}, bf16[192,256]{1,0:T(8,128)(2,1)S(1)}, u32[]{:S(2)}, u32[]{:S(2)}) %collective-permute-start.3) | collective-permute-done | bytes 98336 | tf_op jit(solution)/shard_map/ppermute | solution.py:38
  31.1 5.2 %collective-permute-start.7 = (bf16[192,256]{1,0:T(8,128)(2,1)S(1)}, bf16[192,256]{1,0:T(8,128)(2,1)S(1)}, u32[]{:S(2)}, u32[]{:S(2)}) collective-permute-start(bf16[192,256]{1,0:T(8,128)(2,1)S(1)} %add_convert_fusion.14), channel_id=1, source_target_pairs={{0,64},{8,200},{64,0},{72,136},{128,192},{136,72},{192,128},{200,8... | collective-permute-start | bytes 294920 | tf_op jit(solution)/shard_map/ppermute | solution.py:38
  36.4 2.4 %collective-permute-done.7 = bf16[192,256]{1,0:T(8,128)(2,1)S(1)} collective-permute-done((bf16[192,256]{1,0:T(8,128)(2,1)S(1)}, bf16[192,256]{1,0:T(8,128)(2,1)S(1)}, u32[]{:S(2)}, u32[]{:S(2)}) %collective-permute-start.7) | collective-permute-done | bytes 98336 | tf_op jit(solution)/shard_map/ppermute | solution.py:38
  38.8 1.8 %collective-permute-start.9 = (bf16[192,256]{1,0:T(8,128)(2,1)S(1)}, bf16[192,256]{1,0:T(8,128)(2,1)S(1)}, u32[]{:S(2)}, u32[]{:S(2)}) collective-permute-start(bf16[192,256]{1,0:T(8,128)(2,1)S(1)} %add_convert_fusion.11.refs_0_), channel_id=1, source_target_pairs={{0,192},{8,72},{64,128},{72,8},{128,64},{136,200},{192,0},{200,136... | collective-permute-start | bytes 294920 | tf_op jit(solution)/shard_map/ppermute | solution.py:38
  42.0 2.3 %collective-permute-start.10 = (bf16[192,256]{1,0:T(8,128)(2,1)S(1)}, bf16[192,256]{1,0:T(8,128)(2,1)S(1)}, u32[]{:S(2)}, u32[]{:S(2)}) collective-permute-start(bf16[192,256]{1,0:T(8,128)(2,1)S(1)} %add_convert_fusion.10.refs_1_), channel_id=1, source_target_pairs={{0,192},{8,72},{64,128},{72,8},{128,64},{136,200},{192,0},{200,136... | collective-permute-start | bytes 294920 | tf_op jit(solution)/shard_map/ppermute | solution.py:38
  44.3 2.7 %collective-permute-done.9.refs_2_ = bf16[192,256]{1,0:T(8,128)(2,1)S(1)} collective-permute-done((bf16[192,256]{1,0:T(8,128)(2,1)S(1)}, bf16[192,256]{1,0:T(8,128)(2,1)S(1)}, u32[]{:S(2)}, u32[]{:S(2)}) %collective-permute-start.9) | collective-permute-done | bytes 98336 | tf_op jit(solution)/shard_map/ppermute | solution.py:38
  47.0 2.1 %collective-permute-done.10.refs_3_ = bf16[192,256]{1,0:T(8,128)(2,1)S(1)} collective-permute-done((bf16[192,256]{1,0:T(8,128)(2,1)S(1)}, bf16[192,256]{1,0:T(8,128)(2,1)S(1)}, u32[]{:S(2)}, u32[]{:S(2)}) %collective-permute-start.10) | collective-permute-done | bytes 98336 | tf_op jit(solution)/shard_map/ppermute | solution.py:38
  51.2 3.5 %collective-permute-done.11 = bf16[192,512]{1,0:T(8,128)(2,1)S(1)} collective-permute-done((bf16[192,512]{1,0:T(8,128)(2,1)S(1)}, bf16[192,512]{1,0:T(8,128)(2,1)S(1)}, u32[]{:S(2)}, u32[]{:S(2)}) %collective-permute-start.11) | collective-permute-done | bytes 196640 | tf_op jit(solution)/shard_map/ppermute | solution.py:38
  54.8 6.6 %collective-permute-start.12 = (bf16[384,512]{1,0:T(8,128)(2,1)S(1)}, bf16[384,512]{1,0:T(8,128)(2,1)S(1)}, u32[]{:S(2)}, u32[]{:S(2)}) collective-permute-start(bf16[384,512]{1,0:T(8,128)(2,1)S(1)} %constant_dynamic-update-slice_fusion.rest_0_), channel_id=1, source_target_pairs={{0,16},{8,56},{16,0},{24,40},{32,48},{40,24},{48,32},{56,8},{1,17}... | collective-permute-start | bytes 1179656 | tf_op jit(solution)/shard_map/ppermute | solution.py:38
  61.4 15.9 %all-to-all-start = ((f32[64,8,128]{2,1,0:T(8,128)}), f32[64,8,128]{2,1,0:T(8,128)S(1)}, u32[]{:S(2)}, u32[]{:S(2)}) async-start(f32[64,8,128]{2,1,0:T(8,128)} %get-tuple-element.34), calls=%async_computation | async-start | bytes 524288 | tf_op jit(solution)/shard_map/all_to_all | solution.py:62
  78.3 8.8 %all-to-all-done.square_ref = f32[64,8,128]{2,1,0:T(8,128)S(1)} async-done(((f32[64,8,128]{2,1,0:T(8,128)}), f32[64,8,128]{2,1,0:T(8,128)S(1)}, u32[]{:S(2)}, u32[]{:S(2)}) %all-to-all-start) | async-done | bytes 262176 | tf_op jit(solution)/shard_map/all_to_all | solution.py:62
  87.1 7.3 %shard_map.97 = (f32[1536,512]{1,0:T(8,128)}, bf16[1536,512]{1,0:T(8,128)(2,1)S(1)}, bf16[768,256]{1,0:T(8,128)(2,1)S(1)}, bf16[768,256]{1,0:T(8,128)(2,1)S(1)},...) custom-call(s32[1]{0:T(128)} %bitcast.1.place_ref, s32[8]{0:T(128)S(1)} %broadcast_multiply_fusion.starts_ref, ...), custom_call_target="tpu_custom_call" | custom-call | tf_op jit(solution)/shard_map/pallas_call | solution.py:286
  97.2 2.0 %collective-permute-start.19 = (bf16[384,256]{1,0:T(8,128)(2,1)S(1)}, bf16[384,256]{1,0:T(8,128)(2,1)S(1)}, u32[]{:S(2)}, u32[]{:S(2)}) collective-permute-start(bf16[384,256]{1,0:T(8,128)(2,1)S(1)} %add_convert_fusion), channel_id=1, source_target_pairs={{0,16},{8,56},{16,0},{24,40},{32,48},{40,24},{48,32},{56,8},{1,17}... | collective-permute-start | bytes 589832 | tf_op jit(solution)/shard_map/ppermute | solution.py:38
  99.2 1.9 %collective-permute-start.21 = (bf16[512,512]{1,0:T(8,128)(2,1)S(1)}, bf16[512,512]{1,0:T(8,128)(2,1)S(1)}, u32[]{:S(2)}, u32[]{:S(2)}) collective-permute-start(bf16[512,512]{1,0:T(8,128)(2,1)S(1)} %slice.7), channel_id=1, source_target_pairs={{0,8},{8,16},{16,24},{24,32},{32,40},{40,48},{48,56},{56,64},{64,7... | collective-permute-start | bytes 1572872 | tf_op jit(solution)/shard_map/ppermute | solution.py:310
  102.6 1.6 collective-permute-done.19
  104.3 4.6 %collective-permute-done.17 = bf16[192,256]{1,0:T(8,128)(2,1)S(1)} collective-permute-done((bf16[192,256]{1,0:T(8,128)(2,1)S(1)}, bf16[192,256]{1,0:T(8,128)(2,1)S(1)}, u32[]{:S(2)}, u32[]{:S(2)}) %collective-permute-start.17) | collective-permute-done | bytes 98336 | tf_op jit(solution)/shard_map/ppermute | solution.py:38
  110.1 2.8 %collective-permute-start.23 = (bf16[192,256]{1,0:T(8,128)(2,1)S(1)}, bf16[192,256]{1,0:T(8,128)(2,1)S(1)}, u32[]{:S(2)}, u32[]{:S(2)}) collective-permute-start(bf16[192,256]{1,0:T(8,128)(2,1)S(1)} %add_convert_fusion.6), channel_id=1, source_target_pairs={{0,64},{8,200},{64,0},{72,136},{128,192},{136,72},{192,128},{200,8... | collective-permute-start | bytes 294920 | tf_op jit(solution)/shard_map/ppermute | solution.py:38
  112.9 2.8 %shard_map.98.attn_ref = f32[768,512]{1,0:T(8,128)S(1)} custom-call(s32[3]{0:T(128)S(1)} %pad_add_fusion.meta_ref, bf16[768,512]{1,0:T(8,128)(2,1)S(1)} %copy-done.2, bf16[512,512]{1,0:T(8,128)(2,1)S(1)} %collective-permute-done.halo_k_ref, bf16[768,512]{1,0:T(8,128)(2,1)S(1)} %copy-done.1, bf16[512,512]{1,0:T(8,128)(2,1)S(1)} %collective-permute-done.21.halo_v_ref, ...), custom_call_target="tpu_custom_call" | custom-call | tf_op jit(solution)/shard_map/pallas_call | solution.py:286
  116.0 2.9 %collective-permute-start.24 = (bf16[192,256]{1,0:T(8,128)(2,1)S(1)}, bf16[192,256]{1,0:T(8,128)(2,1)S(1)}, u32[]{:S(2)}, u32[]{:S(2)}) collective-permute-start(bf16[192,256]{1,0:T(8,128)(2,1)S(1)} %add_convert_fusion.5.refs_0_), channel_id=1, source_target_pairs={{0,192},{8,72},{64,128},{72,8},{128,64},{136,200},{192,0},{200,136... | collective-permute-start | bytes 294920 | tf_op jit(solution)/shard_map/ppermute | solution.py:38
  119.2 4.0 %shard_map.99 = bf16[768,512]{1,0:T(8,128)(2,1)} custom-call(s32[3]{0:T(128)S(1)} %pad_add_fusion.meta_ref, bf16[768,512]{1,0:T(8,128)(2,1)S(1)} %copy-done.2, f32[768,512]{1,0:T(8,128)S(1)} %shard_map.98.attn_ref, bf16[1536,512]{1,0:T(8,128)(2,1)S(1)} %copy-done.5, bf16[1536,512]{1,0:T(8,128)(2,1)S(1)} %get-tuple-element.47.late_ref), custom_call_target="tpu_custom_call" | custom-call | tf_op jit(solution)/shard_map/pallas_call | solution.py:286
  123.1 1.7 %collective-permute-done.25.refs_3_ = bf16[192,256]{1,0:T(8,128)(2,1)S(1)} collective-permute-done((bf16[192,256]{1,0:T(8,128)(2,1)S(1)}, bf16[192,256]{1,0:T(8,128)(2,1)S(1)}, u32[]{:S(2)}, u32[]{:S(2)}) %collective-permute-start.25) | collective-permute-done | bytes 98336 | tf_op jit(solution)/shard_map/ppermute | solution.py:38
  127.2 3.0 %collective-permute-done.26 = bf16[192,512]{1,0:T(8,128)(2,1)S(1)} collective-permute-done((bf16[192,512]{1,0:T(8,128)(2,1)S(1)}, bf16[192,512]{1,0:T(8,128)(2,1)S(1)}, u32[]{:S(2)}, u32[]{:S(2)}) %collective-permute-start.26) | collective-permute-done | bytes 196640 | tf_op jit(solution)/shard_map/ppermute | solution.py:38
  130.9 4.3 %collective-permute-start.27 = (bf16[384,512]{1,0:T(8,128)(2,1)}, bf16[384,512]{1,0:T(8,128)(2,1)}, u32[]{:S(2)}, u32[]{:S(2)}) collective-permute-start(bf16[384,512]{1,0:T(8,128)(2,1)} %constant_dynamic-update-slice_fusion.2.rest_0_), channel_id=1, source_target_pairs={{0,16},{8,56},{16,0},{24,40},{32,48},{40,24},{48,32},{56,8},{1,17}... | collective-permute-start | bytes 1179656 | tf_op jit(solution)/shard_map/ppermute | solution.py:38
  135.2 12.5 %all-to-all-start.1 = ((f32[64,8,128]{2,1,0:T(8,128)}), f32[64,8,128]{2,1,0:T(8,128)S(1)}, u32[]{:S(2)}, u32[]{:S(2)}) async-start(f32[64,8,128]{2,1,0:T(8,128)} %copy-done.6), calls=%async_computation.1 | async-start | bytes 524288 | tf_op jit(solution)/shard_map/all_to_all | solution.py:62
  148.4 9.1 %all-to-all-done.1.square_ref = f32[64,8,128]{2,1,0:T(8,128)S(1)} async-done(((f32[64,8,128]{2,1,0:T(8,128)}), f32[64,8,128]{2,1,0:T(8,128)S(1)}, u32[]{:S(2)}, u32[]{:S(2)}) %all-to-all-start.1) | async-done | bytes 262176 | tf_op jit(solution)/shard_map/all_to_all | solution.py:62
  157.5 3.3 %shard_map.101 = f32[1536,512]{1,0:T(8,128)} custom-call(s32[8]{0:T(128)S(1)} %broadcast_multiply_fusion.starts_ref, f32[64,8,128]{2,1,0:T(8,128)S(1)} %all-to-all-done.1.square_ref, f32[1536,512]{1,0:T(8,128)S(1)} %copy-done.3, bf16[384,512]{1,0:T(8,128)(2,1)} %constant_dynamic-update-slice_fusion.2.rest_0_, ...), custom_call_target="tpu_custom_call" | custom-call | tf_op jit(solution)/shard_map/pallas_call | solution.py:286
  (80 shorter events, 23.4 us)
Async XLA Ops:
  8.1 4.8 %collective-permute-start.1 = (bf16[768,256]{1,0:T(8,128)(2,1)S(1)}, bf16[768,256]{1,0:T(8,128)(2,1)}, u32[]{:S(2)}, u32[]{:S(2)}) collective-permute-start(bf16[768,256]{1,0:T(8,128)(2,1)S(1)} %get-tuple-element.29), channel_id=1, source_target_pairs={{0,8},{8,0},{1,9},{9,1},{2,10},{10,2},{3,11},{11,3},{4,12},{12,4},... | collective-permute-start | bytes 1179656 | tf_op jit(solution)/shard_map/ppermute | solution.py:38
  11.5 3.9 %collective-permute-start.4 = (bf16[768,256]{1,0:T(8,128)(2,1)S(1)}, bf16[768,256]{1,0:T(8,128)(2,1)}, u32[]{:S(2)}, u32[]{:S(2)}) collective-permute-start(bf16[768,256]{1,0:T(8,128)(2,1)S(1)} %get-tuple-element.31), channel_id=1, source_target_pairs={{0,8},{8,0},{1,9},{9,1},{2,10},{10,2},{3,11},{11,3},{4,12},{12,4},... | collective-permute-start | bytes 1179656 | tf_op jit(solution)/shard_map/ppermute | solution.py:38
  14.6 7.1 %collective-permute-start.2 = (bf16[384,256]{1,0:T(8,128)(2,1)}, bf16[384,256]{1,0:T(8,128)(2,1)S(1)}, u32[]{:S(2)}, u32[]{:S(2)}) collective-permute-start(bf16[384,256]{1,0:T(8,128)(2,1)} %add_convert_fusion.3), channel_id=1, source_target_pairs={{0,16},{8,56},{16,0},{24,40},{32,48},{40,24},{48,32},{56,8},{1,17}... | collective-permute-start | bytes 589832 | tf_op jit(solution)/shard_map/ppermute | solution.py:38
  17.0 6.0 %collective-permute-start.5 = (bf16[384,256]{1,0:T(8,128)(2,1)}, bf16[384,256]{1,0:T(8,128)(2,1)}, u32[]{:S(2)}, u32[]{:S(2)}) collective-permute-start(bf16[384,256]{1,0:T(8,128)(2,1)} %add_convert_fusion.2), channel_id=1, source_target_pairs={{0,16},{8,56},{16,0},{24,40},{32,48},{40,24},{48,32},{56,8},{1,17}... | collective-permute-start | bytes 589832 | tf_op jit(solution)/shard_map/ppermute | solution.py:38
  19.8 11.3 %collective-permute-start = (bf16[512,512]{1,0:T(8,128)(2,1)}, bf16[512,512]{1,0:T(8,128)(2,1)S(1)}, u32[]{:S(2)}, u32[]{:S(2)}) collective-permute-start(bf16[512,512]{1,0:T(8,128)(2,1)} %slice.6), channel_id=1, source_target_pairs={{0,8},{8,16},{16,24},{24,32},{32,40},{40,48},{48,56},{56,64},{64,7... | collective-permute-start | bytes 1572872 | tf_op jit(solution)/shard_map/ppermute | solution.py:309
  22.7 6.4 %collective-permute-start.3 = (bf16[192,256]{1,0:T(8,128)(2,1)S(1)}, bf16[192,256]{1,0:T(8,128)(2,1)S(1)}, u32[]{:S(2)}, u32[]{:S(2)}) collective-permute-start(bf16[192,256]{1,0:T(8,128)(2,1)S(1)} %add_convert_fusion.15), channel_id=1, source_target_pairs={{0,48},{8,24},{16,32},{24,8},{32,16},{40,56},{48,0},{56,40},{1,49}... | collective-permute-start | bytes 294920 | tf_op jit(solution)/shard_map/ppermute | solution.py:38
  24.0 6.1 %collective-permute-start.6 = (bf16[192,256]{1,0:T(8,128)(2,1)S(1)}, bf16[192,256]{1,0:T(8,128)(2,1)S(1)}, u32[]{:S(2)}, u32[]{:S(2)}) collective-permute-start(bf16[192,256]{1,0:T(8,128)(2,1)S(1)} %add_convert_fusion.13), channel_id=1, source_target_pairs={{0,48},{8,24},{16,32},{24,8},{32,16},{40,56},{48,0},{56,40},{1,49}... | collective-permute-start | bytes 294920 | tf_op jit(solution)/shard_map/ppermute | solution.py:38
  31.1 7.7 %collective-permute-start.7 = (bf16[192,256]{1,0:T(8,128)(2,1)S(1)}, bf16[192,256]{1,0:T(8,128)(2,1)S(1)}, u32[]{:S(2)}, u32[]{:S(2)}) collective-permute-start(bf16[192,256]{1,0:T(8,128)(2,1)S(1)} %add_convert_fusion.14), channel_id=1, source_target_pairs={{0,64},{8,200},{64,0},{72,136},{128,192},{136,72},{192,128},{200,8... | collective-permute-start | bytes 294920 | tf_op jit(solution)/shard_map/ppermute | solution.py:38
  36.3 5.7 %collective-permute-start.8 = (bf16[192,256]{1,0:T(8,128)(2,1)S(1)}, bf16[192,256]{1,0:T(8,128)(2,1)S(1)}, u32[]{:S(2)}, u32[]{:S(2)}) collective-permute-start(bf16[192,256]{1,0:T(8,128)(2,1)S(1)} %add_convert_fusion.12), channel_id=1, source_target_pairs={{0,64},{8,200},{64,0},{72,136},{128,192},{136,72},{192,128},{200,8... | collective-permute-start | bytes 294920 | tf_op jit(solution)/shard_map/ppermute | solution.py:38
  38.8 8.2 %collective-permute-start.9 = (bf16[192,256]{1,0:T(8,128)(2,1)S(1)}, bf16[192,256]{1,0:T(8,128)(2,1)S(1)}, u32[]{:S(2)}, u32[]{:S(2)}) collective-permute-start(bf16[192,256]{1,0:T(8,128)(2,1)S(1)} %add_convert_fusion.11.refs_0_), channel_id=1, source_target_pairs={{0,192},{8,72},{64,128},{72,8},{128,64},{136,200},{192,0},{200,136... | collective-permute-start | bytes 294920 | tf_op jit(solution)/shard_map/ppermute | solution.py:38
  42.0 7.1 %collective-permute-start.10 = (bf16[192,256]{1,0:T(8,128)(2,1)S(1)}, bf16[192,256]{1,0:T(8,128)(2,1)S(1)}, u32[]{:S(2)}, u32[]{:S(2)}) collective-permute-start(bf16[192,256]{1,0:T(8,128)(2,1)S(1)} %add_convert_fusion.10.refs_1_), channel_id=1, source_target_pairs={{0,192},{8,72},{64,128},{72,8},{128,64},{136,200},{192,0},{200,136... | collective-permute-start | bytes 294920 | tf_op jit(solution)/shard_map/ppermute | solution.py:38
  50.0 4.8 %collective-permute-start.11 = (bf16[192,512]{1,0:T(8,128)(2,1)S(1)}, bf16[192,512]{1,0:T(8,128)(2,1)S(1)}, u32[]{:S(2)}, u32[]{:S(2)}) collective-permute-start(bf16[192,512]{1,0:T(8,128)(2,1)S(1)} %get-tuple-element.35), channel_id=1, source_target_pairs={{0,48},{8,24},{16,32},{24,8},{32,16},{40,56},{48,0},{56,40},{1,49}... | collective-permute-start | bytes 589832 | tf_op jit(solution)/shard_map/ppermute | solution.py:38
  54.8 23.3 %collective-permute-start.12 = (bf16[384,512]{1,0:T(8,128)(2,1)S(1)}, bf16[384,512]{1,0:T(8,128)(2,1)S(1)}, u32[]{:S(2)}, u32[]{:S(2)}) collective-permute-start(bf16[384,512]{1,0:T(8,128)(2,1)S(1)} %constant_dynamic-update-slice_fusion.rest_0_), channel_id=1, source_target_pairs={{0,16},{8,56},{16,0},{24,40},{32,48},{40,24},{48,32},{56,8},{1,17}... | collective-permute-start | bytes 1179656 | tf_op jit(solution)/shard_map/ppermute | solution.py:38
  61.4 25.6 %all-to-all-start = ((f32[64,8,128]{2,1,0:T(8,128)}), f32[64,8,128]{2,1,0:T(8,128)S(1)}, u32[]{:S(2)}, u32[]{:S(2)}) async-start(f32[64,8,128]{2,1,0:T(8,128)} %get-tuple-element.34), calls=%async_computation | async-start | bytes 524288 | tf_op jit(solution)/shard_map/all_to_all | solution.py:62
  77.3 9.7 %collective-permute-start.13 = (bf16[384,512]{1,0:T(8,128)(2,1)S(1)}, bf16[384,512]{1,0:T(8,128)(2,1)S(1)}, u32[]{:S(2)}, u32[]{:S(2)}) collective-permute-start(bf16[384,512]{1,0:T(8,128)(2,1)S(1)} %constant_dynamic-update-slice_fusion.rest_0_), channel_id=1, source_target_pairs={{0,8},{8,0},{1,9},{9,1},{2,10},{10,2},{3,11},{11,3},{4,12},{12,4},... | collective-permute-start | bytes 1179656 | tf_op jit(solution)/shard_map/ppermute | solution.py:38
  78.1 9.0 %collective-permute-start.14 = (bf16[384,512]{1,0:T(8,128)(2,1)S(1)}, bf16[384,512]{1,0:T(8,128)(2,1)S(1)}, u32[]{:S(2)}, u32[]{:S(2)}) collective-permute-start(bf16[384,512]{1,0:T(8,128)(2,1)S(1)} %collective-permute-done.12.rest_1_), channel_id=1, source_target_pairs={{0,8},{8,0},{1,9},{9,1},{2,10},{10,2},{3,11},{11,3},{4,12},{12,4},... | collective-permute-start | bytes 1179656 | tf_op jit(solution)/shard_map/ppermute | solution.py:38
  94.4 1.8 %collective-permute-start.15 = (bf16[768,256]{1,0:T(8,128)(2,1)S(1)}, bf16[768,256]{1,0:T(8,128)(2,1)S(1)}, u32[]{:S(2)}, u32[]{:S(2)}) collective-permute-start(bf16[768,256]{1,0:T(8,128)(2,1)S(1)} %get-tuple-element.37), channel_id=1, source_target_pairs={{0,8},{8,0},{1,9},{9,1},{2,10},{10,2},{3,11},{11,3},{4,12},{12,4},... | collective-permute-start | bytes 1179656 | tf_op jit(solution)/shard_map/ppermute | solution.py:38
  94.9 2.3 %collective-permute-start.18 = (bf16[768,256]{1,0:T(8,128)(2,1)S(1)}, bf16[768,256]{1,0:T(8,128)(2,1)S(1)}, u32[]{:S(2)}, u32[]{:S(2)}) collective-permute-start(bf16[768,256]{1,0:T(8,128)(2,1)S(1)} %get-tuple-element.39), channel_id=1, source_target_pairs={{0,8},{8,0},{1,9},{9,1},{2,10},{10,2},{3,11},{11,3},{4,12},{12,4},... | collective-permute-start | bytes 1179656 | tf_op jit(solution)/shard_map/ppermute | solution.py:38
  96.3 5.8 %collective-permute-start.16 = (bf16[384,256]{1,0:T(8,128)(2,1)S(1)}, bf16[384,256]{1,0:T(8,128)(2,1)S(1)}, u32[]{:S(2)}, u32[]{:S(2)}) collective-permute-start(bf16[384,256]{1,0:T(8,128)(2,1)S(1)} %add_convert_fusion.1), channel_id=1, source_target_pairs={{0,16},{8,56},{16,0},{24,40},{32,48},{40,24},{48,32},{56,8},{1,17}... | collective-permute-start | bytes 589832 | tf_op jit(solution)/shard_map/ppermute | solution.py:38
  97.2 7.0 %collective-permute-start.19 = (bf16[384,256]{1,0:T(8,128)(2,1)S(1)}, bf16[384,256]{1,0:T(8,128)(2,1)S(1)}, u32[]{:S(2)}, u32[]{:S(2)}) collective-permute-start(bf16[384,256]{1,0:T(8,128)(2,1)S(1)} %add_convert_fusion), channel_id=1, source_target_pairs={{0,16},{8,56},{16,0},{24,40},{32,48},{40,24},{48,32},{56,8},{1,17}... | collective-permute-start | bytes 589832 | tf_op jit(solution)/shard_map/ppermute | solution.py:38
  99.2 13.7 %collective-permute-start.21 = (bf16[512,512]{1,0:T(8,128)(2,1)S(1)}, bf16[512,512]{1,0:T(8,128)(2,1)S(1)}, u32[]{:S(2)}, u32[]{:S(2)}) collective-permute-start(bf16[512,512]{1,0:T(8,128)(2,1)S(1)} %slice.7), channel_id=1, source_target_pairs={{0,8},{8,16},{16,24},{24,32},{32,40},{40,48},{48,56},{56,64},{64,7... | collective-permute-start | bytes 1572872 | tf_op jit(solution)/shard_map/ppermute | solution.py:310
  102.1 6.8 %collective-permute-start.17 = (bf16[192,256]{1,0:T(8,128)(2,1)S(1)}, bf16[192,256]{1,0:T(8,128)(2,1)S(1)}, u32[]{:S(2)}, u32[]{:S(2)}) collective-permute-start(bf16[192,256]{1,0:T(8,128)(2,1)S(1)} %add_convert_fusion.9), channel_id=1, source_target_pairs={{0,48},{8,24},{16,32},{24,8},{32,16},{40,56},{48,0},{56,40},{1,49}... | collective-permute-start | bytes 294920 | tf_op jit(solution)/shard_map/ppermute | solution.py:38
  104.2 5.8 %collective-permute-start.20 = (bf16[192,256]{1,0:T(8,128)(2,1)S(1)}, bf16[192,256]{1,0:T(8,128)(2,1)S(1)}, u32[]{:S(2)}, u32[]{:S(2)}) collective-permute-start(bf16[192,256]{1,0:T(8,128)(2,1)S(1)} %add_convert_fusion.7), channel_id=1, source_target_pairs={{0,48},{8,24},{16,32},{24,8},{32,16},{40,56},{48,0},{56,40},{1,49}... | collective-permute-start | bytes 294920 | tf_op jit(solution)/shard_map/ppermute | solution.py:38
  109.0 6.7 %collective-permute-start.22 = (bf16[192,256]{1,0:T(8,128)(2,1)S(1)}, bf16[192,256]{1,0:T(8,128)(2,1)S(1)}, u32[]{:S(2)}, u32[]{:S(2)}) collective-permute-start(bf16[192,256]{1,0:T(8,128)(2,1)S(1)} %add_convert_fusion.8), channel_id=1, source_target_pairs={{0,64},{8,200},{64,0},{72,136},{128,192},{136,72},{192,128},{200,8... | collective-permute-start | bytes 294920 | tf_op jit(solution)/shard_map/ppermute | solution.py:38
  110.1 5.8 %collective-permute-start.23 = (bf16[192,256]{1,0:T(8,128)(2,1)S(1)}, bf16[192,256]{1,0:T(8,128)(2,1)S(1)}, u32[]{:S(2)}, u32[]{:S(2)}) collective-permute-start(bf16[192,256]{1,0:T(8,128)(2,1)S(1)} %add_convert_fusion.6), channel_id=1, source_target_pairs={{0,64},{8,200},{64,0},{72,136},{128,192},{136,72},{192,128},{200,8... | collective-permute-start | bytes 294920 | tf_op jit(solution)/shard_map/ppermute | solution.py:38
  116.0 7.2 %collective-permute-start.24 = (bf16[192,256]{1,0:T(8,128)(2,1)S(1)}, bf16[192,256]{1,0:T(8,128)(2,1)S(1)}, u32[]{:S(2)}, u32[]{:S(2)}) collective-permute-start(bf16[192,256]{1,0:T(8,128)(2,1)S(1)} %add_convert_fusion.5.refs_0_), channel_id=1, source_target_pairs={{0,192},{8,72},{64,128},{72,8},{128,64},{136,200},{192,0},{200,136... | collective-permute-start | bytes 294920 | tf_op jit(solution)/shard_map/ppermute | solution.py:38
  118.8 6.0 %collective-permute-start.25 = (bf16[192,256]{1,0:T(8,128)(2,1)S(1)}, bf16[192,256]{1,0:T(8,128)(2,1)S(1)}, u32[]{:S(2)}, u32[]{:S(2)}) collective-permute-start(bf16[192,256]{1,0:T(8,128)(2,1)S(1)} %add_convert_fusion.4.refs_1_), channel_id=1, source_target_pairs={{0,192},{8,72},{64,128},{72,8},{128,64},{136,200},{192,0},{200,136... | collective-permute-start | bytes 294920 | tf_op jit(solution)/shard_map/ppermute | solution.py:38
  125.7 4.5 %collective-permute-start.26 = (bf16[192,512]{1,0:T(8,128)(2,1)S(1)}, bf16[192,512]{1,0:T(8,128)(2,1)S(1)}, u32[]{:S(2)}, u32[]{:S(2)}) collective-permute-start(bf16[192,512]{1,0:T(8,128)(2,1)S(1)} %get-tuple-element.53), channel_id=1, source_target_pairs={{0,48},{8,24},{16,32},{24,8},{32,16},{40,56},{48,0},{56,40},{1,49}... | collective-permute-start | bytes 589832 | tf_op jit(solution)/shard_map/ppermute | solution.py:38
  130.9 17.4 %collective-permute-start.27 = (bf16[384,512]{1,0:T(8,128)(2,1)}, bf16[384,512]{1,0:T(8,128)(2,1)}, u32[]{:S(2)}, u32[]{:S(2)}) collective-permute-start(bf16[384,512]{1,0:T(8,128)(2,1)} %constant_dynamic-update-slice_fusion.2.rest_0_), channel_id=1, source_target_pairs={{0,16},{8,56},{16,0},{24,40},{32,48},{40,24},{48,32},{56,8},{1,17}... | collective-permute-start | bytes 1179656 | tf_op jit(solution)/shard_map/ppermute | solution.py:38
  135.2 22.2 %all-to-all-start.1 = ((f32[64,8,128]{2,1,0:T(8,128)}), f32[64,8,128]{2,1,0:T(8,128)S(1)}, u32[]{:S(2)}, u32[]{:S(2)}) async-start(f32[64,8,128]{2,1,0:T(8,128)} %copy-done.6), calls=%async_computation.1 | async-start | bytes 524288 | tf_op jit(solution)/shard_map/all_to_all | solution.py:62
  147.8 9.7 %collective-permute-start.28 = (bf16[384,512]{1,0:T(8,128)(2,1)}, bf16[384,512]{1,0:T(8,128)(2,1)}, u32[]{:S(2)}, u32[]{:S(2)}) collective-permute-start(bf16[384,512]{1,0:T(8,128)(2,1)} %constant_dynamic-update-slice_fusion.2.rest_0_), channel_id=1, source_target_pairs={{0,8},{8,0},{1,9},{9,1},{2,10},{10,2},{3,11},{11,3},{4,12},{12,4},... | collective-permute-start | bytes 1179656 | tf_op jit(solution)/shard_map/ppermute | solution.py:38
  148.3 9.2 %collective-permute-start.29 = (bf16[384,512]{1,0:T(8,128)(2,1)}, bf16[384,512]{1,0:T(8,128)(2,1)}, u32[]{:S(2)}, u32[]{:S(2)}) collective-permute-start(bf16[384,512]{1,0:T(8,128)(2,1)} %collective-permute-done.27.rest_1_), channel_id=1, source_target_pairs={{0,8},{8,0},{1,9},{9,1},{2,10},{10,2},{3,11},{11,3},{4,12},{12,4},... | collective-permute-start | bytes 1179656 | tf_op jit(solution)/shard_map/ppermute | solution.py:38
  (7 other events, 115.1 us)
where the time goes:
time: 161 us
  starting transfers between devices  74.5 us (46%)
  waiting for transfers between devices  48 us (30%)
  Pallas kernels  24.3 us (15%)
  other arithmetic  7.72 us (5%)
  local copies, waits for them, and re-layouts  3.95 us (2%)
  between operations  2.4 us (1%)
    ppermute x28, starting transfers between devices, exchange(): lax.ppermute(value, mesh_axes, [(i, partner(i)) for i in range(count)])  42.3 us
    ppermute x28, waiting for transfers between devices, exchange(): lax.ppermute(value, mesh_axes, [(i, partner(i)) for i in range(count)])  30.2 us
    all_to_all x2, starting transfers between devices, spread(): return lax.all_to_all(squares, ('x', 'core', 'head'), 0, 0, tiled=True)  28.4 us
    pallas_call x7, Pallas kernels, call(): pl.pallas_call(kernel, out_shape=outs, in_specs=specs, out_specs=jax.tree...  24.3 us
    all_to_all x2, waiting for transfers between devices, spread(): return lax.all_to_all(squares, ('x', 'core', 'head'), 0, 0, tiled=True)  17.9 us
    convert_element_type x4, other arithmetic, reduced(): two(c, (1 - first) * half, half).astype(bf16)  3.4 us
  transfers between devices with their start and end apart: 32, of which 18 were waited for; matrix products, arithmetic and copies ran while one was open for 6% of the time, Pallas kernels for 4%

commit v1 on v0

--- a/solution.py
+++ b/solution.py
@@ -18,6 +18,7 @@
 TILE = 256
 CHUNKS = 2
 SHARES = 64
+EARLY = 128
 
 fast_rate = 0.01
 epsilon = 1e-06
@@ -58,6 +59,15 @@
     return exchange(value, ("core",), lambda i: i ^ 1)
 
 
+def chained(parts, send):
+    arrived = []
+    for value in parts:
+        if arrived:
+            value, arrived[-1] = lax.optimization_barrier((value, arrived[-1]))
+        arrived.append(send(value))
+    return arrived
+
+
 def spread(squares):
     return lax.all_to_all(squares, ("x", "core", "head"), 0, 0, tiled=True)
 
@@ -83,7 +93,7 @@
     return (jnp.stack(places) * (ROWS // 8)).astype(jnp.int32)
 
 
-def reduced(sent, own, before_z=None, beside_first=None, beside_second=None):
+def reduced(sent, own, beside_first=None, beside_second=None):
     _, first, second = halves()
     half, rows = ROWS // 4, ROWS // 8
     chunks = range(len(sent))
@@ -99,8 +109,6 @@
     near = second * rows
     mine = [two(c, first * half + near, rows) + rows_of(got_x[c], near, rows).astype(f32) + got_x2[c].astype(f32) for c in chunks]
     mine = [m.astype(bf16) for m in mine]
-    if before_z is not None:
-        mine = before_z(mine)
     other = [swap_z(m, 0) for m in mine]
     if beside_first is not None:
         other = beside_first(mine, other)
@@ -222,10 +230,12 @@
         copy.wait()
 
 
-def attend_kernel(meta_ref, q_ref, halo_k_ref, k_ref, halo_v_ref, v_ref, out_ref):
+def attend_kernel(meta_ref, q_ref, halo_k_ref, k_ref, halo_v0, halo_v1, v_ref, out_ref, halo_v_ref):
     local = q_ref.shape[0]
     anchor, width = meta_ref[0], meta_ref[1]
     scale = HD ** (-0.5)
+    halo_v_ref[0:EARLY] = halo_v0[...]
+    halo_v_ref[EARLY:] = halo_v1[...]
     held = [(halo_k_ref, halo_v_ref, -WIN, WIN), (k_ref, v_ref, 0, local)]
     for start in range(0, local, TILE):
         spans = []
@@ -306,8 +316,8 @@
     anchor = lax.axis_index(SEQ) * local
     count = lax.axis_size(SEQ)
     onward = [(i, i + 1) for i in range(count - 1)]
-    halo_k = lax.ppermute(keys[local - WIN :], SEQ, onward)
-    halo_v = lax.ppermute(values[local - WIN :], SEQ, onward)
+    tail = local - WIN
+    halo_v = chained([values[tail : tail + EARLY], values[tail + EARLY :]], lambda v: lax.ppermute(v, SEQ, onward))
     positions = anchor + jnp.arange(local, dtype=jnp.int32)[:, None]
     first_block = (positions < split[0]).astype(f32)
     rate_zero = token_rate * first_block
@@ -333,7 +343,7 @@
         [HBM_SPEC] + [VMEM_SPEC] * (2 * CHUNKS),
     )
 
-    def finished(mine, other):
+    def finished(mine, other, later):
         total, square = call(
             finish_kernel,
             [VMEM_SPEC] * (2 * CHUNKS),
@@ -341,15 +351,14 @@
             (*mine, *other),
             8,
         )
-        return spread(square), gathered(total)
+        if later is not None:
+            total, later = lax.optimization_barrier((total, later))
+        return spread(square), gathered(total), later
 
     kept = {}
 
-    def have_keys(mine):
-        kept["halo"], mine = lax.optimization_barrier((halo_k, mine))
-        return mine
-
-    square, pieces = finished(*reduced(halved[:CHUNKS], halved[CHUNKS:], have_keys))
+    square, pieces, send = finished(*reduced(halved[:CHUNKS], halved[CHUNKS:]), keys[tail:])
+    halo_k = lax.ppermute(send, SEQ, onward)
     weights_one, wb_one, *halved = call(
         second_kernel,
         [SMEM_SPEC] * 2 + [VMEM_SPEC, HBM_SPEC, HBM_SPEC, VMEM_SPEC, HBM_SPEC] + [VMEM_SPEC] * 4,
@@ -359,14 +368,17 @@
         [grad] + renewal + fetched + [pltpu.VMEM((ROWS, HID), f32), pltpu.SemaphoreType.DMA((10,))],
         [HBM_SPEC] + [VMEM_SPEC] * (1 + 2 * CHUNKS),
     )
+    kept["halo"], halved = lax.optimization_barrier((halo_k, halved))
+
     def attend(before, after):
         query, _ = lax.optimization_barrier((queries, before))
         attn = call(
             attend_kernel,
-            [SMEM_SPEC] + [VMEM_SPEC] * 5,
+            [SMEM_SPEC] + [VMEM_SPEC] * 6,
             array((local, HD), f32),
-            (meta, query, kept["halo"], keys, halo_v, values),
+            (meta, query, kept["halo"], keys, *halo_v, values),
             20,
+            [pltpu.VMEM((WIN, HD), bf16)],
         )
         kept["attn"], after = lax.optimization_barrier((attn, after))
         return after
@@ -384,7 +396,7 @@
         kept["outputs"], after = lax.optimization_barrier((outputs, after))
         return after
 
-    square, pieces = finished(*reduced(halved[:CHUNKS], halved[CHUNKS:], None, attend, apply))
+    square, pieces, _ = finished(*reduced(halved[:CHUNKS], halved[CHUNKS:], attend, apply), None)
     weights_two = call(
         last_kernel,
         [SMEM_SPEC] + [VMEM_SPEC] * 6,

time: 161 us -> 160 us (level)
  starting transfers between devices: 74.5 us -> 76.9 us
    ppermute x2 -> x3, starting transfers between devices: 3.83 us -> 13.6 us  [the longest x1 9.13 us: per_device(): halo_k = lax.ppermute(send, SEQ, onward)]
    all_to_all x2, starting transfers between devices: 28.4 us -> 22.3 us  [spread(): return lax.all_to_all(squares, ('x', 'core', 'head'), 0, 0, tiled=True)]
  transfers between devices with their start and end apart: 32 -> 33, of which waited for: 18 -> 16; matrix products, arithmetic and copies ran while one was open for 6% -> 4% of each run, Pallas kernels for 4% -> 9%
where the time goes in v1:
time: 160 us
  starting transfers between devices  76.9 us (48%)
  waiting for transfers between devices  46.7 us (29%)
  Pallas kernels  24.1 us (15%)
  other arithmetic  6.22 us (4%)
  local copies, waits for them, and re-layouts  3.16 us (2%)
  between operations  2.42 us (2%)
    ppermute x28, starting transfers between devices, exchange(): lax.ppermute(value, mesh_axes, [(i, partner(i)) for i in range(count)])  41 us
    ppermute x28, waiting for transfers between devices, exchange(): lax.ppermute(value, mesh_axes, [(i, partner(i)) for i in range(count)])  28.8 us
    pallas_call x7, Pallas kernels, call(): pl.pallas_call(kernel, out_shape=outs, in_specs=specs, out_specs=jax.tree...  24.1 us
    all_to_all x2, starting transfers between devices, spread(): return lax.all_to_all(squares, ('x', 'core', 'head'), 0, 0, tiled=True)  22.3 us
    all_to_all x2, waiting for transfers between devices, spread(): return lax.all_to_all(squares, ('x', 'core', 'head'), 0, 0, tiled=True)  17.9 us
    ppermute x1, starting transfers between devices, per_device(): halo_k = lax.ppermute(send, SEQ, onward)  9.13 us
    ppermute x2, starting transfers between devices, per_device(): lax.ppermute(v, SEQ, onward)  4.48 us
  transfers between devices with their start and end apart: 33, of which 16 were waited for; matrix products, arithmetic and copies ran while one was open for 4% of the time, Pallas kernels for 9%

profile of v1, /device:TPU:1, one launch (start us, length us, event | category | flops | bytes accessed | tf_op | source)
XLA Modules:
  0.0 159.5 jit_solution(10038816225001080466)
XLA Ops:
  2.3 5.8 %shard_map.95 = (bf16[1536,512]{1,0:T(8,128)(2,1)}, bf16[768,256]{1,0:T(8,128)(2,1)S(1)}, bf16[768,256]{1,0:T(8,128)(2,1)S(1)}, f32[768,256]{1,0:T(8,128)S(1)}, f32[768,256]{1,0:T(8,128)S(1)}) custom-call(s32[1]{0:T(128)} %bitcast.1.place_ref, bf16[768,512]{1,0:T(8,128)(2,1)} %k_ref.1, bf16[768,512]{1,0:T(8,128)(2,1)} %targets_hbm.3, ...), custom_call_target="tpu_custom_call" | custom-call | tf_op jit(solution)/shard_map/pallas_call | solution.py:296
  8.1 3.3 %collective-permute-start = (bf16[768,256]{1,0:T(8,128)(2,1)S(1)}, bf16[768,256]{1,0:T(8,128)(2,1)}, u32[]{:S(2)}, u32[]{:S(2)}) collective-permute-start(bf16[768,256]{1,0:T(8,128)(2,1)S(1)} %get-tuple-element.35), channel_id=1, source_target_pairs={{0,8},{8,0},{1,9},{9,1},{2,10},{10,2},{3,11},{11,3},{4,12},{12,4},... | collective-permute-start | bytes 1179656 | tf_op jit(solution)/shard_map/ppermute | solution.py:39
  11.5 1.4 collective-permute-done
  15.6 2.0 %collective-permute-start.5 = (bf16[384,256]{1,0:T(8,128)(2,1)S(1)}, bf16[384,256]{1,0:T(8,128)(2,1)S(1)}, u32[]{:S(2)}, u32[]{:S(2)}) collective-permute-start(bf16[384,256]{1,0:T(8,128)(2,1)S(1)} %add_convert_fusion.2), channel_id=1, source_target_pairs={{0,16},{8,56},{16,0},{24,40},{32,48},{40,24},{48,32},{56,8},{1,17}... | collective-permute-start | bytes 589832 | tf_op jit(solution)/shard_map/ppermute | solution.py:39
  17.7 2.0 %collective-permute-done.1 = bf16[384,256]{1,0:T(8,128)(2,1)S(1)} collective-permute-done((bf16[384,256]{1,0:T(8,128)(2,1)S(1)}, bf16[384,256]{1,0:T(8,128)(2,1)S(1)}, u32[]{:S(2)}, u32[]{:S(2)}) %collective-permute-start.1) | collective-permute-done | bytes 196640 | tf_op jit(solution)/shard_map/ppermute | solution.py:39
  25.1 4.5 %collective-permute-start.3 = (bf16[192,256]{1,0:T(8,128)(2,1)S(1)}, bf16[192,256]{1,0:T(8,128)(2,1)S(1)}, u32[]{:S(2)}, u32[]{:S(2)}) collective-permute-start(bf16[192,256]{1,0:T(8,128)(2,1)S(1)} %add_convert_fusion.14), channel_id=1, source_target_pairs={{0,64},{8,200},{64,0},{72,136},{128,192},{136,72},{192,128},{200,8... | collective-permute-start | bytes 294920 | tf_op jit(solution)/shard_map/ppermute | solution.py:39
  30.5 2.5 %collective-permute-start.7 = (bf16[192,256]{1,0:T(8,128)(2,1)S(1)}, bf16[192,256]{1,0:T(8,128)(2,1)S(1)}, u32[]{:S(2)}, u32[]{:S(2)}) collective-permute-start(bf16[192,256]{1,0:T(8,128)(2,1)S(1)} %add_convert_fusion.11), channel_id=1, source_target_pairs={{0,64},{8,200},{64,0},{72,136},{128,192},{136,72},{192,128},{200,8... | collective-permute-start | bytes 294920 | tf_op jit(solution)/shard_map/ppermute | solution.py:39
  34.3 2.8 %collective-permute-done.7 = bf16[192,256]{1,0:T(8,128)(2,1)S(1)} collective-permute-done((bf16[192,256]{1,0:T(8,128)(2,1)S(1)}, bf16[192,256]{1,0:T(8,128)(2,1)S(1)}, u32[]{:S(2)}, u32[]{:S(2)}) %collective-permute-start.7) | collective-permute-done | bytes 98336 | tf_op jit(solution)/shard_map/ppermute | solution.py:39
  37.7 1.4 collective-permute-done.8.refs_2_
  39.0 3.6 %collective-permute-done.9.refs_3_ = bf16[192,256]{1,0:T(8,128)(2,1)S(1)} collective-permute-done((bf16[192,256]{1,0:T(8,128)(2,1)S(1)}, bf16[192,256]{1,0:T(8,128)(2,1)S(1)}, u32[]{:S(2)}, u32[]{:S(2)}) %collective-permute-start.9) | collective-permute-done | bytes 98336 | tf_op jit(solution)/shard_map/ppermute | solution.py:39
  43.6 4.5 %collective-permute-done.11 = bf16[192,512]{1,0:T(8,128)(2,1)S(1)} collective-permute-done((bf16[192,512]{1,0:T(8,128)(2,1)S(1)}, bf16[192,512]{1,0:T(8,128)(2,1)S(1)}, u32[]{:S(2)}, u32[]{:S(2)}) %collective-permute-start.11) | collective-permute-done | bytes 196640 | tf_op jit(solution)/shard_map/ppermute | solution.py:39
  48.1 2.7 %collective-permute-start.12 = (bf16[384,512]{1,0:T(8,128)(2,1)S(1)}, bf16[384,512]{1,0:T(8,128)(2,1)S(1)}, u32[]{:S(2)}, u32[]{:S(2)}) collective-permute-start(bf16[384,512]{1,0:T(8,128)(2,1)S(1)} %constant_dynamic-update-slice_fusion.rest_0_), channel_id=1, source_target_pairs={{0,16},{8,56},{16,0},{24,40},{32,48},{40,24},{48,32},{56,8},{1,17}... | collective-permute-start | bytes 1179656 | tf_op jit(solution)/shard_map/ppermute | solution.py:39
  50.8 9.1 %collective-permute-start.10 = (bf16[512,512]{1,0:T(8,128)(2,1)S(1)}, bf16[512,512]{1,0:T(8,128)(2,1)S(1)}, u32[]{:S(2)}, u32[]{:S(2)}) collective-permute-start(bf16[512,512]{1,0:T(8,128)(2,1)S(1)} %slice.9), channel_id=1, source_target_pairs={{0,8},{8,16},{16,24},{24,32},{32,40},{40,48},{48,56},{56,64},{64,7... | collective-permute-start | bytes 1572872 | tf_op jit(solution)/shard_map/ppermute | solution.py:361
  59.9 9.2 %all-to-all-start = ((f32[64,8,128]{2,1,0:T(8,128)}), f32[64,8,128]{2,1,0:T(8,128)S(1)}, u32[]{:S(2)}, u32[]{:S(2)}) async-start(f32[64,8,128]{2,1,0:T(8,128)} %get-tuple-element.40), calls=%async_computation | async-start | bytes 524288 | tf_op jit(solution)/shard_map/all_to_all | solution.py:72
  70.1 8.8 %all-to-all-done.square_ref = f32[64,8,128]{2,1,0:T(8,128)S(1)} async-done(((f32[64,8,128]{2,1,0:T(8,128)}), f32[64,8,128]{2,1,0:T(8,128)S(1)}, u32[]{:S(2)}, u32[]{:S(2)}) %all-to-all-start) | async-done | bytes 262176 | tf_op jit(solution)/shard_map/all_to_all | solution.py:72
  78.9 7.3 %shard_map.97 = (f32[1536,512]{1,0:T(8,128)}, bf16[1536,512]{1,0:T(8,128)(2,1)S(1)}, bf16[768,256]{1,0:T(8,128)(2,1)S(1)}, bf16[768,256]{1,0:T(8,128)(2,1)S(1)},...) custom-call(s32[1]{0:T(128)} %bitcast.1.place_ref, s32[8]{0:T(128)S(1)} %broadcast_multiply_fusion.starts_ref, ...), custom_call_target="tpu_custom_call" | custom-call | tf_op jit(solution)/shard_map/pallas_call | solution.py:296
  86.8 2.6 %collective-permute-start.21 = (bf16[128,512]{1,0:T(8,128)(2,1)S(1)}, bf16[128,512]{1,0:T(8,128)(2,1)S(1)}, u32[]{:S(2)}, u32[]{:S(2)}) collective-permute-start(bf16[128,512]{1,0:T(8,128)(2,1)S(1)} %slice.11), channel_id=1, source_target_pairs={{0,8},{8,16},{16,24},{24,32},{32,40},{40,48},{48,56},{56,64},{64,7... | collective-permute-start | bytes 393224 | tf_op jit(solution)/shard_map/ppermute | solution.py:320
  89.5 4.2 %collective-permute-start.16 = (bf16[384,256]{1,0:T(8,128)(2,1)S(1)}, bf16[384,256]{1,0:T(8,128)(2,1)S(1)}, u32[]{:S(2)}, u32[]{:S(2)}) collective-permute-start(bf16[384,256]{1,0:T(8,128)(2,1)S(1)} %add_convert_fusion.1), channel_id=1, source_target_pairs={{0,16},{8,56},{16,0},{24,40},{32,48},{40,24},{48,32},{56,8},{1,17}... | collective-permute-start | bytes 589832 | tf_op jit(solution)/shard_map/ppermute | solution.py:39
  94.5 1.9 %collective-permute-start.22 = (bf16[384,512]{1,0:T(8,128)(2,1)S(1)}, bf16[384,512]{1,0:T(8,128)(2,1)S(1)}, u32[]{:S(2)}, u32[]{:S(2)}) collective-permute-start(bf16[384,512]{1,0:T(8,128)(2,1)S(1)} %slice.10), channel_id=1, source_target_pairs={{0,8},{8,16},{16,24},{24,32},{32,40},{40,48},{48,56},{56,64},{64,7... | collective-permute-start | bytes 1179656 | tf_op jit(solution)/shard_map/ppermute | solution.py:320
  96.8 2.7 %collective-permute-done.19 = bf16[384,256]{1,0:T(8,128)(2,1)S(1)} collective-permute-done((bf16[384,256]{1,0:T(8,128)(2,1)S(1)}, bf16[384,256]{1,0:T(8,128)(2,1)S(1)}, u32[]{:S(2)}, u32[]{:S(2)}) %collective-permute-start.19) | collective-permute-done | bytes 196640 | tf_op jit(solution)/shard_map/ppermute | solution.py:39
  99.6 2.5 %collective-permute-done.17 = bf16[192,256]{1,0:T(8,128)(2,1)S(1)} collective-permute-done((bf16[192,256]{1,0:T(8,128)(2,1)S(1)}, bf16[192,256]{1,0:T(8,128)(2,1)S(1)}, u32[]{:S(2)}, u32[]{:S(2)}) %collective-permute-start.17) | collective-permute-done | bytes 98336 | tf_op jit(solution)/shard_map/ppermute | solution.py:39
  102.2 3.6 %collective-permute-start.23 = (bf16[192,256]{1,0:T(8,128)(2,1)S(1)}, bf16[192,256]{1,0:T(8,128)(2,1)S(1)}, u32[]{:S(2)}, u32[]{:S(2)}) collective-permute-start(bf16[192,256]{1,0:T(8,128)(2,1)S(1)} %add_convert_fusion.8), channel_id=1, source_target_pairs={{0,64},{8,200},{64,0},{72,136},{128,192},{136,72},{192,128},{200,8... | collective-permute-start | bytes 294920 | tf_op jit(solution)/shard_map/ppermute | solution.py:39
  107.0 2.8 %shard_map.98.attn_ref = f32[768,512]{1,0:T(8,128)S(1)} custom-call(s32[3]{0:T(128)S(1)} %pad_add_fusion.meta_ref, bf16[768,512]{1,0:T(8,128)(2,1)S(1)} %copy-done.2, bf16[512,512]{1,0:T(8,128)(2,1)S(1)} %collective-permute-done.10.halo_k_ref, bf16[768,512]{1,0:T(8,128)(2,1)S(1)} %copy-done.1, bf16[128,512]{1,0:T(8,128)(2,1)S(1)} %collective-permute-done.21.halo_v0, ...), custom_call_target="tpu_custom_call" | custom-call | tf_op jit(solution)/shard_map/pallas_call | solution.py:296
  109.8 1.9 %collective-permute-done.24 = bf16[192,256]{1,0:T(8,128)(2,1)S(1)} collective-permute-done((bf16[192,256]{1,0:T(8,128)(2,1)S(1)}, bf16[192,256]{1,0:T(8,128)(2,1)S(1)}, u32[]{:S(2)}, u32[]{:S(2)}) %collective-permute-start.24) | collective-permute-done | bytes 98336 | tf_op jit(solution)/shard_map/ppermute | solution.py:39
  112.5 1.7 %collective-permute-start.26 = (bf16[192,256]{1,0:T(8,128)(2,1)S(1)}, bf16[192,256]{1,0:T(8,128)(2,1)S(1)}, u32[]{:S(2)}, u32[]{:S(2)}) collective-permute-start(bf16[192,256]{1,0:T(8,128)(2,1)S(1)} %add_convert_fusion.4.refs_1_), channel_id=1, source_target_pairs={{0,192},{8,72},{64,128},{72,8},{128,64},{136,200},{192,0},{200,136... | collective-permute-start | bytes 294920 | tf_op jit(solution)/shard_map/ppermute | solution.py:39
  114.2 3.9 %shard_map.99 = bf16[768,512]{1,0:T(8,128)(2,1)} custom-call(s32[3]{0:T(128)S(1)} %pad_add_fusion.meta_ref, bf16[768,512]{1,0:T(8,128)(2,1)S(1)} %copy-done.2, f32[768,512]{1,0:T(8,128)S(1)} %shard_map.98.attn_ref, bf16[1536,512]{1,0:T(8,128)(2,1)S(1)} %copy-done.5, bf16[1536,512]{1,0:T(8,128)(2,1)S(1)} %get-tuple-element.59.late_ref), custom_call_target="tpu_custom_call" | custom-call | tf_op jit(solution)/shard_map/pallas_call | solution.py:296
  120.3 1.4 collective-permute-start.27
  122.4 2.4 %collective-permute-done.27 = bf16[192,512]{1,0:T(8,128)(2,1)S(1)} collective-permute-done((bf16[192,512]{1,0:T(8,128)(2,1)S(1)}, bf16[192,512]{1,0:T(8,128)(2,1)S(1)}, u32[]{:S(2)}, u32[]{:S(2)}) %collective-permute-start.27) | collective-permute-done | bytes 196640 | tf_op jit(solution)/shard_map/ppermute | solution.py:39
  125.5 7.7 %collective-permute-start.28 = (bf16[384,512]{1,0:T(8,128)(2,1)}, bf16[384,512]{1,0:T(8,128)(2,1)}, u32[]{:S(2)}, u32[]{:S(2)}) collective-permute-start(bf16[384,512]{1,0:T(8,128)(2,1)} %constant_dynamic-update-slice_fusion.2.rest_0_), channel_id=1, source_target_pairs={{0,16},{8,56},{16,0},{24,40},{32,48},{40,24},{48,32},{56,8},{1,17}... | collective-permute-start | bytes 1179656 | tf_op jit(solution)/shard_map/ppermute | solution.py:39
  133.2 13.2 %all-to-all-start.1 = ((f32[64,8,128]{2,1,0:T(8,128)}), f32[64,8,128]{2,1,0:T(8,128)S(1)}, u32[]{:S(2)}, u32[]{:S(2)}) async-start(f32[64,8,128]{2,1,0:T(8,128)} %copy-done.6), calls=%async_computation.1 | async-start | bytes 524288 | tf_op jit(solution)/shard_map/all_to_all | solution.py:72
  147.0 9.1 %all-to-all-done.1.square_ref = f32[64,8,128]{2,1,0:T(8,128)S(1)} async-done(((f32[64,8,128]{2,1,0:T(8,128)}), f32[64,8,128]{2,1,0:T(8,128)S(1)}, u32[]{:S(2)}, u32[]{:S(2)}) %all-to-all-start.1) | async-done | bytes 262176 | tf_op jit(solution)/shard_map/all_to_all | solution.py:72
  156.1 3.3 %shard_map.101 = f32[1536,512]{1,0:T(8,128)} custom-call(s32[8]{0:T(128)S(1)} %broadcast_multiply_fusion.starts_ref, f32[64,8,128]{2,1,0:T(8,128)S(1)} %all-to-all-done.1.square_ref, f32[1536,512]{1,0:T(8,128)S(1)} %copy-done.3, bf16[384,512]{1,0:T(8,128)(2,1)} %constant_dynamic-update-slice_fusion.2.rest_0_, ...), custom_call_target="tpu_custom_call" | custom-call | tf_op jit(solution)/shard_map/pallas_call | solution.py:296
  (83 shorter events, 21.4 us)
Async XLA Ops:
  8.1 4.8 %collective-permute-start = (bf16[768,256]{1,0:T(8,128)(2,1)S(1)}, bf16[768,256]{1,0:T(8,128)(2,1)}, u32[]{:S(2)}, u32[]{:S(2)}) collective-permute-start(bf16[768,256]{1,0:T(8,128)(2,1)S(1)} %get-tuple-element.35), channel_id=1, source_target_pairs={{0,8},{8,0},{1,9},{9,1},{2,10},{10,2},{3,11},{11,3},{4,12},{12,4},... | collective-permute-start | bytes 1179656 | tf_op jit(solution)/shard_map/ppermute | solution.py:39
  11.4 3.3 %collective-permute-start.4 = (bf16[768,256]{1,0:T(8,128)(2,1)S(1)}, bf16[768,256]{1,0:T(8,128)(2,1)}, u32[]{:S(2)}, u32[]{:S(2)}) collective-permute-start(bf16[768,256]{1,0:T(8,128)(2,1)S(1)} %get-tuple-element.37), channel_id=1, source_target_pairs={{0,8},{8,0},{1,9},{9,1},{2,10},{10,2},{3,11},{11,3},{4,12},{12,4},... | collective-permute-start | bytes 1179656 | tf_op jit(solution)/shard_map/ppermute | solution.py:39
  13.8 5.8 %collective-permute-start.1 = (bf16[384,256]{1,0:T(8,128)(2,1)S(1)}, bf16[384,256]{1,0:T(8,128)(2,1)S(1)}, u32[]{:S(2)}, u32[]{:S(2)}) collective-permute-start(bf16[384,256]{1,0:T(8,128)(2,1)S(1)} %add_convert_fusion.3), channel_id=1, source_target_pairs={{0,16},{8,56},{16,0},{24,40},{32,48},{40,24},{48,32},{56,8},{1,17}... | collective-permute-start | bytes 589832 | tf_op jit(solution)/shard_map/ppermute | solution.py:39
  15.6 6.1 %collective-permute-start.5 = (bf16[384,256]{1,0:T(8,128)(2,1)S(1)}, bf16[384,256]{1,0:T(8,128)(2,1)S(1)}, u32[]{:S(2)}, u32[]{:S(2)}) collective-permute-start(bf16[384,256]{1,0:T(8,128)(2,1)S(1)} %add_convert_fusion.2), channel_id=1, source_target_pairs={{0,16},{8,56},{16,0},{24,40},{32,48},{40,24},{48,32},{56,8},{1,17}... | collective-permute-start | bytes 589832 | tf_op jit(solution)/shard_map/ppermute | solution.py:39
  20.6 3.6 %collective-permute-start.2 = (bf16[192,256]{1,0:T(8,128)(2,1)S(1)}, bf16[192,256]{1,0:T(8,128)(2,1)S(1)}, u32[]{:S(2)}, u32[]{:S(2)}) collective-permute-start(bf16[192,256]{1,0:T(8,128)(2,1)S(1)} %add_convert_fusion.15), channel_id=1, source_target_pairs={{0,48},{8,24},{16,32},{24,8},{32,16},{40,56},{48,0},{56,40},{1,49}... | collective-permute-start | bytes 294920 | tf_op jit(solution)/shard_map/ppermute | solution.py:39
  22.7 6.9 %collective-permute-start.6 = (bf16[192,256]{1,0:T(8,128)(2,1)S(1)}, bf16[192,256]{1,0:T(8,128)(2,1)S(1)}, u32[]{:S(2)}, u32[]{:S(2)}) collective-permute-start(bf16[192,256]{1,0:T(8,128)(2,1)S(1)} %add_convert_fusion.12), channel_id=1, source_target_pairs={{0,48},{8,24},{16,32},{24,8},{32,16},{40,56},{48,0},{56,40},{1,49}... | collective-permute-start | bytes 294920 | tf_op jit(solution)/shard_map/ppermute | solution.py:39
  25.1 7.9 %collective-permute-start.3 = (bf16[192,256]{1,0:T(8,128)(2,1)S(1)}, bf16[192,256]{1,0:T(8,128)(2,1)S(1)}, u32[]{:S(2)}, u32[]{:S(2)}) collective-permute-start(bf16[192,256]{1,0:T(8,128)(2,1)S(1)} %add_convert_fusion.14), channel_id=1, source_target_pairs={{0,64},{8,200},{64,0},{72,136},{128,192},{136,72},{192,128},{200,8... | collective-permute-start | bytes 294920 | tf_op jit(solution)/shard_map/ppermute | solution.py:39
  30.5 6.6 %collective-permute-start.7 = (bf16[192,256]{1,0:T(8,128)(2,1)S(1)}, bf16[192,256]{1,0:T(8,128)(2,1)S(1)}, u32[]{:S(2)}, u32[]{:S(2)}) collective-permute-start(bf16[192,256]{1,0:T(8,128)(2,1)S(1)} %add_convert_fusion.11), channel_id=1, source_target_pairs={{0,64},{8,200},{64,0},{72,136},{128,192},{136,72},{192,128},{200,8... | collective-permute-start | bytes 294920 | tf_op jit(solution)/shard_map/ppermute | solution.py:39
  33.0 6.0 %collective-permute-start.8 = (bf16[192,256]{1,0:T(8,128)(2,1)S(1)}, bf16[192,256]{1,0:T(8,128)(2,1)S(1)}, u32[]{:S(2)}, u32[]{:S(2)}) collective-permute-start(bf16[192,256]{1,0:T(8,128)(2,1)S(1)} %add_convert_fusion.13.refs_0_), channel_id=1, source_target_pairs={{0,192},{8,72},{64,128},{72,8},{128,64},{136,200},{192,0},{200,136... | collective-permute-start | bytes 294920 | tf_op jit(solution)/shard_map/ppermute | solution.py:39
  37.2 5.5 %collective-permute-start.9 = (bf16[192,256]{1,0:T(8,128)(2,1)S(1)}, bf16[192,256]{1,0:T(8,128)(2,1)S(1)}, u32[]{:S(2)}, u32[]{:S(2)}) collective-permute-start(bf16[192,256]{1,0:T(8,128)(2,1)S(1)} %add_convert_fusion.10.refs_1_), channel_id=1, source_target_pairs={{0,192},{8,72},{64,128},{72,8},{128,64},{136,200},{192,0},{200,136... | collective-permute-start | bytes 294920 | tf_op jit(solution)/shard_map/ppermute | solution.py:39
  43.6 4.5 %collective-permute-start.11 = (bf16[192,512]{1,0:T(8,128)(2,1)S(1)}, bf16[192,512]{1,0:T(8,128)(2,1)S(1)}, u32[]{:S(2)}, u32[]{:S(2)}) collective-permute-start(bf16[192,512]{1,0:T(8,128)(2,1)S(1)} %get-tuple-element.41), channel_id=1, source_target_pairs={{0,48},{8,24},{16,32},{24,8},{32,16},{40,56},{48,0},{56,40},{1,49}... | collective-permute-start | bytes 589832 | tf_op jit(solution)/shard_map/ppermute | solution.py:39
  48.1 21.8 %collective-permute-start.12 = (bf16[384,512]{1,0:T(8,128)(2,1)S(1)}, bf16[384,512]{1,0:T(8,128)(2,1)S(1)}, u32[]{:S(2)}, u32[]{:S(2)}) collective-permute-start(bf16[384,512]{1,0:T(8,128)(2,1)S(1)} %constant_dynamic-update-slice_fusion.rest_0_), channel_id=1, source_target_pairs={{0,16},{8,56},{16,0},{24,40},{32,48},{40,24},{48,32},{56,8},{1,17}... | collective-permute-start | bytes 1179656 | tf_op jit(solution)/shard_map/ppermute | solution.py:39
  50.8 35.4 %collective-permute-start.10 = (bf16[512,512]{1,0:T(8,128)(2,1)S(1)}, bf16[512,512]{1,0:T(8,128)(2,1)S(1)}, u32[]{:S(2)}, u32[]{:S(2)}) collective-permute-start(bf16[512,512]{1,0:T(8,128)(2,1)S(1)} %slice.9), channel_id=1, source_target_pairs={{0,8},{8,16},{16,24},{24,32},{32,40},{40,48},{48,56},{56,64},{64,7... | collective-permute-start | bytes 1572872 | tf_op jit(solution)/shard_map/ppermute | solution.py:361
  59.9 18.9 %all-to-all-start = ((f32[64,8,128]{2,1,0:T(8,128)}), f32[64,8,128]{2,1,0:T(8,128)S(1)}, u32[]{:S(2)}, u32[]{:S(2)}) async-start(f32[64,8,128]{2,1,0:T(8,128)} %get-tuple-element.40), calls=%async_computation | async-start | bytes 524288 | tf_op jit(solution)/shard_map/all_to_all | solution.py:72
  69.1 9.7 %collective-permute-start.13 = (bf16[384,512]{1,0:T(8,128)(2,1)S(1)}, bf16[384,512]{1,0:T(8,128)(2,1)S(1)}, u32[]{:S(2)}, u32[]{:S(2)}) collective-permute-start(bf16[384,512]{1,0:T(8,128)(2,1)S(1)} %constant_dynamic-update-slice_fusion.rest_0_), channel_id=1, source_target_pairs={{0,8},{8,0},{1,9},{9,1},{2,10},{10,2},{3,11},{11,3},{4,12},{12,4},... | collective-permute-start | bytes 1179656 | tf_op jit(solution)/shard_map/ppermute | solution.py:39
  69.9 9.0 %collective-permute-start.14 = (bf16[384,512]{1,0:T(8,128)(2,1)S(1)}, bf16[384,512]{1,0:T(8,128)(2,1)S(1)}, u32[]{:S(2)}, u32[]{:S(2)}) collective-permute-start(bf16[384,512]{1,0:T(8,128)(2,1)S(1)} %collective-permute-done.12.rest_1_), channel_id=1, source_target_pairs={{0,8},{8,0},{1,9},{9,1},{2,10},{10,2},{3,11},{11,3},{4,12},{12,4},... | collective-permute-start | bytes 1179656 | tf_op jit(solution)/shard_map/ppermute | solution.py:39
  86.7 7.0 %collective-permute-start.18 = (bf16[768,256]{1,0:T(8,128)(2,1)S(1)}, bf16[768,256]{1,0:T(8,128)(2,1)S(1)}, u32[]{:S(2)}, u32[]{:S(2)}) collective-permute-start(bf16[768,256]{1,0:T(8,128)(2,1)S(1)} %get-tuple-element.49), channel_id=1, source_target_pairs={{0,8},{8,0},{1,9},{9,1},{2,10},{10,2},{3,11},{11,3},{4,12},{12,4},... | collective-permute-start | bytes 1179656 | tf_op jit(solution)/shard_map/ppermute | solution.py:39
  86.8 7.7 %collective-permute-start.21 = (bf16[128,512]{1,0:T(8,128)(2,1)S(1)}, bf16[128,512]{1,0:T(8,128)(2,1)S(1)}, u32[]{:S(2)}, u32[]{:S(2)}) collective-permute-start(bf16[128,512]{1,0:T(8,128)(2,1)S(1)} %slice.11), channel_id=1, source_target_pairs={{0,8},{8,16},{16,24},{24,32},{32,40},{40,48},{48,56},{56,64},{64,7... | collective-permute-start | bytes 393224 | tf_op jit(solution)/shard_map/ppermute | solution.py:320
  89.5 7.2 %collective-permute-start.16 = (bf16[384,256]{1,0:T(8,128)(2,1)S(1)}, bf16[384,256]{1,0:T(8,128)(2,1)S(1)}, u32[]{:S(2)}, u32[]{:S(2)}) collective-permute-start(bf16[384,256]{1,0:T(8,128)(2,1)S(1)} %add_convert_fusion.1), channel_id=1, source_target_pairs={{0,16},{8,56},{16,0},{24,40},{32,48},{40,24},{48,32},{56,8},{1,17}... | collective-permute-start | bytes 589832 | tf_op jit(solution)/shard_map/ppermute | solution.py:39
  93.7 5.8 %collective-permute-start.19 = (bf16[384,256]{1,0:T(8,128)(2,1)S(1)}, bf16[384,256]{1,0:T(8,128)(2,1)S(1)}, u32[]{:S(2)}, u32[]{:S(2)}) collective-permute-start(bf16[384,256]{1,0:T(8,128)(2,1)S(1)} %add_convert_fusion), channel_id=1, source_target_pairs={{0,16},{8,56},{16,0},{24,40},{32,48},{40,24},{48,32},{56,8},{1,17}... | collective-permute-start | bytes 589832 | tf_op jit(solution)/shard_map/ppermute | solution.py:39
  94.5 12.5 %collective-permute-start.22 = (bf16[384,512]{1,0:T(8,128)(2,1)S(1)}, bf16[384,512]{1,0:T(8,128)(2,1)S(1)}, u32[]{:S(2)}, u32[]{:S(2)}) collective-permute-start(bf16[384,512]{1,0:T(8,128)(2,1)S(1)} %slice.10), channel_id=1, source_target_pairs={{0,8},{8,16},{16,24},{24,32},{32,40},{40,48},{48,56},{56,64},{64,7... | collective-permute-start | bytes 1179656 | tf_op jit(solution)/shard_map/ppermute | solution.py:320
  96.7 5.4 %collective-permute-start.17 = (bf16[192,256]{1,0:T(8,128)(2,1)S(1)}, bf16[192,256]{1,0:T(8,128)(2,1)S(1)}, u32[]{:S(2)}, u32[]{:S(2)}) collective-permute-start(bf16[192,256]{1,0:T(8,128)(2,1)S(1)} %add_convert_fusion.9), channel_id=1, source_target_pairs={{0,48},{8,24},{16,32},{24,8},{32,16},{40,56},{48,0},{56,40},{1,49}... | collective-permute-start | bytes 294920 | tf_op jit(solution)/shard_map/ppermute | solution.py:39
  99.5 6.3 %collective-permute-start.20 = (bf16[192,256]{1,0:T(8,128)(2,1)S(1)}, bf16[192,256]{1,0:T(8,128)(2,1)S(1)}, u32[]{:S(2)}, u32[]{:S(2)}) collective-permute-start(bf16[192,256]{1,0:T(8,128)(2,1)S(1)} %add_convert_fusion.7), channel_id=1, source_target_pairs={{0,48},{8,24},{16,32},{24,8},{32,16},{40,56},{48,0},{56,40},{1,49}... | collective-permute-start | bytes 294920 | tf_op jit(solution)/shard_map/ppermute | solution.py:39
  102.2 7.5 %collective-permute-start.23 = (bf16[192,256]{1,0:T(8,128)(2,1)S(1)}, bf16[192,256]{1,0:T(8,128)(2,1)S(1)}, u32[]{:S(2)}, u32[]{:S(2)}) collective-permute-start(bf16[192,256]{1,0:T(8,128)(2,1)S(1)} %add_convert_fusion.8), channel_id=1, source_target_pairs={{0,64},{8,200},{64,0},{72,136},{128,192},{136,72},{192,128},{200,8... | collective-permute-start | bytes 294920 | tf_op jit(solution)/shard_map/ppermute | solution.py:39
  105.9 5.8 %collective-permute-start.24 = (bf16[192,256]{1,0:T(8,128)(2,1)S(1)}, bf16[192,256]{1,0:T(8,128)(2,1)S(1)}, u32[]{:S(2)}, u32[]{:S(2)}) collective-permute-start(bf16[192,256]{1,0:T(8,128)(2,1)S(1)} %add_convert_fusion.6), channel_id=1, source_target_pairs={{0,64},{8,200},{64,0},{72,136},{128,192},{136,72},{192,128},{200,8... | collective-permute-start | bytes 294920 | tf_op jit(solution)/shard_map/ppermute | solution.py:39
  111.8 6.4 %collective-permute-start.25 = (bf16[192,256]{1,0:T(8,128)(2,1)S(1)}, bf16[192,256]{1,0:T(8,128)(2,1)S(1)}, u32[]{:S(2)}, u32[]{:S(2)}) collective-permute-start(bf16[192,256]{1,0:T(8,128)(2,1)S(1)} %add_convert_fusion.5.refs_0_), channel_id=1, source_target_pairs={{0,192},{8,72},{64,128},{72,8},{128,64},{136,200},{192,0},{200,136... | collective-permute-start | bytes 294920 | tf_op jit(solution)/shard_map/ppermute | solution.py:39
  112.5 6.9 %collective-permute-start.26 = (bf16[192,256]{1,0:T(8,128)(2,1)S(1)}, bf16[192,256]{1,0:T(8,128)(2,1)S(1)}, u32[]{:S(2)}, u32[]{:S(2)}) collective-permute-start(bf16[192,256]{1,0:T(8,128)(2,1)S(1)} %add_convert_fusion.4.refs_1_), channel_id=1, source_target_pairs={{0,192},{8,72},{64,128},{72,8},{128,64},{136,200},{192,0},{200,136... | collective-permute-start | bytes 294920 | tf_op jit(solution)/shard_map/ppermute | solution.py:39
  120.3 4.5 %collective-permute-start.27 = (bf16[192,512]{1,0:T(8,128)(2,1)S(1)}, bf16[192,512]{1,0:T(8,128)(2,1)S(1)}, u32[]{:S(2)}, u32[]{:S(2)}) collective-permute-start(bf16[192,512]{1,0:T(8,128)(2,1)S(1)} %get-tuple-element.65), channel_id=1, source_target_pairs={{0,48},{8,24},{16,32},{24,8},{32,16},{40,56},{48,0},{56,40},{1,49}... | collective-permute-start | bytes 589832 | tf_op jit(solution)/shard_map/ppermute | solution.py:39
  125.5 21.4 %collective-permute-start.28 = (bf16[384,512]{1,0:T(8,128)(2,1)}, bf16[384,512]{1,0:T(8,128)(2,1)}, u32[]{:S(2)}, u32[]{:S(2)}) collective-permute-start(bf16[384,512]{1,0:T(8,128)(2,1)} %constant_dynamic-update-slice_fusion.2.rest_0_), channel_id=1, source_target_pairs={{0,16},{8,56},{16,0},{24,40},{32,48},{40,24},{48,32},{56,8},{1,17}... | collective-permute-start | bytes 1179656 | tf_op jit(solution)/shard_map/ppermute | solution.py:39
  133.2 22.9 %all-to-all-start.1 = ((f32[64,8,128]{2,1,0:T(8,128)}), f32[64,8,128]{2,1,0:T(8,128)S(1)}, u32[]{:S(2)}, u32[]{:S(2)}) async-start(f32[64,8,128]{2,1,0:T(8,128)} %copy-done.6), calls=%async_computation.1 | async-start | bytes 524288 | tf_op jit(solution)/shard_map/all_to_all | solution.py:72
  146.3 9.7 %collective-permute-start.29 = (bf16[384,512]{1,0:T(8,128)(2,1)}, bf16[384,512]{1,0:T(8,128)(2,1)}, u32[]{:S(2)}, u32[]{:S(2)}) collective-permute-start(bf16[384,512]{1,0:T(8,128)(2,1)} %constant_dynamic-update-slice_fusion.2.rest_0_), channel_id=1, source_target_pairs={{0,8},{8,0},{1,9},{9,1},{2,10},{10,2},{3,11},{11,3},{4,12},{12,4},... | collective-permute-start | bytes 1179656 | tf_op jit(solution)/shard_map/ppermute | solution.py:39
  146.9 9.2 %collective-permute-start.30 = (bf16[384,512]{1,0:T(8,128)(2,1)}, bf16[384,512]{1,0:T(8,128)(2,1)}, u32[]{:S(2)}, u32[]{:S(2)}) collective-permute-start(bf16[384,512]{1,0:T(8,128)(2,1)} %collective-permute-done.28.rest_1_), channel_id=1, source_target_pairs={{0,8},{8,0},{1,9},{9,1},{2,10},{10,2},{3,11},{11,3},{4,12},{12,4},... | collective-permute-start | bytes 1179656 | tf_op jit(solution)/shard_map/ppermute | solution.py:39
  (8 other events, 136.9 us)

commit v2 on v1

--- a/solution.py
+++ b/solution.py
@@ -18,7 +18,7 @@
 TILE = 256
 CHUNKS = 2
 SHARES = 64
-EARLY = 128
+EARLY = 256
 
 fast_rate = 0.01
 epsilon = 1e-06
@@ -57,15 +57,6 @@
 
 def swap_core(value):
     return exchange(value, ("core",), lambda i: i ^ 1)
-
-
-def chained(parts, send):
-    arrived = []
-    for value in parts:
-        if arrived:
-            value, arrived[-1] = lax.optimization_barrier((value, arrived[-1]))
-        arrived.append(send(value))
-    return arrived
 
 
 def spread(squares):
@@ -127,7 +118,7 @@
 
 
 def finish_kernel(*refs):
-    total_ref, square_ref = refs[2 * CHUNKS :]
+    total_ref, square_hbm, square_ref, sem = refs[2 * CHUNKS :]
     wide = HID // CHUNKS
     for c in range(CHUNKS):
         total = refs[c][...].astype(f32) + refs[CHUNKS + c][...].astype(f32)
@@ -136,6 +127,9 @@
         square = square if c == 0 else before + square
         before = square
     square_ref[...] = jnp.broadcast_to(jnp.sum(square, axis=1, keepdims=True), (8, 128))[None] + jnp.zeros(square_ref.shape, f32)
+    leave = pltpu.make_async_copy(square_ref, square_hbm, sem)
+    leave.start()
+    leave.wait()
 
 
 def fetch(sources, targets, sem):
@@ -145,14 +139,33 @@
     return copies
 
 
-def grads(place, keys_ref, targets_ref, rate_ref, wb_ref, grad_ref, outs):
+def rates_of(block, meta_ref, rate_ref):
+    count = rate_ref.shape[1]
+    position = meta_ref[0] + lax.broadcasted_iota(jnp.int32, (1, count), 1)
+    mine = (position < meta_ref[2]) if block == 0 else (position >= meta_ref[2])
+    rates = jnp.broadcast_to(jnp.where(mine, rate_ref[...], 0.0), (128, count))
+    return jnp.transpose(rates)[:, 0:1]
+
+
+def grads(block, meta_ref, keys_ref, targets_ref, rate_ref, wb_ref, grad_ref, outs, ready=lambda what: None):
+    place = meta_ref[3]
+    rates = rates_of(block, meta_ref, rate_ref)
+    ready(3)
     keys = keys_ref[...]
-    d_out = (-rate_ref[...] * targets_ref[...].astype(f32)).astype(bf16)
+    d_out = None
     half, wide = ROWS // 2, HID // CHUNKS
     for c in range(CHUNKS):
         cols = slice(c * wide, (c + 1) * wide)
+        if c == 0:
+            ready(0)
         first = dot(keys, wb_ref[0:HD, cols], 1, 0)
+        if c == 0:
+            ready(1)
         third = dot(keys, wb_ref[HD : 2 * HD, cols], 1, 0)
+        if c == 0:
+            ready(4)
+            d_out = (-rates * targets_ref[...].astype(f32)).astype(bf16)
+            ready(2)
         d_act = dot(d_out, wb_ref[2 * HD :, cols], 1, 0)
         sigma = jax.nn.sigmoid(first)
         swish = first * sigma
@@ -166,22 +179,24 @@
         outs[CHUNKS + c][...] = grad_ref[pl.ds(pl.multiple_of(place * half, half), half)]
 
 
-def first_kernel(place_ref, keys_hbm, targets_hbm, rate_ref, w_hbm, wb_hbm, *rest):
+def first_kernel(meta_ref, keys_hbm, targets_hbm, rate_ref, w_hbm, wb_hbm, *rest):
     outs, (grad_ref, keys_ref, targets_ref, w_ref, wb_ref, sem) = rest[: 2 * CHUNKS], rest[2 * CHUNKS :]
     thirds = [pl.ds(i * HD, HD) for i in range(3)]
-    copies = fetch(
-        [w_hbm.at[t] for t in thirds] + [keys_hbm, targets_hbm],
-        [w_ref.at[t] for t in thirds] + [keys_ref, targets_ref],
-        sem,
-    )
-    for copy, third in zip(copies, thirds):
-        copy.wait()
-        wb_ref[third] = w_ref[third].astype(bf16)
+    sources = [w_hbm.at[t] for t in thirds] + [keys_hbm, targets_hbm]
+    targets = [w_ref.at[t] for t in thirds] + [keys_ref, targets_ref]
+    copies = [pltpu.make_async_copy(a, b, sem.at[i]) for i, (a, b) in enumerate(zip(sources, targets))]
+    for i in (3, 0, 1, 4, 2):
+        copies[i].start()
+
+    def ready(what):
+        copies[what].wait()
+        if what < 3:
+            wb_ref[thirds[what]] = w_ref[thirds[what]].astype(bf16)
+        if what == 2:
+            leave.start()
+
     leave = pltpu.make_async_copy(wb_ref, wb_hbm, sem.at[5])
-    leave.start()
-    copies[3].wait()
-    copies[4].wait()
-    grads(place_ref[0], keys_ref, targets_ref, rate_ref, wb_ref, grad_ref, outs)
+    grads(0, meta_ref, keys_ref, targets_ref, rate_ref, wb_ref, grad_ref, outs, ready)
     leave.wait()
 
 
@@ -207,7 +222,7 @@
     return copies
 
 
-def second_kernel(place_ref, starts_ref, square_ref, keys_hbm, targets_hbm, rate_ref, w_hbm, *rest):
+def second_kernel(meta_ref, starts_ref, square_ref, keys_hbm, targets_hbm, rate_ref, w_hbm, *rest):
     pieces, (out_ref, wb_ref, *outs) = rest[:4], rest[4 : 6 + 2 * CHUNKS]
     grad_ref, new_ref, sem, keys_ref, targets_ref, w_ref, fetched = rest[6 + 2 * CHUNKS :]
     spans = piece_rows(starts_ref)
@@ -219,7 +234,7 @@
     copies = renew(starts_ref, square_ref, w_ref, pieces, new_ref, out_ref, sem, wb_ref, arrive)
     for copy in arrive[8:]:
         copy.wait()
-    grads(place_ref[0], keys_ref, targets_ref, rate_ref, wb_ref, grad_ref, outs)
+    grads(1, meta_ref, keys_ref, targets_ref, rate_ref, wb_ref, grad_ref, outs)
     for copy in copies:
         copy.wait()
 
@@ -230,13 +245,13 @@
         copy.wait()
 
 
-def attend_kernel(meta_ref, q_ref, halo_k_ref, k_ref, halo_v0, halo_v1, v_ref, out_ref, halo_v_ref):
+def attend_kernel(meta_ref, q_ref, halo_ref, k_ref, late_v_ref, v_ref, out_ref, halo_v_ref):
     local = q_ref.shape[0]
     anchor, width = meta_ref[0], meta_ref[1]
     scale = HD ** (-0.5)
-    halo_v_ref[0:EARLY] = halo_v0[...]
-    halo_v_ref[EARLY:] = halo_v1[...]
-    held = [(halo_k_ref, halo_v_ref, -WIN, WIN), (k_ref, v_ref, 0, local)]
+    halo_v_ref[0:EARLY] = halo_ref[WIN:]
+    halo_v_ref[EARLY:] = late_v_ref[...]
+    held = [(halo_ref, halo_v_ref, -WIN, WIN), (k_ref, v_ref, 0, local)]
     for start in range(0, local, TILE):
         spans = []
         for keys, values, base, count in held:
@@ -317,14 +332,11 @@
     count = lax.axis_size(SEQ)
     onward = [(i, i + 1) for i in range(count - 1)]
     tail = local - WIN
-    halo_v = chained([values[tail : tail + EARLY], values[tail + EARLY :]], lambda v: lax.ppermute(v, SEQ, onward))
-    positions = anchor + jnp.arange(local, dtype=jnp.int32)[:, None]
-    first_block = (positions < split[0]).astype(f32)
-    rate_zero = token_rate * first_block
-    rate_one = token_rate * (1.0 - first_block)
-    core = lax.axis_index("core").astype(jnp.int32).reshape(1)
+    halo_v = lax.ppermute(values[tail + EARLY :], SEQ, onward)
+    with_gather = jnp.concatenate([keys[tail:], values[tail : tail + EARLY]], axis=0)
+    rate = token_rate.reshape(1, local)
     starts = piece_starts()
-    meta = jnp.stack([anchor, window[0], split[0]]).astype(jnp.int32)
+    meta = jnp.stack([anchor, window[0], split[0], lax.axis_index("core")]).astype(jnp.int32)
     weights_zero = fast_init.reshape(ROWS, HID)
     half = ROWS // 2
     wide = [array((half, HID // CHUNKS), kind) for kind in (bf16, f32) for _ in range(CHUNKS)]
@@ -337,7 +349,7 @@
         first_kernel,
         [SMEM_SPEC, HBM_SPEC, HBM_SPEC, VMEM_SPEC, HBM_SPEC],
         [pltpu.HBM((ROWS, HID), bf16)] + wide,
-        (core, in_hbm(keys), in_hbm(targets), rate_zero, in_hbm(weights_zero)),
+        (meta, in_hbm(keys), in_hbm(targets), rate, in_hbm(weights_zero)),
         24,
         [grad] + fetched + [pltpu.VMEM((ROWS, HID), f32), pltpu.VMEM((ROWS, HID), bf16), pltpu.SemaphoreType.DMA((6,))],
         [HBM_SPEC] + [VMEM_SPEC] * (2 * CHUNKS),
@@ -347,9 +359,11 @@
         total, square = call(
             finish_kernel,
             [VMEM_SPEC] * (2 * CHUNKS),
-            [array((ROWS // 8, HID), bf16), array((SHARES, 8, 128), f32)],
+            [array((ROWS // 8, HID), bf16), pltpu.HBM((SHARES, 8, 128), f32)],
             (*mine, *other),
             8,
+            [pltpu.VMEM((SHARES, 8, 128), f32), pltpu.SemaphoreType.DMA],
+            [VMEM_SPEC, HBM_SPEC],
         )
         if later is not None:
             total, later = lax.optimization_barrier((total, later))
@@ -357,26 +371,26 @@
 
     kept = {}
 
-    square, pieces, send = finished(*reduced(halved[:CHUNKS], halved[CHUNKS:]), keys[tail:])
-    halo_k = lax.ppermute(send, SEQ, onward)
+    square, pieces, send = finished(*reduced(halved[:CHUNKS], halved[CHUNKS:]), with_gather)
+    halo = lax.ppermute(send, SEQ, onward)
     weights_one, wb_one, *halved = call(
         second_kernel,
         [SMEM_SPEC] * 2 + [VMEM_SPEC, HBM_SPEC, HBM_SPEC, VMEM_SPEC, HBM_SPEC] + [VMEM_SPEC] * 4,
         [pltpu.HBM((ROWS, HID), f32), array((ROWS, HID), bf16)] + wide,
-        (core, starts, square, in_hbm(keys), in_hbm(targets), rate_one, in_hbm(weights_zero), *pieces),
+        (meta, starts, square, in_hbm(keys), in_hbm(targets), rate, in_hbm(weights_zero), *pieces),
         24,
         [grad] + renewal + fetched + [pltpu.VMEM((ROWS, HID), f32), pltpu.SemaphoreType.DMA((10,))],
         [HBM_SPEC] + [VMEM_SPEC] * (1 + 2 * CHUNKS),
     )
-    kept["halo"], halved = lax.optimization_barrier((halo_k, halved))
+    kept["halo"], halved = lax.optimization_barrier((halo, halved))
 
     def attend(before, after):
         query, _ = lax.optimization_barrier((queries, before))
         attn = call(
             attend_kernel,
-            [SMEM_SPEC] + [VMEM_SPEC] * 6,
+            [SMEM_SPEC] + [VMEM_SPEC] * 5,
             array((local, HD), f32),
-            (meta, query, kept["halo"], keys, *halo_v, values),
+            (meta, query, kept["halo"], keys, halo_v, values),
             20,
             [pltpu.VMEM((WIN, HD), bf16)],
         )

time: 160 us -> 161 us (level)
  waiting for transfers between devices: 46.7 us -> 40.8 us
  starting transfers between devices: 76.9 us -> 79.7 us
  other arithmetic: 6.22 us -> 8.55 us
  Pallas kernels: 24.1 us -> 25.9 us
    all_to_all x2, starting transfers between devices: 22.3 us -> 28.7 us  [spread(): return lax.all_to_all(squares, ('x', 'core', 'head'), 0, 0, tiled=True)]
    ppermute x28, waiting for transfers between devices: 28.8 us -> 22.9 us  [exchange(): lax.ppermute(value, mesh_axes, [(i, partner(i)) for i in range(count)])]
    ppermute x3 -> x2, starting transfers between devices: 13.6 us -> 10.3 us  [the longest x1 8.4 us: per_device(): halo = lax.ppermute(send, SEQ, onward)]
    pallas_call x7, Pallas kernels: 24.1 us -> 25.9 us  [call(): pl.pallas_call(kernel, out_shape=outs, in_specs=specs, out_specs=jax.tree...]
  transfers between devices with their start and end apart: 33 -> 32, of which waited for: 16 -> 16; matrix products, arithmetic and copies ran while one was open for 4% -> 6% of each run, Pallas kernels for 9% -> 9%
where the time goes in v2:
time: 161 us; the launch traced here: 160 us
  starting transfers between devices  79.7 us (50%)
  waiting for transfers between devices  40.8 us (25%)
  Pallas kernels  25.9 us (16%)
  other arithmetic  8.55 us (5%)
  local copies, waits for them, and re-layouts  2.98 us (2%)
  between operations  2.37 us (1%)
    ppermute x28, starting transfers between devices, exchange(): lax.ppermute(value, mesh_axes, [(i, partner(i)) for i in range(count)])  40.7 us
    all_to_all x2, starting transfers between devices, spread(): return lax.all_to_all(squares, ('x', 'core', 'head'), 0, 0, tiled=True)  28.7 us
    pallas_call x7, Pallas kernels, call(): pl.pallas_call(kernel, out_shape=outs, in_specs=specs, out_specs=jax.tree...  25.9 us
    ppermute x28, waiting for transfers between devices, exchange(): lax.ppermute(value, mesh_axes, [(i, partner(i)) for i in range(count)])  22.9 us
    all_to_all x2, waiting for transfers between devices, spread(): return lax.all_to_all(squares, ('x', 'core', 'head'), 0, 0, tiled=True)  17.9 us
    ppermute x1, starting transfers between devices, per_device(): halo = lax.ppermute(send, SEQ, onward)  8.4 us
    convert_element_type x4, other arithmetic, reduced(): two(c, (1 - first) * half, half).astype(bf16)  3.39 us
  transfers between devices with their start and end apart: 32, of which 16 were waited for; matrix products, arithmetic and copies ran while one was open for 6% of the time, Pallas kernels for 9%

profile of v2, /device:TPU:1, one launch (start us, length us, event | category | flops | bytes accessed | tf_op | source)
XLA Modules:
  0.0 160.3 jit_solution(1108219778175895245)
XLA Ops:
  2.7 6.3 %shard_map.95 = (bf16[1536,512]{1,0:T(8,128)(2,1)}, bf16[768,256]{1,0:T(8,128)(2,1)S(1)}, bf16[768,256]{1,0:T(8,128)(2,1)S(1)}, f32[768,256]{1,0:T(8,128)S(1)}, f32[768,256]{1,0:T(8,128)S(1)}) custom-call(s32[4]{0:T(128)S(1)} %pad_add_fusion.meta_ref, bf16[768,512]{1,0:T(8,128)(2,1)} %k_ref.1, bf16[768,512]{1,0:T(8,128)(2,1)} %targets_hbm.3, ...), custom_call_target="tpu_custom_call" | custom-call | tf_op jit(solution)/shard_map/pallas_call | solution.py:311
  9.0 3.3 %collective-permute-start = (bf16[768,256]{1,0:T(8,128)(2,1)S(1)}, bf16[768,256]{1,0:T(8,128)(2,1)}, u32[]{:S(2)}, u32[]{:S(2)}) collective-permute-start(bf16[768,256]{1,0:T(8,128)(2,1)S(1)} %get-tuple-element.33), channel_id=1, source_target_pairs={{0,8},{8,0},{1,9},{9,1},{2,10},{10,2},{3,11},{11,3},{4,12},{12,4},... | collective-permute-start | bytes 1179656 | tf_op jit(solution)/shard_map/ppermute | solution.py:39
  12.4 1.4 collective-permute-done
  13.8 1.6 %add_convert_fusion.3 = bf16[384,256]{1,0:T(8,128)(2,1)} fusion(f32[768,256]{1,0:T(8,128)S(1)} %get-tuple-element.32, s32[]{:T(128)S(6)} %select_n.24, bf16[768,256]{1,0:T(8,128)(2,1)} %collective-permute-done), kind=kLoop, calls=%fused_computation.4 | loop fusion | flops 294912 | bytes 786436 | tf_op jit(solution)/shard_map/convert_element_type | solution.py:96
  16.2 1.6 %add_convert_fusion.2 = bf16[384,256]{1,0:T(8,128)(2,1)} fusion(f32[768,256]{1,0:T(8,128)S(1)} %get-tuple-element.34, s32[]{:T(128)S(6)} %select_n.24, bf16[768,256]{1,0:T(8,128)(2,1)} %collective-permute-done.4), kind=kLoop, calls=%fused_computation.3 | loop fusion | flops 294912 | bytes 786436 | tf_op jit(solution)/shard_map/convert_element_type | solution.py:96
  17.9 1.9 %collective-permute-start.5 = (bf16[384,256]{1,0:T(8,128)(2,1)}, bf16[384,256]{1,0:T(8,128)(2,1)S(1)}, u32[]{:S(2)}, u32[]{:S(2)}) collective-permute-start(bf16[384,256]{1,0:T(8,128)(2,1)} %add_convert_fusion.2), channel_id=1, source_target_pairs={{0,16},{8,56},{16,0},{24,40},{32,48},{40,24},{48,32},{56,8},{1,17}... | collective-permute-start | bytes 589832 | tf_op jit(solution)/shard_map/ppermute | solution.py:39
  27.0 4.9 %collective-permute-start.3 = (bf16[192,256]{1,0:T(8,128)(2,1)S(1)}, bf16[192,256]{1,0:T(8,128)(2,1)S(1)}, u32[]{:S(2)}, u32[]{:S(2)}) collective-permute-start(bf16[192,256]{1,0:T(8,128)(2,1)S(1)} %add_convert_fusion.14), channel_id=1, source_target_pairs={{0,64},{8,200},{64,0},{72,136},{128,192},{136,72},{192,128},{200,8... | collective-permute-start | bytes 294920 | tf_op jit(solution)/shard_map/ppermute | solution.py:39
  32.9 2.4 %collective-permute-start.7 = (bf16[192,256]{1,0:T(8,128)(2,1)S(1)}, bf16[192,256]{1,0:T(8,128)(2,1)S(1)}, u32[]{:S(2)}, u32[]{:S(2)}) collective-permute-start(bf16[192,256]{1,0:T(8,128)(2,1)S(1)} %add_convert_fusion.11), channel_id=1, source_target_pairs={{0,64},{8,200},{64,0},{72,136},{128,192},{136,72},{192,128},{200,8... | collective-permute-start | bytes 294920 | tf_op jit(solution)/shard_map/ppermute | solution.py:39
  35.4 1.3 collective-permute-start.8
  36.6 2.5 %collective-permute-done.7 = bf16[192,256]{1,0:T(8,128)(2,1)S(1)} collective-permute-done((bf16[192,256]{1,0:T(8,128)(2,1)S(1)}, bf16[192,256]{1,0:T(8,128)(2,1)S(1)}, u32[]{:S(2)}, u32[]{:S(2)}) %collective-permute-start.7) | collective-permute-done | bytes 98336 | tf_op jit(solution)/shard_map/ppermute | solution.py:39
  39.2 1.8 %collective-permute-start.9 = (bf16[192,256]{1,0:T(8,128)(2,1)S(1)}, bf16[192,256]{1,0:T(8,128)(2,1)S(1)}, u32[]{:S(2)}, u32[]{:S(2)}) collective-permute-start(bf16[192,256]{1,0:T(8,128)(2,1)S(1)} %add_convert_fusion.10.refs_1_), channel_id=1, source_target_pairs={{0,192},{8,72},{64,128},{72,8},{128,64},{136,200},{192,0},{200,136... | collective-permute-start | bytes 294920 | tf_op jit(solution)/shard_map/ppermute | solution.py:39
  41.9 1.8 %collective-permute-done.9.refs_3_ = bf16[192,256]{1,0:T(8,128)(2,1)S(1)} collective-permute-done((bf16[192,256]{1,0:T(8,128)(2,1)S(1)}, bf16[192,256]{1,0:T(8,128)(2,1)S(1)}, u32[]{:S(2)}, u32[]{:S(2)}) %collective-permute-start.9) | collective-permute-done | bytes 98336 | tf_op jit(solution)/shard_map/ppermute | solution.py:39
  44.6 1.3 collective-permute-start.11
  45.9 3.3 %collective-permute-done.11 = bf16[192,512]{1,0:T(8,128)(2,1)S(1)} collective-permute-done((bf16[192,512]{1,0:T(8,128)(2,1)S(1)}, bf16[192,512]{1,0:T(8,128)(2,1)S(1)}, u32[]{:S(2)}, u32[]{:S(2)}) %collective-permute-start.11) | collective-permute-done | bytes 196640 | tf_op jit(solution)/shard_map/ppermute | solution.py:39
  49.2 3.6 %collective-permute-start.12 = (bf16[384,512]{1,0:T(8,128)(2,1)S(1)}, bf16[384,512]{1,0:T(8,128)(2,1)S(1)}, u32[]{:S(2)}, u32[]{:S(2)}) collective-permute-start(bf16[384,512]{1,0:T(8,128)(2,1)S(1)} %constant_dynamic-update-slice_fusion.rest_0_), channel_id=1, source_target_pairs={{0,16},{8,56},{16,0},{24,40},{32,48},{40,24},{48,32},{56,8},{1,17}... | collective-permute-start | bytes 1179656 | tf_op jit(solution)/shard_map/ppermute | solution.py:39
  52.9 8.4 %collective-permute-start.10 = (bf16[768,512]{1,0:T(8,128)(2,1)}, bf16[768,512]{1,0:T(8,128)(2,1)S(1)}, u32[]{:S(2)}, u32[]{:S(2)}) collective-permute-start(bf16[768,512]{1,0:T(8,128)(2,1)} %pad_maximum_fusion), channel_id=1, source_target_pairs={{0,8},{8,16},{16,24},{24,32},{32,40},{40,48},{48,56},{56,64},{64,7... | collective-permute-start | bytes 2359304 | tf_op jit(solution)/shard_map/ppermute | solution.py:375
  61.3 9.9 %all-to-all-start = ((f32[64,8,128]{2,1,0:T(8,128)}), f32[64,8,128]{2,1,0:T(8,128)S(1)}, u32[]{:S(2)}, u32[]{:S(2)}) async-start(f32[64,8,128]{2,1,0:T(8,128)} %get-tuple-element.38), calls=%async_computation | async-start | bytes 524288 | tf_op jit(solution)/shard_map/all_to_all | solution.py:63
  72.1 8.9 %all-to-all-done.square_ref = f32[64,8,128]{2,1,0:T(8,128)S(1)} async-done(((f32[64,8,128]{2,1,0:T(8,128)}), f32[64,8,128]{2,1,0:T(8,128)S(1)}, u32[]{:S(2)}, u32[]{:S(2)}) %all-to-all-start) | async-done | bytes 262176 | tf_op jit(solution)/shard_map/all_to_all | solution.py:63
  81.0 7.7 %shard_map.97 = (f32[1536,512]{1,0:T(8,128)}, bf16[1536,512]{1,0:T(8,128)(2,1)S(1)}, bf16[768,256]{1,0:T(8,128)(2,1)S(1)}, bf16[768,256]{1,0:T(8,128)(2,1)S(1)},...) custom-call(s32[4]{0:T(128)S(1)} %pad_add_fusion.meta_ref, s32[8]{0:T(128)S(1)} %broadcast_multiply_fusion.starts_ref, ...), custom_call_target="tpu_custom_call" | custom-call | tf_op jit(solution)/shard_map/pallas_call | solution.py:311
  91.6 2.4 %collective-permute-start.19 = (bf16[384,256]{1,0:T(8,128)(2,1)S(1)}, bf16[384,256]{1,0:T(8,128)(2,1)S(1)}, u32[]{:S(2)}, u32[]{:S(2)}) collective-permute-start(bf16[384,256]{1,0:T(8,128)(2,1)S(1)} %add_convert_fusion), channel_id=1, source_target_pairs={{0,16},{8,56},{16,0},{24,40},{32,48},{40,24},{48,32},{56,8},{1,17}... | collective-permute-start | bytes 589832 | tf_op jit(solution)/shard_map/ppermute | solution.py:39
  93.9 1.9 %collective-permute-start.21 = (bf16[256,512]{1,0:T(8,128)(2,1)S(1)}, bf16[256,512]{1,0:T(8,128)(2,1)S(1)}, u32[]{:S(2)}, u32[]{:S(2)}) collective-permute-start(bf16[256,512]{1,0:T(8,128)(2,1)S(1)} %copy-done.7), channel_id=1, source_target_pairs={{0,8},{8,16},{16,24},{24,32},{32,40},{40,48},{48,56},{56,64},{64,7... | collective-permute-start | bytes 786440 | tf_op jit(solution)/shard_map/ppermute | solution.py:335
  97.0 2.0 %collective-permute-done.19 = bf16[384,256]{1,0:T(8,128)(2,1)S(1)} collective-permute-done((bf16[384,256]{1,0:T(8,128)(2,1)S(1)}, bf16[384,256]{1,0:T(8,128)(2,1)S(1)}, u32[]{:S(2)}, u32[]{:S(2)}) %collective-permute-start.19) | collective-permute-done | bytes 196640 | tf_op jit(solution)/shard_map/ppermute | solution.py:39
  99.1 1.4 collective-permute-done.17
  100.5 4.1 %collective-permute-start.22 = (bf16[192,256]{1,0:T(8,128)(2,1)S(1)}, bf16[192,256]{1,0:T(8,128)(2,1)S(1)}, u32[]{:S(2)}, u32[]{:S(2)}) collective-permute-start(bf16[192,256]{1,0:T(8,128)(2,1)S(1)} %add_convert_fusion.8), channel_id=1, source_target_pairs={{0,64},{8,200},{64,0},{72,136},{128,192},{136,72},{192,128},{200,8... | collective-permute-start | bytes 294920 | tf_op jit(solution)/shard_map/ppermute | solution.py:39
  104.8 2.3 %collective-permute-start.23 = (bf16[192,256]{1,0:T(8,128)(2,1)S(1)}, bf16[192,256]{1,0:T(8,128)(2,1)S(1)}, u32[]{:S(2)}, u32[]{:S(2)}) collective-permute-start(bf16[192,256]{1,0:T(8,128)(2,1)S(1)} %add_convert_fusion.6), channel_id=1, source_target_pairs={{0,64},{8,200},{64,0},{72,136},{128,192},{136,72},{192,128},{200,8... | collective-permute-start | bytes 294920 | tf_op jit(solution)/shard_map/ppermute | solution.py:39
  107.1 2.8 %shard_map.98.attn_ref = f32[768,512]{1,0:T(8,128)S(1)} custom-call(s32[4]{0:T(128)S(1)} %pad_add_fusion.meta_ref, bf16[768,512]{1,0:T(8,128)(2,1)S(1)} %copy-done.1, bf16[768,512]{1,0:T(8,128)(2,1)S(1)} %collective-permute-done.10.halo_ref, bf16[768,512]{1,0:T(8,128)(2,1)S(1)} %copy-done, bf16[256,512]{1,0:T(8,128)(2,1)S(1)} %collective-permute-done.21.late_v_ref, ...), custom_call_target="tpu_custom_call" | custom-call | tf_op jit(solution)/shard_map/pallas_call | solution.py:311
  110.5 6.3 %collective-permute-start.25 = (bf16[192,256]{1,0:T(8,128)(2,1)S(1)}, bf16[192,256]{1,0:T(8,128)(2,1)S(1)}, u32[]{:S(2)}, u32[]{:S(2)}) collective-permute-start(bf16[192,256]{1,0:T(8,128)(2,1)S(1)} %add_convert_fusion.4.refs_1_), channel_id=1, source_target_pairs={{0,192},{8,72},{64,128},{72,8},{128,64},{136,200},{192,0},{200,136... | collective-permute-start | bytes 294920 | tf_op jit(solution)/shard_map/ppermute | solution.py:39
  117.2 4.0 %shard_map.99 = bf16[768,512]{1,0:T(8,128)(2,1)} custom-call(s32[4]{0:T(128)S(1)} %pad_add_fusion.meta_ref, bf16[768,512]{1,0:T(8,128)(2,1)S(1)} %copy-done.1, f32[768,512]{1,0:T(8,128)S(1)} %shard_map.98.attn_ref, bf16[1536,512]{1,0:T(8,128)(2,1)S(1)} %copy-done.4, bf16[1536,512]{1,0:T(8,128)(2,1)S(1)} %get-tuple-element.55.late_ref), custom_call_target="tpu_custom_call" | custom-call | tf_op jit(solution)/shard_map/pallas_call | solution.py:311
  123.6 3.8 %collective-permute-done.26 = bf16[192,512]{1,0:T(8,128)(2,1)S(1)} collective-permute-done((bf16[192,512]{1,0:T(8,128)(2,1)S(1)}, bf16[192,512]{1,0:T(8,128)(2,1)S(1)}, u32[]{:S(2)}, u32[]{:S(2)}) %collective-permute-start.26) | collective-permute-done | bytes 196640 | tf_op jit(solution)/shard_map/ppermute | solution.py:39
  128.4 18.7 %all-to-all-start.1 = ((f32[64,8,128]{2,1,0:T(8,128)}), f32[64,8,128]{2,1,0:T(8,128)S(1)}, u32[]{:S(2)}, u32[]{:S(2)}) async-start(f32[64,8,128]{2,1,0:T(8,128)} %get-tuple-element.59), calls=%async_computation.1 | async-start | bytes 524288 | tf_op jit(solution)/shard_map/all_to_all | solution.py:63
  147.8 9.1 %all-to-all-done.1.square_ref = f32[64,8,128]{2,1,0:T(8,128)S(1)} async-done(((f32[64,8,128]{2,1,0:T(8,128)}), f32[64,8,128]{2,1,0:T(8,128)S(1)}, u32[]{:S(2)}, u32[]{:S(2)}) %all-to-all-start.1) | async-done | bytes 262176 | tf_op jit(solution)/shard_map/all_to_all | solution.py:63
  156.9 3.3 %shard_map.101 = f32[1536,512]{1,0:T(8,128)} custom-call(s32[8]{0:T(128)S(1)} %broadcast_multiply_fusion.starts_ref, f32[64,8,128]{2,1,0:T(8,128)S(1)} %all-to-all-done.1.square_ref, f32[1536,512]{1,0:T(8,128)S(1)} %copy-done.2, bf16[384,512]{1,0:T(8,128)(2,1)} %constant_dynamic-update-slice_fusion.2.rest_0_, ...), custom_call_target="tpu_custom_call" | custom-call | tf_op jit(solution)/shard_map/pallas_call | solution.py:311
  (82 shorter events, 21.8 us)
Async XLA Ops:
  9.0 4.8 %collective-permute-start = (bf16[768,256]{1,0:T(8,128)(2,1)S(1)}, bf16[768,256]{1,0:T(8,128)(2,1)}, u32[]{:S(2)}, u32[]{:S(2)}) collective-permute-start(bf16[768,256]{1,0:T(8,128)(2,1)S(1)} %get-tuple-element.33), channel_id=1, source_target_pairs={{0,8},{8,0},{1,9},{9,1},{2,10},{10,2},{3,11},{11,3},{4,12},{12,4},... | collective-permute-start | bytes 1179656 | tf_op jit(solution)/shard_map/ppermute | solution.py:39
  12.3 3.9 %collective-permute-start.4 = (bf16[768,256]{1,0:T(8,128)(2,1)S(1)}, bf16[768,256]{1,0:T(8,128)(2,1)}, u32[]{:S(2)}, u32[]{:S(2)}) collective-permute-start(bf16[768,256]{1,0:T(8,128)(2,1)S(1)} %get-tuple-element.35), channel_id=1, source_target_pairs={{0,8},{8,0},{1,9},{9,1},{2,10},{10,2},{3,11},{11,3},{4,12},{12,4},... | collective-permute-start | bytes 1179656 | tf_op jit(solution)/shard_map/ppermute | solution.py:39
  15.5 6.0 %collective-permute-start.1 = (bf16[384,256]{1,0:T(8,128)(2,1)}, bf16[384,256]{1,0:T(8,128)(2,1)}, u32[]{:S(2)}, u32[]{:S(2)}) collective-permute-start(bf16[384,256]{1,0:T(8,128)(2,1)} %add_convert_fusion.3), channel_id=1, source_target_pairs={{0,16},{8,56},{16,0},{24,40},{32,48},{40,24},{48,32},{56,8},{1,17}... | collective-permute-start | bytes 589832 | tf_op jit(solution)/shard_map/ppermute | solution.py:39
  17.9 5.9 %collective-permute-start.5 = (bf16[384,256]{1,0:T(8,128)(2,1)}, bf16[384,256]{1,0:T(8,128)(2,1)S(1)}, u32[]{:S(2)}, u32[]{:S(2)}) collective-permute-start(bf16[384,256]{1,0:T(8,128)(2,1)} %add_convert_fusion.2), channel_id=1, source_target_pairs={{0,16},{8,56},{16,0},{24,40},{32,48},{40,24},{48,32},{56,8},{1,17}... | collective-permute-start | bytes 589832 | tf_op jit(solution)/shard_map/ppermute | solution.py:39
  22.5 3.6 %collective-permute-start.2 = (bf16[192,256]{1,0:T(8,128)(2,1)S(1)}, bf16[192,256]{1,0:T(8,128)(2,1)S(1)}, u32[]{:S(2)}, u32[]{:S(2)}) collective-permute-start(bf16[192,256]{1,0:T(8,128)(2,1)S(1)} %add_convert_fusion.15), channel_id=1, source_target_pairs={{0,48},{8,24},{16,32},{24,8},{32,16},{40,56},{48,0},{56,40},{1,49}... | collective-permute-start | bytes 294920 | tf_op jit(solution)/shard_map/ppermute | solution.py:39
  24.7 7.2 %collective-permute-start.6 = (bf16[192,256]{1,0:T(8,128)(2,1)S(1)}, bf16[192,256]{1,0:T(8,128)(2,1)S(1)}, u32[]{:S(2)}, u32[]{:S(2)}) collective-permute-start(bf16[192,256]{1,0:T(8,128)(2,1)S(1)} %add_convert_fusion.12), channel_id=1, source_target_pairs={{0,48},{8,24},{16,32},{24,8},{32,16},{40,56},{48,0},{56,40},{1,49}... | collective-permute-start | bytes 294920 | tf_op jit(solution)/shard_map/ppermute | solution.py:39
  27.0 8.3 %collective-permute-start.3 = (bf16[192,256]{1,0:T(8,128)(2,1)S(1)}, bf16[192,256]{1,0:T(8,128)(2,1)S(1)}, u32[]{:S(2)}, u32[]{:S(2)}) collective-permute-start(bf16[192,256]{1,0:T(8,128)(2,1)S(1)} %add_convert_fusion.14), channel_id=1, source_target_pairs={{0,64},{8,200},{64,0},{72,136},{128,192},{136,72},{192,128},{200,8... | collective-permute-start | bytes 294920 | tf_op jit(solution)/shard_map/ppermute | solution.py:39
  32.9 6.2 %collective-permute-start.7 = (bf16[192,256]{1,0:T(8,128)(2,1)S(1)}, bf16[192,256]{1,0:T(8,128)(2,1)S(1)}, u32[]{:S(2)}, u32[]{:S(2)}) collective-permute-start(bf16[192,256]{1,0:T(8,128)(2,1)S(1)} %add_convert_fusion.11), channel_id=1, source_target_pairs={{0,64},{8,200},{64,0},{72,136},{128,192},{136,72},{192,128},{200,8... | collective-permute-start | bytes 294920 | tf_op jit(solution)/shard_map/ppermute | solution.py:39
  35.4 6.5 %collective-permute-start.8 = (bf16[192,256]{1,0:T(8,128)(2,1)S(1)}, bf16[192,256]{1,0:T(8,128)(2,1)S(1)}, u32[]{:S(2)}, u32[]{:S(2)}) collective-permute-start(bf16[192,256]{1,0:T(8,128)(2,1)S(1)} %add_convert_fusion.13.refs_0_), channel_id=1, source_target_pairs={{0,192},{8,72},{64,128},{72,8},{128,64},{136,200},{192,0},{200,136... | collective-permute-start | bytes 294920 | tf_op jit(solution)/shard_map/ppermute | solution.py:39
  39.2 4.5 %collective-permute-start.9 = (bf16[192,256]{1,0:T(8,128)(2,1)S(1)}, bf16[192,256]{1,0:T(8,128)(2,1)S(1)}, u32[]{:S(2)}, u32[]{:S(2)}) collective-permute-start(bf16[192,256]{1,0:T(8,128)(2,1)S(1)} %add_convert_fusion.10.refs_1_), channel_id=1, source_target_pairs={{0,192},{8,72},{64,128},{72,8},{128,64},{136,200},{192,0},{200,136... | collective-permute-start | bytes 294920 | tf_op jit(solution)/shard_map/ppermute | solution.py:39
  44.6 4.6 %collective-permute-start.11 = (bf16[192,512]{1,0:T(8,128)(2,1)S(1)}, bf16[192,512]{1,0:T(8,128)(2,1)S(1)}, u32[]{:S(2)}, u32[]{:S(2)}) collective-permute-start(bf16[192,512]{1,0:T(8,128)(2,1)S(1)} %get-tuple-element.39), channel_id=1, source_target_pairs={{0,48},{8,24},{16,32},{24,8},{32,16},{40,56},{48,0},{56,40},{1,49}... | collective-permute-start | bytes 589832 | tf_op jit(solution)/shard_map/ppermute | solution.py:39
  49.2 22.7 %collective-permute-start.12 = (bf16[384,512]{1,0:T(8,128)(2,1)S(1)}, bf16[384,512]{1,0:T(8,128)(2,1)S(1)}, u32[]{:S(2)}, u32[]{:S(2)}) collective-permute-start(bf16[384,512]{1,0:T(8,128)(2,1)S(1)} %constant_dynamic-update-slice_fusion.rest_0_), channel_id=1, source_target_pairs={{0,16},{8,56},{16,0},{24,40},{32,48},{40,24},{48,32},{56,8},{1,17}... | collective-permute-start | bytes 1179656 | tf_op jit(solution)/shard_map/ppermute | solution.py:39
  52.9 35.9 %collective-permute-start.10 = (bf16[768,512]{1,0:T(8,128)(2,1)}, bf16[768,512]{1,0:T(8,128)(2,1)S(1)}, u32[]{:S(2)}, u32[]{:S(2)}) collective-permute-start(bf16[768,512]{1,0:T(8,128)(2,1)} %pad_maximum_fusion), channel_id=1, source_target_pairs={{0,8},{8,16},{16,24},{24,32},{32,40},{40,48},{48,56},{56,64},{64,7... | collective-permute-start | bytes 2359304 | tf_op jit(solution)/shard_map/ppermute | solution.py:375
  61.3 19.7 %all-to-all-start = ((f32[64,8,128]{2,1,0:T(8,128)}), f32[64,8,128]{2,1,0:T(8,128)S(1)}, u32[]{:S(2)}, u32[]{:S(2)}) async-start(f32[64,8,128]{2,1,0:T(8,128)} %get-tuple-element.38), calls=%async_computation | async-start | bytes 524288 | tf_op jit(solution)/shard_map/all_to_all | solution.py:63
  71.2 9.8 %collective-permute-start.13 = (bf16[384,512]{1,0:T(8,128)(2,1)S(1)}, bf16[384,512]{1,0:T(8,128)(2,1)S(1)}, u32[]{:S(2)}, u32[]{:S(2)}) collective-permute-start(bf16[384,512]{1,0:T(8,128)(2,1)S(1)} %constant_dynamic-update-slice_fusion.rest_0_), channel_id=1, source_target_pairs={{0,8},{8,0},{1,9},{9,1},{2,10},{10,2},{3,11},{11,3},{4,12},{12,4},... | collective-permute-start | bytes 1179656 | tf_op jit(solution)/shard_map/ppermute | solution.py:39
  71.9 9.1 %collective-permute-start.14 = (bf16[384,512]{1,0:T(8,128)(2,1)S(1)}, bf16[384,512]{1,0:T(8,128)(2,1)}, u32[]{:S(2)}, u32[]{:S(2)}) collective-permute-start(bf16[384,512]{1,0:T(8,128)(2,1)S(1)} %collective-permute-done.12.rest_1_), channel_id=1, source_target_pairs={{0,8},{8,0},{1,9},{9,1},{2,10},{10,2},{3,11},{11,3},{4,12},{12,4},... | collective-permute-start | bytes 1179656 | tf_op jit(solution)/shard_map/ppermute | solution.py:39
  88.7 2.2 %collective-permute-start.15 = (bf16[768,256]{1,0:T(8,128)(2,1)S(1)}, bf16[768,256]{1,0:T(8,128)(2,1)S(1)}, u32[]{:S(2)}, u32[]{:S(2)}) collective-permute-start(bf16[768,256]{1,0:T(8,128)(2,1)S(1)} %get-tuple-element.45), channel_id=1, source_target_pairs={{0,8},{8,0},{1,9},{9,1},{2,10},{10,2},{3,11},{11,3},{4,12},{12,4},... | collective-permute-start | bytes 1179656 | tf_op jit(solution)/shard_map/ppermute | solution.py:39
  89.6 1.9 %collective-permute-start.18 = (bf16[768,256]{1,0:T(8,128)(2,1)S(1)}, bf16[768,256]{1,0:T(8,128)(2,1)S(1)}, u32[]{:S(2)}, u32[]{:S(2)}) collective-permute-start(bf16[768,256]{1,0:T(8,128)(2,1)S(1)} %get-tuple-element.47), channel_id=1, source_target_pairs={{0,8},{8,0},{1,9},{9,1},{2,10},{10,2},{3,11},{11,3},{4,12},{12,4},... | collective-permute-start | bytes 1179656 | tf_op jit(solution)/shard_map/ppermute | solution.py:39
  91.0 5.8 %collective-permute-start.16 = (bf16[384,256]{1,0:T(8,128)(2,1)S(1)}, bf16[384,256]{1,0:T(8,128)(2,1)S(1)}, u32[]{:S(2)}, u32[]{:S(2)}) collective-permute-start(bf16[384,256]{1,0:T(8,128)(2,1)S(1)} %add_convert_fusion.1), channel_id=1, source_target_pairs={{0,16},{8,56},{16,0},{24,40},{32,48},{40,24},{48,32},{56,8},{1,17}... | collective-permute-start | bytes 589832 | tf_op jit(solution)/shard_map/ppermute | solution.py:39
  91.6 7.4 %collective-permute-start.19 = (bf16[384,256]{1,0:T(8,128)(2,1)S(1)}, bf16[384,256]{1,0:T(8,128)(2,1)S(1)}, u32[]{:S(2)}, u32[]{:S(2)}) collective-permute-start(bf16[384,256]{1,0:T(8,128)(2,1)S(1)} %add_convert_fusion), channel_id=1, source_target_pairs={{0,16},{8,56},{16,0},{24,40},{32,48},{40,24},{48,32},{56,8},{1,17}... | collective-permute-start | bytes 589832 | tf_op jit(solution)/shard_map/ppermute | solution.py:39
  93.9 13.1 %collective-permute-start.21 = (bf16[256,512]{1,0:T(8,128)(2,1)S(1)}, bf16[256,512]{1,0:T(8,128)(2,1)S(1)}, u32[]{:S(2)}, u32[]{:S(2)}) collective-permute-start(bf16[256,512]{1,0:T(8,128)(2,1)S(1)} %copy-done.7), channel_id=1, source_target_pairs={{0,8},{8,16},{16,24},{24,32},{32,40},{40,48},{48,56},{56,64},{64,7... | collective-permute-start | bytes 786440 | tf_op jit(solution)/shard_map/ppermute | solution.py:335
  96.9 3.6 %collective-permute-start.17 = (bf16[192,256]{1,0:T(8,128)(2,1)S(1)}, bf16[192,256]{1,0:T(8,128)(2,1)S(1)}, u32[]{:S(2)}, u32[]{:S(2)}) collective-permute-start(bf16[192,256]{1,0:T(8,128)(2,1)S(1)} %add_convert_fusion.9), channel_id=1, source_target_pairs={{0,48},{8,24},{16,32},{24,8},{32,16},{40,56},{48,0},{56,40},{1,49}... | collective-permute-start | bytes 294920 | tf_op jit(solution)/shard_map/ppermute | solution.py:39
  99.0 5.7 %collective-permute-start.20 = (bf16[192,256]{1,0:T(8,128)(2,1)S(1)}, bf16[192,256]{1,0:T(8,128)(2,1)S(1)}, u32[]{:S(2)}, u32[]{:S(2)}) collective-permute-start(bf16[192,256]{1,0:T(8,128)(2,1)S(1)} %add_convert_fusion.7), channel_id=1, source_target_pairs={{0,48},{8,24},{16,32},{24,8},{32,16},{40,56},{48,0},{56,40},{1,49}... | collective-permute-start | bytes 294920 | tf_op jit(solution)/shard_map/ppermute | solution.py:39
  100.5 9.4 %collective-permute-start.22 = (bf16[192,256]{1,0:T(8,128)(2,1)S(1)}, bf16[192,256]{1,0:T(8,128)(2,1)S(1)}, u32[]{:S(2)}, u32[]{:S(2)}) collective-permute-start(bf16[192,256]{1,0:T(8,128)(2,1)S(1)} %add_convert_fusion.8), channel_id=1, source_target_pairs={{0,64},{8,200},{64,0},{72,136},{128,192},{136,72},{192,128},{200,8... | collective-permute-start | bytes 294920 | tf_op jit(solution)/shard_map/ppermute | solution.py:39
  104.8 5.7 %collective-permute-start.23 = (bf16[192,256]{1,0:T(8,128)(2,1)S(1)}, bf16[192,256]{1,0:T(8,128)(2,1)S(1)}, u32[]{:S(2)}, u32[]{:S(2)}) collective-permute-start(bf16[192,256]{1,0:T(8,128)(2,1)S(1)} %add_convert_fusion.6), channel_id=1, source_target_pairs={{0,64},{8,200},{64,0},{72,136},{128,192},{136,72},{192,128},{200,8... | collective-permute-start | bytes 294920 | tf_op jit(solution)/shard_map/ppermute | solution.py:39
  110.5 10.6 %collective-permute-start.25 = (bf16[192,256]{1,0:T(8,128)(2,1)S(1)}, bf16[192,256]{1,0:T(8,128)(2,1)S(1)}, u32[]{:S(2)}, u32[]{:S(2)}) collective-permute-start(bf16[192,256]{1,0:T(8,128)(2,1)S(1)} %add_convert_fusion.4.refs_1_), channel_id=1, source_target_pairs={{0,192},{8,72},{64,128},{72,8},{128,64},{136,200},{192,0},{200,136... | collective-permute-start | bytes 294920 | tf_op jit(solution)/shard_map/ppermute | solution.py:39
  116.8 5.1 %collective-permute-start.24 = (bf16[192,256]{1,0:T(8,128)(2,1)S(1)}, bf16[192,256]{1,0:T(8,128)(2,1)S(1)}, u32[]{:S(2)}, u32[]{:S(2)}) collective-permute-start(bf16[192,256]{1,0:T(8,128)(2,1)S(1)} %add_convert_fusion.5.refs_0_), channel_id=1, source_target_pairs={{0,192},{8,72},{64,128},{72,8},{128,64},{136,200},{192,0},{200,136... | collective-permute-start | bytes 294920 | tf_op jit(solution)/shard_map/ppermute | solution.py:39
  122.9 4.6 %collective-permute-start.26 = (bf16[192,512]{1,0:T(8,128)(2,1)S(1)}, bf16[192,512]{1,0:T(8,128)(2,1)S(1)}, u32[]{:S(2)}, u32[]{:S(2)}) collective-permute-start(bf16[192,512]{1,0:T(8,128)(2,1)S(1)} %get-tuple-element.61), channel_id=1, source_target_pairs={{0,48},{8,24},{16,32},{24,8},{32,16},{40,56},{48,0},{56,40},{1,49}... | collective-permute-start | bytes 589832 | tf_op jit(solution)/shard_map/ppermute | solution.py:39
  128.2 19.5 %collective-permute-start.27 = (bf16[384,512]{1,0:T(8,128)(2,1)}, bf16[384,512]{1,0:T(8,128)(2,1)}, u32[]{:S(2)}, u32[]{:S(2)}) collective-permute-start(bf16[384,512]{1,0:T(8,128)(2,1)} %constant_dynamic-update-slice_fusion.2.rest_0_), channel_id=1, source_target_pairs={{0,16},{8,56},{16,0},{24,40},{32,48},{40,24},{48,32},{56,8},{1,17}... | collective-permute-start | bytes 1179656 | tf_op jit(solution)/shard_map/ppermute | solution.py:39
  128.4 28.5 %all-to-all-start.1 = ((f32[64,8,128]{2,1,0:T(8,128)}), f32[64,8,128]{2,1,0:T(8,128)S(1)}, u32[]{:S(2)}, u32[]{:S(2)}) async-start(f32[64,8,128]{2,1,0:T(8,128)} %get-tuple-element.59), calls=%async_computation.1 | async-start | bytes 524288 | tf_op jit(solution)/shard_map/all_to_all | solution.py:63
  147.1 9.7 %collective-permute-start.28 = (bf16[384,512]{1,0:T(8,128)(2,1)}, bf16[384,512]{1,0:T(8,128)(2,1)}, u32[]{:S(2)}, u32[]{:S(2)}) collective-permute-start(bf16[384,512]{1,0:T(8,128)(2,1)} %constant_dynamic-update-slice_fusion.2.rest_0_), channel_id=1, source_target_pairs={{0,8},{8,0},{1,9},{9,1},{2,10},{10,2},{3,11},{11,3},{4,12},{12,4},... | collective-permute-start | bytes 1179656 | tf_op jit(solution)/shard_map/ppermute | solution.py:39
  147.7 9.2 %collective-permute-start.29 = (bf16[384,512]{1,0:T(8,128)(2,1)}, bf16[384,512]{1,0:T(8,128)(2,1)}, u32[]{:S(2)}, u32[]{:S(2)}) collective-permute-start(bf16[384,512]{1,0:T(8,128)(2,1)} %collective-permute-done.27.rest_1_), channel_id=1, source_target_pairs={{0,8},{8,0},{1,9},{9,1},{2,10},{10,2},{3,11},{11,3},{4,12},{12,4},... | collective-permute-start | bytes 1179656 | tf_op jit(solution)/shard_map/ppermute | solution.py:39
  (9 other events, 161.4 us)

commit v3 on v1

--- a/solution.py
+++ b/solution.py
@@ -18,7 +18,7 @@
 TILE = 256
 CHUNKS = 2
 SHARES = 64
-EARLY = 128
+EARLY = 256
 
 fast_rate = 0.01
 epsilon = 1e-06
@@ -57,15 +57,6 @@
 
 def swap_core(value):
     return exchange(value, ("core",), lambda i: i ^ 1)
-
-
-def chained(parts, send):
-    arrived = []
-    for value in parts:
-        if arrived:
-            value, arrived[-1] = lax.optimization_barrier((value, arrived[-1]))
-        arrived.append(send(value))
-    return arrived
 
 
 def spread(squares):
@@ -119,15 +110,16 @@
     return mine, other
 
 
-def gathered(own):
+def gathered(own, squares):
     near = swap_x(own, 1)
     pair = jnp.concatenate([own, near], axis=0)
     far = swap_x(pair, 0)
-    return [pair, far, swap_core(pair), swap_core(far)]
+    far, squares = lax.optimization_barrier((far, squares))
+    return squares, [pair, far, swap_core(pair), swap_core(far)]
 
 
 def finish_kernel(*refs):
-    total_ref, square_ref = refs[2 * CHUNKS :]
+    total_ref, square_hbm, square_ref, sem = refs[2 * CHUNKS :]
     wide = HID // CHUNKS
     for c in range(CHUNKS):
         total = refs[c][...].astype(f32) + refs[CHUNKS + c][...].astype(f32)
@@ -136,6 +128,9 @@
         square = square if c == 0 else before + square
         before = square
     square_ref[...] = jnp.broadcast_to(jnp.sum(square, axis=1, keepdims=True), (8, 128))[None] + jnp.zeros(square_ref.shape, f32)
+    leave = pltpu.make_async_copy(square_ref, square_hbm, sem)
+    leave.start()
+    leave.wait()
 
 
 def fetch(sources, targets, sem):
@@ -230,13 +225,13 @@
         copy.wait()
 
 
-def attend_kernel(meta_ref, q_ref, halo_k_ref, k_ref, halo_v0, halo_v1, v_ref, out_ref, halo_v_ref):
+def attend_kernel(meta_ref, q_ref, halo_ref, k_ref, late_v_ref, v_ref, out_ref, halo_v_ref):
     local = q_ref.shape[0]
     anchor, width = meta_ref[0], meta_ref[1]
     scale = HD ** (-0.5)
-    halo_v_ref[0:EARLY] = halo_v0[...]
-    halo_v_ref[EARLY:] = halo_v1[...]
-    held = [(halo_k_ref, halo_v_ref, -WIN, WIN), (k_ref, v_ref, 0, local)]
+    halo_v_ref[0:EARLY] = halo_ref[WIN:]
+    halo_v_ref[EARLY:] = late_v_ref[...]
+    held = [(halo_ref, halo_v_ref, -WIN, WIN), (k_ref, v_ref, 0, local)]
     for start in range(0, local, TILE):
         spans = []
         for keys, values, base, count in held:
@@ -317,7 +312,8 @@
     count = lax.axis_size(SEQ)
     onward = [(i, i + 1) for i in range(count - 1)]
     tail = local - WIN
-    halo_v = chained([values[tail : tail + EARLY], values[tail + EARLY :]], lambda v: lax.ppermute(v, SEQ, onward))
+    halo_v = lax.ppermute(values[tail + EARLY :], SEQ, onward)
+    with_gather = jnp.concatenate([keys[tail:], values[tail : tail + EARLY]], axis=0)
     positions = anchor + jnp.arange(local, dtype=jnp.int32)[:, None]
     first_block = (positions < split[0]).astype(f32)
     rate_zero = token_rate * first_block
@@ -347,18 +343,20 @@
         total, square = call(
             finish_kernel,
             [VMEM_SPEC] * (2 * CHUNKS),
-            [array((ROWS // 8, HID), bf16), array((SHARES, 8, 128), f32)],
+            [array((ROWS // 8, HID), bf16), pltpu.HBM((SHARES, 8, 128), f32)],
             (*mine, *other),
             8,
+            [pltpu.VMEM((SHARES, 8, 128), f32), pltpu.SemaphoreType.DMA],
+            [VMEM_SPEC, HBM_SPEC],
         )
         if later is not None:
             total, later = lax.optimization_barrier((total, later))
-        return spread(square), gathered(total), later
+        return *gathered(total, spread(square)), later
 
     kept = {}
 
-    square, pieces, send = finished(*reduced(halved[:CHUNKS], halved[CHUNKS:]), keys[tail:])
-    halo_k = lax.ppermute(send, SEQ, onward)
+    square, pieces, send = finished(*reduced(halved[:CHUNKS], halved[CHUNKS:]), with_gather)
+    halo = lax.ppermute(send, SEQ, onward)
     weights_one, wb_one, *halved = call(
         second_kernel,
         [SMEM_SPEC] * 2 + [VMEM_SPEC, HBM_SPEC, HBM_SPEC, VMEM_SPEC, HBM_SPEC] + [VMEM_SPEC] * 4,
@@ -368,15 +366,15 @@
         [grad] + renewal + fetched + [pltpu.VMEM((ROWS, HID), f32), pltpu.SemaphoreType.DMA((10,))],
         [HBM_SPEC] + [VMEM_SPEC] * (1 + 2 * CHUNKS),
     )
-    kept["halo"], halved = lax.optimization_barrier((halo_k, halved))
+    kept["halo"], halved = lax.optimization_barrier((halo, halved))
 
     def attend(before, after):
         query, _ = lax.optimization_barrier((queries, before))
         attn = call(
             attend_kernel,
-            [SMEM_SPEC] + [VMEM_SPEC] * 6,
+            [SMEM_SPEC] + [VMEM_SPEC] * 5,
             array((local, HD), f32),
-            (meta, query, kept["halo"], keys, *halo_v, values),
+            (meta, query, kept["halo"], keys, halo_v, values),
             20,
             [pltpu.VMEM((WIN, HD), bf16)],
         )

time: 160 us -> 150 us (0.938)
  waiting for transfers between devices: 46.7 us -> 27.3 us
  Pallas kernels: 24.1 us -> 26.8 us
  starting transfers between devices: 76.9 us -> 79.5 us
  other arithmetic: 6.22 us -> 8.74 us
  local copies, waits for them, and re-layouts: 3.16 us -> 4.99 us
    all_to_all x2, waiting for transfers between devices: 17.9 us -> 7.69 us  [spread(): return lax.all_to_all(squares, ('x', 'core', 'head'), 0, 0, tiled=True)]
    ppermute x3 -> x2, starting transfers between devices: 13.6 us -> 3.82 us  [the longest x1 1.91 us: per_device(): halo_v = lax.ppermute(values[tail + EARLY:], SEQ, onward)]
    ppermute x28, waiting for transfers between devices: 28.8 us -> 19.6 us  [exchange(): lax.ppermute(value, mesh_axes, [(i, partner(i)) for i in range(count)])]
    ppermute x28, starting transfers between devices: 41 us -> 49.1 us  [exchange(): lax.ppermute(value, mesh_axes, [(i, partner(i)) for i in range(count)])]
    all_to_all x2, starting transfers between devices: 22.3 us -> 26.6 us  [spread(): return lax.all_to_all(squares, ('x', 'core', 'head'), 0, 0, tiled=True)]
    pallas_call x7, Pallas kernels: 24.1 us -> 26.8 us  [call(): pl.pallas_call(kernel, out_shape=outs, in_specs=specs, out_specs=jax.tree...]
  transfers between devices with their start and end apart: 33 -> 32, of which waited for: 16 -> 16; matrix products, arithmetic and copies ran while one was open for 4% -> 8% of each run, Pallas kernels for 9% -> 10%
where the time goes in v3:
time: 150 us
  starting transfers between devices  79.5 us (53%)
  waiting for transfers between devices  27.3 us (18%)
  Pallas kernels  26.8 us (18%)
  other arithmetic  8.74 us (6%)
  local copies, waits for them, and re-layouts  4.99 us (3%)
  between operations  2.4 us (2%)
    ppermute x28, starting transfers between devices, exchange(): lax.ppermute(value, mesh_axes, [(i, partner(i)) for i in range(count)])  49.1 us
    pallas_call x7, Pallas kernels, call(): pl.pallas_call(kernel, out_shape=outs, in_specs=specs, out_specs=jax.tree...  26.8 us
    all_to_all x2, starting transfers between devices, spread(): return lax.all_to_all(squares, ('x', 'core', 'head'), 0, 0, tiled=True)  26.6 us
    ppermute x28, waiting for transfers between devices, exchange(): lax.ppermute(value, mesh_axes, [(i, partner(i)) for i in range(count)])  19.6 us
    all_to_all x2, waiting for transfers between devices, spread(): return lax.all_to_all(squares, ('x', 'core', 'head'), 0, 0, tiled=True)  7.69 us
    convert_element_type x4, other arithmetic, reduced(): two(c, (1 - first) * half, half).astype(bf16)  3.4 us
  transfers between devices with their start and end apart: 32, of which 16 were waited for; matrix products, arithmetic and copies ran while one was open for 8% of the time, Pallas kernels for 10%

profile of v3, /device:TPU:1, one launch (start us, length us, event | category | flops | bytes accessed | tf_op | source)
XLA Modules:
  0.0 149.8 jit_solution(5428660419848114069)
XLA Ops:
  2.3 6.5 %shard_map.95 = (bf16[1536,512]{1,0:T(8,128)(2,1)}, bf16[768,256]{1,0:T(8,128)(2,1)}, bf16[768,256]{1,0:T(8,128)(2,1)S(1)}, f32[768,256]{1,0:T(8,128)S(1)}, f32[768,256]{1,0:T(8,128)S(1)}) custom-call(s32[1]{0:T(128)} %bitcast.1.place_ref, bf16[768,512]{1,0:T(8,128)(2,1)} %k_ref.1, bf16[768,512]{1,0:T(8,128)(2,1)} %targets_hbm.3, ...), custom_call_target="tpu_custom_call" | custom-call | tf_op jit(solution)/shard_map/pallas_call | solution.py:291
  8.8 3.3 %collective-permute-start = (bf16[768,256]{1,0:T(8,128)(2,1)}, bf16[768,256]{1,0:T(8,128)(2,1)}, u32[]{:S(2)}, u32[]{:S(2)}) collective-permute-start(bf16[768,256]{1,0:T(8,128)(2,1)} %get-tuple-element.37), channel_id=1, source_target_pairs={{0,8},{8,0},{1,9},{9,1},{2,10},{10,2},{3,11},{11,3},{4,12},{12,4},... | collective-permute-start | bytes 1179656 | tf_op jit(solution)/shard_map/ppermute | solution.py:39
  12.2 1.6 %collective-permute-done = bf16[768,256]{1,0:T(8,128)(2,1)} collective-permute-done((bf16[768,256]{1,0:T(8,128)(2,1)}, bf16[768,256]{1,0:T(8,128)(2,1)}, u32[]{:S(2)}, u32[]{:S(2)}) %collective-permute-start) | collective-permute-done | bytes 393248 | tf_op jit(solution)/shard_map/ppermute | solution.py:39
  13.8 1.6 %add_convert_fusion.3 = bf16[384,256]{1,0:T(8,128)(2,1)} fusion(f32[768,256]{1,0:T(8,128)S(1)} %get-tuple-element.36, s32[]{:T(128)S(6)} %select_n.24, bf16[768,256]{1,0:T(8,128)(2,1)} %collective-permute-done), kind=kLoop, calls=%fused_computation.5 | loop fusion | flops 294912 | bytes 786436 | tf_op jit(solution)/shard_map/convert_element_type | solution.py:96
  16.2 1.6 %add_convert_fusion.2 = bf16[384,256]{1,0:T(8,128)(2,1)} fusion(f32[768,256]{1,0:T(8,128)S(1)} %get-tuple-element.38, s32[]{:T(128)S(6)} %select_n.24, bf16[768,256]{1,0:T(8,128)(2,1)} %collective-permute-done.4), kind=kLoop, calls=%fused_computation.4 | loop fusion | flops 294912 | bytes 786436 | tf_op jit(solution)/shard_map/convert_element_type | solution.py:96
  17.9 1.9 %collective-permute-start.5 = (bf16[384,256]{1,0:T(8,128)(2,1)}, bf16[384,256]{1,0:T(8,128)(2,1)}, u32[]{:S(2)}, u32[]{:S(2)}) collective-permute-start(bf16[384,256]{1,0:T(8,128)(2,1)} %add_convert_fusion.2), channel_id=1, source_target_pairs={{0,16},{8,56},{16,0},{24,40},{32,48},{40,24},{48,32},{56,8},{1,17}... | collective-permute-start | bytes 589832 | tf_op jit(solution)/shard_map/ppermute | solution.py:39
  27.0 5.1 %collective-permute-start.3 = (bf16[192,256]{1,0:T(8,128)(2,1)S(1)}, bf16[192,256]{1,0:T(8,128)(2,1)S(1)}, u32[]{:S(2)}, u32[]{:S(2)}) collective-permute-start(bf16[192,256]{1,0:T(8,128)(2,1)S(1)} %add_convert_fusion.14), channel_id=1, source_target_pairs={{0,64},{8,200},{64,0},{72,136},{128,192},{136,72},{192,128},{200,8... | collective-permute-start | bytes 294920 | tf_op jit(solution)/shard_map/ppermute | solution.py:39
  33.1 2.4 %collective-permute-start.7 = (bf16[192,256]{1,0:T(8,128)(2,1)S(1)}, bf16[192,256]{1,0:T(8,128)(2,1)S(1)}, u32[]{:S(2)}, u32[]{:S(2)}) collective-permute-start(bf16[192,256]{1,0:T(8,128)(2,1)S(1)} %add_convert_fusion.11), channel_id=1, source_target_pairs={{0,64},{8,200},{64,0},{72,136},{128,192},{136,72},{192,128},{200,8... | collective-permute-start | bytes 294920 | tf_op jit(solution)/shard_map/ppermute | solution.py:39
  36.8 2.4 %collective-permute-done.7 = bf16[192,256]{1,0:T(8,128)(2,1)S(1)} collective-permute-done((bf16[192,256]{1,0:T(8,128)(2,1)S(1)}, bf16[192,256]{1,0:T(8,128)(2,1)S(1)}, u32[]{:S(2)}, u32[]{:S(2)}) %collective-permute-start.7) | collective-permute-done | bytes 98336 | tf_op jit(solution)/shard_map/ppermute | solution.py:39
  39.3 1.9 %collective-permute-start.9 = (bf16[192,256]{1,0:T(8,128)(2,1)S(1)}, bf16[192,256]{1,0:T(8,128)(2,1)S(1)}, u32[]{:S(2)}, u32[]{:S(2)}) collective-permute-start(bf16[192,256]{1,0:T(8,128)(2,1)S(1)} %add_convert_fusion.10.refs_1_), channel_id=1, source_target_pairs={{0,192},{8,72},{64,128},{72,8},{128,64},{136,200},{192,0},{200,136... | collective-permute-start | bytes 294920 | tf_op jit(solution)/shard_map/ppermute | solution.py:39
  42.1 1.7 %collective-permute-done.9.refs_3_ = bf16[192,256]{1,0:T(8,128)(2,1)S(1)} collective-permute-done((bf16[192,256]{1,0:T(8,128)(2,1)S(1)}, bf16[192,256]{1,0:T(8,128)(2,1)S(1)}, u32[]{:S(2)}, u32[]{:S(2)}) %collective-permute-start.9) | collective-permute-done | bytes 98336 | tf_op jit(solution)/shard_map/ppermute | solution.py:39
  46.3 13.0 %all-to-all-start = ((f32[64,8,128]{2,1,0:T(8,128)}), f32[64,8,128]{2,1,0:T(8,128)S(1)}, u32[]{:S(2)}, u32[]{:S(2)}) async-start(f32[64,8,128]{2,1,0:T(8,128)} %get-tuple-element.43), calls=%async_computation | async-start | bytes 524288 | tf_op jit(solution)/shard_map/all_to_all | solution.py:63
  59.3 2.9 %collective-permute-start.12 = (bf16[384,512]{1,0:T(8,128)(2,1)S(1)}, bf16[384,512]{1,0:T(8,128)(2,1)S(1)}, u32[]{:S(2)}, u32[]{:S(2)}) collective-permute-start(bf16[384,512]{1,0:T(8,128)(2,1)S(1)} %constant_dynamic-update-slice_fusion.rest_0_), channel_id=1, source_target_pairs={{0,16},{8,56},{16,0},{24,40},{32,48},{40,24},{48,32},{56,8},{1,17}... | collective-permute-start | bytes 1179656 | tf_op jit(solution)/shard_map/ppermute | solution.py:39
  62.2 1.9 %collective-permute-start.10 = (bf16[768,512]{1,0:T(8,128)(2,1)}, bf16[768,512]{1,0:T(8,128)(2,1)S(1)}, u32[]{:S(2)}, u32[]{:S(2)}) collective-permute-start(bf16[768,512]{1,0:T(8,128)(2,1)} %pad_maximum_fusion), channel_id=1, source_target_pairs={{0,8},{8,16},{16,24},{24,32},{32,40},{40,48},{48,56},{56,64},{64,7... | collective-permute-start | bytes 2359304 | tf_op jit(solution)/shard_map/ppermute | solution.py:359
  64.9 4.0 %all-to-all-done.square_ref = f32[64,8,128]{2,1,0:T(8,128)S(1)} async-done(((f32[64,8,128]{2,1,0:T(8,128)}), f32[64,8,128]{2,1,0:T(8,128)S(1)}, u32[]{:S(2)}, u32[]{:S(2)}) %all-to-all-start) | async-done | bytes 262176 | tf_op jit(solution)/shard_map/all_to_all | solution.py:63
  70.0 1.8 %collective-permute-done.14.rest_3_ = bf16[384,512]{1,0:T(8,128)(2,1)} collective-permute-done((bf16[384,512]{1,0:T(8,128)(2,1)S(1)}, bf16[384,512]{1,0:T(8,128)(2,1)}, u32[]{:S(2)}, u32[]{:S(2)}) %collective-permute-start.14) | collective-permute-done | bytes 393248 | tf_op jit(solution)/shard_map/ppermute | solution.py:39
  71.7 7.9 %shard_map.97 = (f32[1536,512]{1,0:T(8,128)}, bf16[1536,512]{1,0:T(8,128)(2,1)S(1)}, bf16[768,256]{1,0:T(8,128)(2,1)S(1)}, bf16[768,256]{1,0:T(8,128)(2,1)S(1)},...) custom-call(s32[1]{0:T(128)} %bitcast.1.place_ref, s32[8]{0:T(128)S(1)} %broadcast_multiply_fusion.starts_ref, ...), custom_call_target="tpu_custom_call" | custom-call | tf_op jit(solution)/shard_map/pallas_call | solution.py:291
  81.5 3.6 %collective-permute-start.16 = (bf16[384,256]{1,0:T(8,128)(2,1)S(1)}, bf16[384,256]{1,0:T(8,128)(2,1)S(1)}, u32[]{:S(2)}, u32[]{:S(2)}) collective-permute-start(bf16[384,256]{1,0:T(8,128)(2,1)S(1)} %add_convert_fusion.1), channel_id=1, source_target_pairs={{0,16},{8,56},{16,0},{24,40},{32,48},{40,24},{48,32},{56,8},{1,17}... | collective-permute-start | bytes 589832 | tf_op jit(solution)/shard_map/ppermute | solution.py:39
  85.6 1.9 %collective-permute-start.21 = (bf16[256,512]{1,0:T(8,128)(2,1)S(1)}, bf16[256,512]{1,0:T(8,128)(2,1)S(1)}, u32[]{:S(2)}, u32[]{:S(2)}) collective-permute-start(bf16[256,512]{1,0:T(8,128)(2,1)S(1)} %copy-done.5), channel_id=1, source_target_pairs={{0,8},{8,16},{16,24},{24,32},{32,40},{40,48},{48,56},{56,64},{64,7... | collective-permute-start | bytes 786440 | tf_op jit(solution)/shard_map/ppermute | solution.py:315
  92.5 10.8 %collective-permute-start.22 = (bf16[192,256]{1,0:T(8,128)(2,1)S(1)}, bf16[192,256]{1,0:T(8,128)(2,1)S(1)}, u32[]{:S(2)}, u32[]{:S(2)}) collective-permute-start(bf16[192,256]{1,0:T(8,128)(2,1)S(1)} %add_convert_fusion.8), channel_id=1, source_target_pairs={{0,64},{8,200},{64,0},{72,136},{128,192},{136,72},{192,128},{200,8... | collective-permute-start | bytes 294920 | tf_op jit(solution)/shard_map/ppermute | solution.py:39
  103.3 2.3 %collective-permute-start.23 = (bf16[192,256]{1,0:T(8,128)(2,1)S(1)}, bf16[192,256]{1,0:T(8,128)(2,1)S(1)}, u32[]{:S(2)}, u32[]{:S(2)}) collective-permute-start(bf16[192,256]{1,0:T(8,128)(2,1)S(1)} %add_convert_fusion.6), channel_id=1, source_target_pairs={{0,64},{8,200},{64,0},{72,136},{128,192},{136,72},{192,128},{200,8... | collective-permute-start | bytes 294920 | tf_op jit(solution)/shard_map/ppermute | solution.py:39
  105.7 2.8 %shard_map.98.attn_ref = f32[768,512]{1,0:T(8,128)S(1)} custom-call(s32[3]{0:T(128)S(1)} %pad_add_fusion.meta_ref, bf16[768,512]{1,0:T(8,128)(2,1)S(1)} %copy-done.1, bf16[768,512]{1,0:T(8,128)(2,1)S(1)} %collective-permute-done.10.halo_ref, bf16[768,512]{1,0:T(8,128)(2,1)S(1)} %copy-done, bf16[256,512]{1,0:T(8,128)(2,1)S(1)} %collective-permute-done.21.late_v_ref, ...), custom_call_target="tpu_custom_call" | custom-call | tf_op jit(solution)/shard_map/pallas_call | solution.py:291
  111.5 4.0 %shard_map.99 = bf16[768,512]{1,0:T(8,128)(2,1)} custom-call(s32[3]{0:T(128)S(1)} %pad_add_fusion.meta_ref, bf16[768,512]{1,0:T(8,128)(2,1)S(1)} %copy-done.1, f32[768,512]{1,0:T(8,128)S(1)} %shard_map.98.attn_ref, bf16[1536,512]{1,0:T(8,128)(2,1)S(1)} %copy-done.4, bf16[1536,512]{1,0:T(8,128)(2,1)S(1)} %get-tuple-element.61.late_ref), custom_call_target="tpu_custom_call" | custom-call | tf_op jit(solution)/shard_map/pallas_call | solution.py:291
  117.0 2.1 %collective-permute-start.26 = (bf16[192,512]{1,0:T(8,128)(2,1)}, bf16[192,512]{1,0:T(8,128)(2,1)}, u32[]{:S(2)}, u32[]{:S(2)}) collective-permute-start(bf16[192,512]{1,0:T(8,128)(2,1)} %get-tuple-element.65), channel_id=1, source_target_pairs={{0,48},{8,24},{16,32},{24,8},{32,16},{40,56},{48,0},{56,40},{1,49}... | collective-permute-start | bytes 589832 | tf_op jit(solution)/shard_map/ppermute | solution.py:39
  119.2 13.7 %all-to-all-start.1 = ((f32[64,8,128]{2,1,0:T(8,128)}), f32[64,8,128]{2,1,0:T(8,128)S(1)}, u32[]{:S(2)}, u32[]{:S(2)}) async-start(f32[64,8,128]{2,1,0:T(8,128)} %get-tuple-element.66), calls=%async_computation.1 | async-start | bytes 524288 | tf_op jit(solution)/shard_map/all_to_all | solution.py:63
  132.9 1.6 %constant_dynamic-update-slice_fusion.3 = bf16[384,512]{1,0:T(8,128)(2,1)} fusion(bf16[192,512]{1,0:T(8,128)(2,1)} %get-tuple-element.65), kind=kLoop, calls=%fused_computation.23 | loop fusion | bytes 393216
  134.5 1.6 %constant_dynamic-update-slice_fusion.2.rest_0_ = bf16[384,512]{1,0:T(8,128)(2,1)} fusion(bf16[384,512]{1,0:T(8,128)(2,1)} %constant_dynamic-update-slice_fusion.3, bf16[192,512]{1,0:T(8,128)(2,1)} %collective-permute-done.26), kind=kLoop, calls=%fused_computation.22 | loop fusion | bytes 393216 | tf_op jit(solution)/shard_map/concatenate | solution.py:115
  136.1 2.8 %collective-permute-start.27 = (bf16[384,512]{1,0:T(8,128)(2,1)}, bf16[384,512]{1,0:T(8,128)(2,1)}, u32[]{:S(2)}, u32[]{:S(2)}) collective-permute-start(bf16[384,512]{1,0:T(8,128)(2,1)} %constant_dynamic-update-slice_fusion.2.rest_0_), channel_id=1, source_target_pairs={{0,16},{8,56},{16,0},{24,40},{32,48},{40,24},{48,32},{56,8},{1,17}... | collective-permute-start | bytes 1179656 | tf_op jit(solution)/shard_map/ppermute | solution.py:39
  138.9 3.7 %all-to-all-done.1.square_ref = f32[64,8,128]{2,1,0:T(8,128)S(1)} async-done(((f32[64,8,128]{2,1,0:T(8,128)}), f32[64,8,128]{2,1,0:T(8,128)S(1)}, u32[]{:S(2)}, u32[]{:S(2)}) %all-to-all-start.1) | async-done | bytes 262176 | tf_op jit(solution)/shard_map/all_to_all | solution.py:63
  142.6 1.9 %collective-permute-done.27.rest_1_ = bf16[384,512]{1,0:T(8,128)(2,1)} collective-permute-done((bf16[384,512]{1,0:T(8,128)(2,1)}, bf16[384,512]{1,0:T(8,128)(2,1)}, u32[]{:S(2)}, u32[]{:S(2)}) %collective-permute-start.27) | collective-permute-done | bytes 393248 | tf_op jit(solution)/shard_map/ppermute | solution.py:39
  144.6 1.8 %collective-permute-done.29.rest_3_ = bf16[384,512]{1,0:T(8,128)(2,1)S(1)} collective-permute-done((bf16[384,512]{1,0:T(8,128)(2,1)}, bf16[384,512]{1,0:T(8,128)(2,1)S(1)}, u32[]{:S(2)}, u32[]{:S(2)}) %collective-permute-start.29) | collective-permute-done | bytes 393248 | tf_op jit(solution)/shard_map/ppermute | solution.py:39
  146.5 3.1 %shard_map.101 = f32[1536,512]{1,0:T(8,128)} custom-call(s32[8]{0:T(128)S(1)} %broadcast_multiply_fusion.starts_ref, f32[64,8,128]{2,1,0:T(8,128)S(1)} %all-to-all-done.1.square_ref, f32[1536,512]{1,0:T(8,128)S(1)} %copy-done.2, bf16[384,512]{1,0:T(8,128)(2,1)} %constant_dynamic-update-slice_fusion.2.rest_0_, ...), custom_call_target="tpu_custom_call" | custom-call | tf_op jit(solution)/shard_map/pallas_call | solution.py:291
  (80 shorter events, 28.0 us)
Async XLA Ops:
  8.8 5.0 %collective-permute-start = (bf16[768,256]{1,0:T(8,128)(2,1)}, bf16[768,256]{1,0:T(8,128)(2,1)}, u32[]{:S(2)}, u32[]{:S(2)}) collective-permute-start(bf16[768,256]{1,0:T(8,128)(2,1)} %get-tuple-element.37), channel_id=1, source_target_pairs={{0,8},{8,0},{1,9},{9,1},{2,10},{10,2},{3,11},{11,3},{4,12},{12,4},... | collective-permute-start | bytes 1179656 | tf_op jit(solution)/shard_map/ppermute | solution.py:39
  12.1 4.1 %collective-permute-start.4 = (bf16[768,256]{1,0:T(8,128)(2,1)S(1)}, bf16[768,256]{1,0:T(8,128)(2,1)}, u32[]{:S(2)}, u32[]{:S(2)}) collective-permute-start(bf16[768,256]{1,0:T(8,128)(2,1)S(1)} %get-tuple-element.39), channel_id=1, source_target_pairs={{0,8},{8,0},{1,9},{9,1},{2,10},{10,2},{3,11},{11,3},{4,12},{12,4},... | collective-permute-start | bytes 1179656 | tf_op jit(solution)/shard_map/ppermute | solution.py:39
  15.5 6.0 %collective-permute-start.1 = (bf16[384,256]{1,0:T(8,128)(2,1)}, bf16[384,256]{1,0:T(8,128)(2,1)}, u32[]{:S(2)}, u32[]{:S(2)}) collective-permute-start(bf16[384,256]{1,0:T(8,128)(2,1)} %add_convert_fusion.3), channel_id=1, source_target_pairs={{0,16},{8,56},{16,0},{24,40},{32,48},{40,24},{48,32},{56,8},{1,17}... | collective-permute-start | bytes 589832 | tf_op jit(solution)/shard_map/ppermute | solution.py:39
  17.9 6.0 %collective-permute-start.5 = (bf16[384,256]{1,0:T(8,128)(2,1)}, bf16[384,256]{1,0:T(8,128)(2,1)}, u32[]{:S(2)}, u32[]{:S(2)}) collective-permute-start(bf16[384,256]{1,0:T(8,128)(2,1)} %add_convert_fusion.2), channel_id=1, source_target_pairs={{0,16},{8,56},{16,0},{24,40},{32,48},{40,24},{48,32},{56,8},{1,17}... | collective-permute-start | bytes 589832 | tf_op jit(solution)/shard_map/ppermute | solution.py:39
  22.5 3.6 %collective-permute-start.2 = (bf16[192,256]{1,0:T(8,128)(2,1)S(1)}, bf16[192,256]{1,0:T(8,128)(2,1)S(1)}, u32[]{:S(2)}, u32[]{:S(2)}) collective-permute-start(bf16[192,256]{1,0:T(8,128)(2,1)S(1)} %add_convert_fusion.15), channel_id=1, source_target_pairs={{0,48},{8,24},{16,32},{24,8},{32,16},{40,56},{48,0},{56,40},{1,49}... | collective-permute-start | bytes 294920 | tf_op jit(solution)/shard_map/ppermute | solution.py:39
  24.9 7.2 %collective-permute-start.6 = (bf16[192,256]{1,0:T(8,128)(2,1)S(1)}, bf16[192,256]{1,0:T(8,128)(2,1)S(1)}, u32[]{:S(2)}, u32[]{:S(2)}) collective-permute-start(bf16[192,256]{1,0:T(8,128)(2,1)S(1)} %add_convert_fusion.12), channel_id=1, source_target_pairs={{0,48},{8,24},{16,32},{24,8},{32,16},{40,56},{48,0},{56,40},{1,49}... | collective-permute-start | bytes 294920 | tf_op jit(solution)/shard_map/ppermute | solution.py:39
  27.0 8.5 %collective-permute-start.3 = (bf16[192,256]{1,0:T(8,128)(2,1)S(1)}, bf16[192,256]{1,0:T(8,128)(2,1)S(1)}, u32[]{:S(2)}, u32[]{:S(2)}) collective-permute-start(bf16[192,256]{1,0:T(8,128)(2,1)S(1)} %add_convert_fusion.14), channel_id=1, source_target_pairs={{0,64},{8,200},{64,0},{72,136},{128,192},{136,72},{192,128},{200,8... | collective-permute-start | bytes 294920 | tf_op jit(solution)/shard_map/ppermute | solution.py:39
  33.1 6.2 %collective-permute-start.7 = (bf16[192,256]{1,0:T(8,128)(2,1)S(1)}, bf16[192,256]{1,0:T(8,128)(2,1)S(1)}, u32[]{:S(2)}, u32[]{:S(2)}) collective-permute-start(bf16[192,256]{1,0:T(8,128)(2,1)S(1)} %add_convert_fusion.11), channel_id=1, source_target_pairs={{0,64},{8,200},{64,0},{72,136},{128,192},{136,72},{192,128},{200,8... | collective-permute-start | bytes 294920 | tf_op jit(solution)/shard_map/ppermute | solution.py:39
  35.6 6.5 %collective-permute-start.8 = (bf16[192,256]{1,0:T(8,128)(2,1)S(1)}, bf16[192,256]{1,0:T(8,128)(2,1)S(1)}, u32[]{:S(2)}, u32[]{:S(2)}) collective-permute-start(bf16[192,256]{1,0:T(8,128)(2,1)S(1)} %add_convert_fusion.13.refs_0_), channel_id=1, source_target_pairs={{0,192},{8,72},{64,128},{72,8},{128,64},{136,200},{192,0},{200,136... | collective-permute-start | bytes 294920 | tf_op jit(solution)/shard_map/ppermute | solution.py:39
  39.3 4.5 %collective-permute-start.9 = (bf16[192,256]{1,0:T(8,128)(2,1)S(1)}, bf16[192,256]{1,0:T(8,128)(2,1)S(1)}, u32[]{:S(2)}, u32[]{:S(2)}) collective-permute-start(bf16[192,256]{1,0:T(8,128)(2,1)S(1)} %add_convert_fusion.10.refs_1_), channel_id=1, source_target_pairs={{0,192},{8,72},{64,128},{72,8},{128,64},{136,200},{192,0},{200,136... | collective-permute-start | bytes 294920 | tf_op jit(solution)/shard_map/ppermute | solution.py:39
  44.8 14.5 %collective-permute-start.11 = (bf16[192,512]{1,0:T(8,128)(2,1)S(1)}, bf16[192,512]{1,0:T(8,128)(2,1)S(1)}, u32[]{:S(2)}, u32[]{:S(2)}) collective-permute-start(bf16[192,512]{1,0:T(8,128)(2,1)S(1)} %get-tuple-element.42), channel_id=1, source_target_pairs={{0,48},{8,24},{16,32},{24,8},{32,16},{40,56},{48,0},{56,40},{1,49}... | collective-permute-start | bytes 589832 | tf_op jit(solution)/shard_map/ppermute | solution.py:39
  46.3 22.7 %all-to-all-start = ((f32[64,8,128]{2,1,0:T(8,128)}), f32[64,8,128]{2,1,0:T(8,128)S(1)}, u32[]{:S(2)}, u32[]{:S(2)}) async-start(f32[64,8,128]{2,1,0:T(8,128)} %get-tuple-element.43), calls=%async_computation | async-start | bytes 524288 | tf_op jit(solution)/shard_map/all_to_all | solution.py:63
  59.3 10.6 %collective-permute-start.12 = (bf16[384,512]{1,0:T(8,128)(2,1)S(1)}, bf16[384,512]{1,0:T(8,128)(2,1)S(1)}, u32[]{:S(2)}, u32[]{:S(2)}) collective-permute-start(bf16[384,512]{1,0:T(8,128)(2,1)S(1)} %constant_dynamic-update-slice_fusion.rest_0_), channel_id=1, source_target_pairs={{0,16},{8,56},{16,0},{24,40},{32,48},{40,24},{48,32},{56,8},{1,17}... | collective-permute-start | bytes 1179656 | tf_op jit(solution)/shard_map/ppermute | solution.py:39
  62.2 17.4 %collective-permute-start.10 = (bf16[768,512]{1,0:T(8,128)(2,1)}, bf16[768,512]{1,0:T(8,128)(2,1)S(1)}, u32[]{:S(2)}, u32[]{:S(2)}) collective-permute-start(bf16[768,512]{1,0:T(8,128)(2,1)} %pad_maximum_fusion), channel_id=1, source_target_pairs={{0,8},{8,16},{16,24},{24,32},{32,40},{40,48},{48,56},{56,64},{64,7... | collective-permute-start | bytes 2359304 | tf_op jit(solution)/shard_map/ppermute | solution.py:359
  64.1 5.9 %collective-permute-start.13 = (bf16[384,512]{1,0:T(8,128)(2,1)S(1)}, bf16[384,512]{1,0:T(8,128)(2,1)}, u32[]{:S(2)}, u32[]{:S(2)}) collective-permute-start(bf16[384,512]{1,0:T(8,128)(2,1)S(1)} %constant_dynamic-update-slice_fusion.rest_0_), channel_id=1, source_target_pairs={{0,8},{8,0},{1,9},{9,1},{2,10},{10,2},{3,11},{11,3},{4,12},{12,4},... | collective-permute-start | bytes 1179656 | tf_op jit(solution)/shard_map/ppermute | solution.py:39
  69.9 1.9 %collective-permute-start.14 = (bf16[384,512]{1,0:T(8,128)(2,1)S(1)}, bf16[384,512]{1,0:T(8,128)(2,1)}, u32[]{:S(2)}, u32[]{:S(2)}) collective-permute-start(bf16[384,512]{1,0:T(8,128)(2,1)S(1)} %collective-permute-done.12.rest_1_), channel_id=1, source_target_pairs={{0,8},{8,0},{1,9},{9,1},{2,10},{10,2},{3,11},{11,3},{4,12},{12,4},... | collective-permute-start | bytes 1179656 | tf_op jit(solution)/shard_map/ppermute | solution.py:39
  79.6 1.8 %collective-permute-start.15 = (bf16[768,256]{1,0:T(8,128)(2,1)S(1)}, bf16[768,256]{1,0:T(8,128)(2,1)S(1)}, u32[]{:S(2)}, u32[]{:S(2)}) collective-permute-start(bf16[768,256]{1,0:T(8,128)(2,1)S(1)} %get-tuple-element.51), channel_id=1, source_target_pairs={{0,8},{8,0},{1,9},{9,1},{2,10},{10,2},{3,11},{11,3},{4,12},{12,4},... | collective-permute-start | bytes 1179656 | tf_op jit(solution)/shard_map/ppermute | solution.py:39
  79.8 5.2 %collective-permute-start.18 = (bf16[768,256]{1,0:T(8,128)(2,1)S(1)}, bf16[768,256]{1,0:T(8,128)(2,1)S(1)}, u32[]{:S(2)}, u32[]{:S(2)}) collective-permute-start(bf16[768,256]{1,0:T(8,128)(2,1)S(1)} %get-tuple-element.53), channel_id=1, source_target_pairs={{0,8},{8,0},{1,9},{9,1},{2,10},{10,2},{3,11},{11,3},{4,12},{12,4},... | collective-permute-start | bytes 1179656 | tf_op jit(solution)/shard_map/ppermute | solution.py:39
  81.5 6.7 %collective-permute-start.16 = (bf16[384,256]{1,0:T(8,128)(2,1)S(1)}, bf16[384,256]{1,0:T(8,128)(2,1)S(1)}, u32[]{:S(2)}, u32[]{:S(2)}) collective-permute-start(bf16[384,256]{1,0:T(8,128)(2,1)S(1)} %add_convert_fusion.1), channel_id=1, source_target_pairs={{0,16},{8,56},{16,0},{24,40},{32,48},{40,24},{48,32},{56,8},{1,17}... | collective-permute-start | bytes 589832 | tf_op jit(solution)/shard_map/ppermute | solution.py:39
  85.1 5.8 %collective-permute-start.19 = (bf16[384,256]{1,0:T(8,128)(2,1)S(1)}, bf16[384,256]{1,0:T(8,128)(2,1)S(1)}, u32[]{:S(2)}, u32[]{:S(2)}) collective-permute-start(bf16[384,256]{1,0:T(8,128)(2,1)S(1)} %add_convert_fusion), channel_id=1, source_target_pairs={{0,16},{8,56},{16,0},{24,40},{32,48},{40,24},{48,32},{56,8},{1,17}... | collective-permute-start | bytes 589832 | tf_op jit(solution)/shard_map/ppermute | solution.py:39
  85.6 20.1 %collective-permute-start.21 = (bf16[256,512]{1,0:T(8,128)(2,1)S(1)}, bf16[256,512]{1,0:T(8,128)(2,1)S(1)}, u32[]{:S(2)}, u32[]{:S(2)}) collective-permute-start(bf16[256,512]{1,0:T(8,128)(2,1)S(1)} %copy-done.5), channel_id=1, source_target_pairs={{0,8},{8,16},{16,24},{24,32},{32,40},{40,48},{48,56},{56,64},{64,7... | collective-permute-start | bytes 786440 | tf_op jit(solution)/shard_map/ppermute | solution.py:315
  88.2 4.2 %collective-permute-start.17 = (bf16[192,256]{1,0:T(8,128)(2,1)S(1)}, bf16[192,256]{1,0:T(8,128)(2,1)S(1)}, u32[]{:S(2)}, u32[]{:S(2)}) collective-permute-start(bf16[192,256]{1,0:T(8,128)(2,1)S(1)} %add_convert_fusion.9), channel_id=1, source_target_pairs={{0,48},{8,24},{16,32},{24,8},{32,16},{40,56},{48,0},{56,40},{1,49}... | collective-permute-start | bytes 294920 | tf_op jit(solution)/shard_map/ppermute | solution.py:39
  91.0 12.2 %collective-permute-start.20 = (bf16[192,256]{1,0:T(8,128)(2,1)S(1)}, bf16[192,256]{1,0:T(8,128)(2,1)S(1)}, u32[]{:S(2)}, u32[]{:S(2)}) collective-permute-start(bf16[192,256]{1,0:T(8,128)(2,1)S(1)} %add_convert_fusion.7), channel_id=1, source_target_pairs={{0,48},{8,24},{16,32},{24,8},{32,16},{40,56},{48,0},{56,40},{1,49}... | collective-permute-start | bytes 294920 | tf_op jit(solution)/shard_map/ppermute | solution.py:39
  92.5 16.1 %collective-permute-start.22 = (bf16[192,256]{1,0:T(8,128)(2,1)S(1)}, bf16[192,256]{1,0:T(8,128)(2,1)S(1)}, u32[]{:S(2)}, u32[]{:S(2)}) collective-permute-start(bf16[192,256]{1,0:T(8,128)(2,1)S(1)} %add_convert_fusion.8), channel_id=1, source_target_pairs={{0,64},{8,200},{64,0},{72,136},{128,192},{136,72},{192,128},{200,8... | collective-permute-start | bytes 294920 | tf_op jit(solution)/shard_map/ppermute | solution.py:39
  103.3 5.7 %collective-permute-start.23 = (bf16[192,256]{1,0:T(8,128)(2,1)S(1)}, bf16[192,256]{1,0:T(8,128)(2,1)S(1)}, u32[]{:S(2)}, u32[]{:S(2)}) collective-permute-start(bf16[192,256]{1,0:T(8,128)(2,1)S(1)} %add_convert_fusion.6), channel_id=1, source_target_pairs={{0,64},{8,200},{64,0},{72,136},{128,192},{136,72},{192,128},{200,8... | collective-permute-start | bytes 294920 | tf_op jit(solution)/shard_map/ppermute | solution.py:39
  109.0 6.4 %collective-permute-start.25 = (bf16[192,256]{1,0:T(8,128)(2,1)S(1)}, bf16[192,256]{1,0:T(8,128)(2,1)S(1)}, u32[]{:S(2)}, u32[]{:S(2)}) collective-permute-start(bf16[192,256]{1,0:T(8,128)(2,1)S(1)} %add_convert_fusion.4.refs_1_), channel_id=1, source_target_pairs={{0,192},{8,72},{64,128},{72,8},{128,64},{136,200},{192,0},{200,136... | collective-permute-start | bytes 294920 | tf_op jit(solution)/shard_map/ppermute | solution.py:39
  109.9 5.5 %collective-permute-start.24 = (bf16[192,256]{1,0:T(8,128)(2,1)S(1)}, bf16[192,256]{1,0:T(8,128)(2,1)S(1)}, u32[]{:S(2)}, u32[]{:S(2)}) collective-permute-start(bf16[192,256]{1,0:T(8,128)(2,1)S(1)} %add_convert_fusion.5.refs_0_), channel_id=1, source_target_pairs={{0,192},{8,72},{64,128},{72,8},{128,64},{136,200},{192,0},{200,136... | collective-permute-start | bytes 294920 | tf_op jit(solution)/shard_map/ppermute | solution.py:39
  117.0 17.4 %collective-permute-start.26 = (bf16[192,512]{1,0:T(8,128)(2,1)}, bf16[192,512]{1,0:T(8,128)(2,1)}, u32[]{:S(2)}, u32[]{:S(2)}) collective-permute-start(bf16[192,512]{1,0:T(8,128)(2,1)} %get-tuple-element.65), channel_id=1, source_target_pairs={{0,48},{8,24},{16,32},{24,8},{32,16},{40,56},{48,0},{56,40},{1,49}... | collective-permute-start | bytes 589832 | tf_op jit(solution)/shard_map/ppermute | solution.py:39
  119.2 23.4 %all-to-all-start.1 = ((f32[64,8,128]{2,1,0:T(8,128)}), f32[64,8,128]{2,1,0:T(8,128)S(1)}, u32[]{:S(2)}, u32[]{:S(2)}) async-start(f32[64,8,128]{2,1,0:T(8,128)} %get-tuple-element.66), calls=%async_computation.1 | async-start | bytes 524288 | tf_op jit(solution)/shard_map/all_to_all | solution.py:63
  136.1 8.4 %collective-permute-start.27 = (bf16[384,512]{1,0:T(8,128)(2,1)}, bf16[384,512]{1,0:T(8,128)(2,1)}, u32[]{:S(2)}, u32[]{:S(2)}) collective-permute-start(bf16[384,512]{1,0:T(8,128)(2,1)} %constant_dynamic-update-slice_fusion.2.rest_0_), channel_id=1, source_target_pairs={{0,16},{8,56},{16,0},{24,40},{32,48},{40,24},{48,32},{56,8},{1,17}... | collective-permute-start | bytes 1179656 | tf_op jit(solution)/shard_map/ppermute | solution.py:39
  138.9 5.7 %collective-permute-start.28 = (bf16[384,512]{1,0:T(8,128)(2,1)}, bf16[384,512]{1,0:T(8,128)(2,1)}, u32[]{:S(2)}, u32[]{:S(2)}) collective-permute-start(bf16[384,512]{1,0:T(8,128)(2,1)} %constant_dynamic-update-slice_fusion.2.rest_0_), channel_id=1, source_target_pairs={{0,8},{8,0},{1,9},{9,1},{2,10},{10,2},{3,11},{11,3},{4,12},{12,4},... | collective-permute-start | bytes 1179656 | tf_op jit(solution)/shard_map/ppermute | solution.py:39
  144.5 1.9 %collective-permute-start.29 = (bf16[384,512]{1,0:T(8,128)(2,1)}, bf16[384,512]{1,0:T(8,128)(2,1)S(1)}, u32[]{:S(2)}, u32[]{:S(2)}) collective-permute-start(bf16[384,512]{1,0:T(8,128)(2,1)} %collective-permute-done.27.rest_1_), channel_id=1, source_target_pairs={{0,8},{8,0},{1,9},{9,1},{2,10},{10,2},{3,11},{11,3},{4,12},{12,4},... | collective-permute-start | bytes 1179656 | tf_op jit(solution)/shard_map/ppermute | solution.py:39
  (7 other events, 126.8 us)

commit v4 on v3

--- a/solution.py
+++ b/solution.py
@@ -84,7 +84,7 @@
     return (jnp.stack(places) * (ROWS // 8)).astype(jnp.int32)
 
 
-def reduced(sent, own, beside_first=None, beside_second=None):
+def reduced(sent, own, before_z=None, beside_first=None, beside_second=None):
     _, first, second = halves()
     half, rows = ROWS // 4, ROWS // 8
     chunks = range(len(sent))
@@ -100,6 +100,8 @@
     near = second * rows
     mine = [two(c, first * half + near, rows) + rows_of(got_x[c], near, rows).astype(f32) + got_x2[c].astype(f32) for c in chunks]
     mine = [m.astype(bf16) for m in mine]
+    if before_z is not None:
+        mine = before_z(mine)
     other = [swap_z(m, 0) for m in mine]
     if beside_first is not None:
         other = beside_first(mine, other)
@@ -219,19 +221,23 @@
         copy.wait()
 
 
-def last_kernel(starts_ref, square_ref, w_ref, *rest):
-    pieces, (out_ref, new_ref, sem) = rest[:4], rest[4:]
-    for copy in renew(starts_ref, square_ref, w_ref, pieces, new_ref, out_ref, sem):
+def last_kernel(starts_ref, square_ref, w_hbm, *rest):
+    pieces, (out_ref, new_ref, sem, w_ref, fetched) = rest[:4], rest[4:]
+    spans = piece_rows(starts_ref)
+    arrive = fetch([w_hbm.at[at] for at in spans], [w_ref.at[at] for at in spans], fetched)
+    for copy in renew(starts_ref, square_ref, w_ref, pieces, new_ref, out_ref, sem, None, arrive):
         copy.wait()
 
 
-def attend_kernel(meta_ref, q_ref, halo_ref, k_ref, late_v_ref, v_ref, out_ref, halo_v_ref):
+def attend_kernel(meta_ref, q_ref, first_k_ref, halo_ref, k_ref, late_v_ref, v_ref, out_ref, halo_k_ref, halo_v_ref):
     local = q_ref.shape[0]
     anchor, width = meta_ref[0], meta_ref[1]
     scale = HD ** (-0.5)
-    halo_v_ref[0:EARLY] = halo_ref[WIN:]
+    halo_k_ref[0:EARLY] = first_k_ref[...]
+    halo_k_ref[EARLY:] = halo_ref[: WIN - EARLY]
+    halo_v_ref[0:EARLY] = halo_ref[WIN - EARLY :]
     halo_v_ref[EARLY:] = late_v_ref[...]
-    held = [(halo_ref, halo_v_ref, -WIN, WIN), (k_ref, v_ref, 0, local)]
+    held = [(halo_k_ref, halo_v_ref, -WIN, WIN), (k_ref, v_ref, 0, local)]
     for start in range(0, local, TILE):
         spans = []
         for keys, values, base, count in held:
@@ -313,7 +319,8 @@
     onward = [(i, i + 1) for i in range(count - 1)]
     tail = local - WIN
     halo_v = lax.ppermute(values[tail + EARLY :], SEQ, onward)
-    with_gather = jnp.concatenate([keys[tail:], values[tail : tail + EARLY]], axis=0)
+    halo_first = lax.ppermute(keys[tail : tail + EARLY], SEQ, onward)
+    with_gather = jnp.concatenate([keys[tail + EARLY :], values[tail : tail + EARLY]], axis=0)
     positions = anchor + jnp.arange(local, dtype=jnp.int32)[:, None]
     first_block = (positions < split[0]).astype(f32)
     rate_zero = token_rate * first_block
@@ -355,7 +362,11 @@
 
     kept = {}
 
-    square, pieces, send = finished(*reduced(halved[:CHUNKS], halved[CHUNKS:]), with_gather)
+    def have_first(mine):
+        kept["first"], mine = lax.optimization_barrier((halo_first, mine))
+        return mine
+
+    square, pieces, send = finished(*reduced(halved[:CHUNKS], halved[CHUNKS:], have_first), with_gather)
     halo = lax.ppermute(send, SEQ, onward)
     weights_one, wb_one, *halved = call(
         second_kernel,
@@ -372,11 +383,11 @@
         query, _ = lax.optimization_barrier((queries, before))
         attn = call(
             attend_kernel,
-            [SMEM_SPEC] + [VMEM_SPEC] * 5,
+            [SMEM_SPEC] + [VMEM_SPEC] * 6,
             array((local, HD), f32),
-            (meta, query, kept["halo"], keys, halo_v, values),
+            (meta, query, kept["first"], kept["halo"], keys, halo_v, values),
             20,
-            [pltpu.VMEM((WIN, HD), bf16)],
+            [pltpu.VMEM((WIN, HD), bf16)] * 2,
         )
         kept["attn"], after = lax.optimization_barrier((attn, after))
         return after
@@ -394,14 +405,14 @@
         kept["outputs"], after = lax.optimization_barrier((outputs, after))
         return after
 
-    square, pieces, _ = finished(*reduced(halved[:CHUNKS], halved[CHUNKS:], attend, apply), None)
+    square, pieces, _ = finished(*reduced(halved[:CHUNKS], halved[CHUNKS:], None, attend, apply), None)
     weights_two = call(
         last_kernel,
-        [SMEM_SPEC] + [VMEM_SPEC] * 6,
+        [SMEM_SPEC, VMEM_SPEC, HBM_SPEC] + [VMEM_SPEC] * 4,
         array((ROWS, HID), f32),
-        (starts, square, weights_one, *pieces),
+        (starts, square, in_hbm(weights_one), *pieces),
         20,
-        renewal,
+        renewal + [pltpu.VMEM((ROWS, HID), f32), pltpu.SemaphoreType.DMA((8,))],
         ANY_SPEC,
     )
     return (kept["outputs"], weights_two.reshape(1, 3, HD, HID))

time: 150 us -> 152 us (1.013)
  starting transfers between devices: 79.5 us -> 82.6 us
  local copies, waits for them, and re-layouts: 4.99 us -> 1.9 us
  waiting for transfers between devices: 27.3 us -> 29.1 us
    all_to_all x2, waiting for transfers between devices: 7.69 us -> 10.8 us  [spread(): return lax.all_to_all(squares, ('x', 'core', 'head'), 0, 0, tiled=True)]
    all_to_all x2, starting transfers between devices: 26.6 us -> 29.5 us  [spread(): return lax.all_to_all(squares, ('x', 'core', 'head'), 0, 0, tiled=True)]
    ppermute x0 -> x1, starting transfers between devices: none -> 2.04 us  [per_device(): halo_first = lax.ppermute(keys[tail:tail + EARLY], SEQ, onward)]
    ppermute x28, starting transfers between devices: 49.1 us -> 47.2 us  [exchange(): lax.ppermute(value, mesh_axes, [(i, partner(i)) for i in range(count)])]
    concatenate x2, local copies, waits for them, and re-layouts: 1.63 us -> 0.03 us  [gathered(): pair = jnp.concatenate([own, near], axis=0)]
    unnamed x15 -> x19, local copies, waits for them, and re-layouts: 2.52 us -> 0.93 us
  transfers between devices with their start and end apart: 32 -> 33, of which waited for: 16 -> 17; matrix products, arithmetic and copies ran while one was open for 8% -> 6% of each run, Pallas kernels for 10% -> 10%
where the time goes in v4:
time: 152 us; the launch traced here: 151 us
  starting transfers between devices  82.6 us (54%)
  waiting for transfers between devices  29.1 us (19%)
  Pallas kernels  26.4 us (17%)
  other arithmetic  8.6 us (6%)
  between operations  2.51 us (2%)
  local copies, waits for them, and re-layouts  1.9 us (1%)
    ppermute x28, starting transfers between devices, exchange(): lax.ppermute(value, mesh_axes, [(i, partner(i)) for i in range(count)])  47.2 us
    all_to_all x2, starting transfers between devices, spread(): return lax.all_to_all(squares, ('x', 'core', 'head'), 0, 0, tiled=True)  29.5 us
    pallas_call x7, Pallas kernels, call(): pl.pallas_call(kernel, out_shape=outs, in_specs=specs, out_specs=jax.tree...  26.4 us
    ppermute x28, waiting for transfers between devices, exchange(): lax.ppermute(value, mesh_axes, [(i, partner(i)) for i in range(count)])  18.3 us
    all_to_all x2, waiting for transfers between devices, spread(): return lax.all_to_all(squares, ('x', 'core', 'head'), 0, 0, tiled=True)  10.8 us
    convert_element_type x4, other arithmetic, reduced(): two(c, (1 - first) * half, half).astype(bf16)  3.36 us
  transfers between devices with their start and end apart: 33, of which 17 were waited for; matrix products, arithmetic and copies ran while one was open for 6% of the time, Pallas kernels for 10%

profile of v4, /device:TPU:1, one launch (start us, length us, event | category | flops | bytes accessed | tf_op | source)
XLA Modules:
  0.0 151.0 jit_solution(15731062243004324479)
XLA Ops:
  2.3 6.7 %shard_map.95 = (bf16[1536,512]{1,0:T(8,128)(2,1)}, bf16[768,256]{1,0:T(8,128)(2,1)}, bf16[768,256]{1,0:T(8,128)(2,1)}, f32[768,256]{1,0:T(8,128)S(1)}, f32[768,256]{1,0:T(8,128)S(1)}) custom-call(s32[1]{0:T(128)} %bitcast.1.place_ref, bf16[768,512]{1,0:T(8,128)(2,1)} %k_ref.1, bf16[768,512]{1,0:T(8,128)(2,1)} %targets_hbm.3, ...), custom_call_target="tpu_custom_call" | custom-call | tf_op jit(solution)/shard_map/pallas_call | solution.py:297
  9.0 3.3 %collective-permute-start.1 = (bf16[768,256]{1,0:T(8,128)(2,1)}, bf16[768,256]{1,0:T(8,128)(2,1)}, u32[]{:S(2)}, u32[]{:S(2)}) collective-permute-start(bf16[768,256]{1,0:T(8,128)(2,1)} %get-tuple-element.40), channel_id=1, source_target_pairs={{0,8},{8,0},{1,9},{9,1},{2,10},{10,2},{3,11},{11,3},{4,12},{12,4},... | collective-permute-start | bytes 1179656 | tf_op jit(solution)/shard_map/ppermute | solution.py:39
  12.5 1.6 %collective-permute-done.1 = bf16[768,256]{1,0:T(8,128)(2,1)} collective-permute-done((bf16[768,256]{1,0:T(8,128)(2,1)}, bf16[768,256]{1,0:T(8,128)(2,1)}, u32[]{:S(2)}, u32[]{:S(2)}) %collective-permute-start.1) | collective-permute-done | bytes 393248 | tf_op jit(solution)/shard_map/ppermute | solution.py:39
  14.0 1.6 %add_convert_fusion.3 = bf16[384,256]{1,0:T(8,128)(2,1)} fusion(f32[768,256]{1,0:T(8,128)S(1)} %get-tuple-element.39, s32[]{:T(128)S(6)} %select_n.24, bf16[768,256]{1,0:T(8,128)(2,1)} %collective-permute-done.1), kind=kLoop, calls=%fused_computation.5 | loop fusion | flops 294912 | bytes 786436 | tf_op jit(solution)/shard_map/convert_element_type | solution.py:96
  16.4 1.6 %add_convert_fusion.2 = bf16[384,256]{1,0:T(8,128)(2,1)} fusion(f32[768,256]{1,0:T(8,128)S(1)} %get-tuple-element.41, s32[]{:T(128)S(6)} %select_n.24, bf16[768,256]{1,0:T(8,128)(2,1)} %collective-permute-done.4), kind=kLoop, calls=%fused_computation.4 | loop fusion | flops 294912 | bytes 786436 | tf_op jit(solution)/shard_map/convert_element_type | solution.py:96
  18.1 1.9 %collective-permute-start.5 = (bf16[384,256]{1,0:T(8,128)(2,1)}, bf16[384,256]{1,0:T(8,128)(2,1)}, u32[]{:S(2)}, u32[]{:S(2)}) collective-permute-start(bf16[384,256]{1,0:T(8,128)(2,1)} %add_convert_fusion.2), channel_id=1, source_target_pairs={{0,16},{8,56},{16,0},{24,40},{32,48},{40,24},{48,32},{56,8},{1,17}... | collective-permute-start | bytes 589832 | tf_op jit(solution)/shard_map/ppermute | solution.py:39
  20.8 2.0 %collective-permute-start = (bf16[256,512]{1,0:T(8,128)(2,1)}, bf16[256,512]{1,0:T(8,128)(2,1)S(1)}, u32[]{:S(2)}, u32[]{:S(2)}) collective-permute-start(bf16[256,512]{1,0:T(8,128)(2,1)} %get-tuple-element.79), channel_id=1, source_target_pairs={{0,8},{8,16},{16,24},{24,32},{32,40},{40,48},{48,56},{56,64},{64,7... | collective-permute-start | bytes 786440 | tf_op jit(solution)/shard_map/ppermute | solution.py:322
  30.1 6.1 %collective-permute-start.7 = (bf16[192,256]{1,0:T(8,128)(2,1)S(1)}, bf16[192,256]{1,0:T(8,128)(2,1)S(1)}, u32[]{:S(2)}, u32[]{:S(2)}) collective-permute-start(bf16[192,256]{1,0:T(8,128)(2,1)S(1)} %add_convert_fusion.14), channel_id=1, source_target_pairs={{0,64},{8,200},{64,0},{72,136},{128,192},{136,72},{192,128},{200,8... | collective-permute-start | bytes 294920 | tf_op jit(solution)/shard_map/ppermute | solution.py:39
  36.4 2.0 %collective-permute-done.7 = bf16[192,256]{1,0:T(8,128)(2,1)S(1)} collective-permute-done((bf16[192,256]{1,0:T(8,128)(2,1)S(1)}, bf16[192,256]{1,0:T(8,128)(2,1)S(1)}, u32[]{:S(2)}, u32[]{:S(2)}) %collective-permute-start.7) | collective-permute-done | bytes 98336 | tf_op jit(solution)/shard_map/ppermute | solution.py:39
  38.4 2.3 %collective-permute-start.9 = (bf16[192,256]{1,0:T(8,128)(2,1)S(1)}, bf16[192,256]{1,0:T(8,128)(2,1)S(1)}, u32[]{:S(2)}, u32[]{:S(2)}) collective-permute-start(bf16[192,256]{1,0:T(8,128)(2,1)S(1)} %add_convert_fusion.11.refs_0_), channel_id=1, source_target_pairs={{0,192},{8,72},{64,128},{72,8},{128,64},{136,200},{192,0},{200,136... | collective-permute-start | bytes 294920 | tf_op jit(solution)/shard_map/ppermute | solution.py:39
  42.1 2.3 %collective-permute-start.10 = (bf16[192,256]{1,0:T(8,128)(2,1)S(1)}, bf16[192,256]{1,0:T(8,128)(2,1)S(1)}, u32[]{:S(2)}, u32[]{:S(2)}) collective-permute-start(bf16[192,256]{1,0:T(8,128)(2,1)S(1)} %add_convert_fusion.10.refs_1_), channel_id=1, source_target_pairs={{0,192},{8,72},{64,128},{72,8},{128,64},{136,200},{192,0},{200,136... | collective-permute-start | bytes 294920 | tf_op jit(solution)/shard_map/ppermute | solution.py:39
  45.2 1.4 collective-permute-done.10.refs_3_
  47.5 2.6 %collective-permute-start.12 = (bf16[192,512]{1,0:T(8,128)(2,1)S(1)}, bf16[192,512]{1,0:T(8,128)(2,1)S(1)}, u32[]{:S(2)}, u32[]{:S(2)}) collective-permute-start(bf16[192,512]{1,0:T(8,128)(2,1)S(1)} %get-tuple-element.47), channel_id=1, source_target_pairs={{0,48},{8,24},{16,32},{24,8},{32,16},{40,56},{48,0},{56,40},{1,49}... | collective-permute-start | bytes 589832 | tf_op jit(solution)/shard_map/ppermute | solution.py:39
  50.2 15.1 %all-to-all-start = ((f32[64,8,128]{2,1,0:T(8,128)}), f32[64,8,128]{2,1,0:T(8,128)S(1)}, u32[]{:S(2)}, u32[]{:S(2)}) async-start(f32[64,8,128]{2,1,0:T(8,128)} %get-tuple-element.48), calls=%async_computation | async-start | bytes 524288 | tf_op jit(solution)/shard_map/all_to_all | solution.py:63
  65.3 2.9 %collective-permute-start.13 = (bf16[384,512]{1,0:T(8,128)(2,1)S(1)}, bf16[384,512]{1,0:T(8,128)(2,1)S(1)}, u32[]{:S(2)}, u32[]{:S(2)}) collective-permute-start(bf16[384,512]{1,0:T(8,128)(2,1)S(1)} %constant_dynamic-update-slice_fusion.rest_0_), channel_id=1, source_target_pairs={{0,16},{8,56},{16,0},{24,40},{32,48},{40,24},{48,32},{56,8},{1,17}... | collective-permute-start | bytes 1179656 | tf_op jit(solution)/shard_map/ppermute | solution.py:39
  68.2 1.9 %collective-permute-start.11 = (bf16[512,512]{1,0:T(8,128)(2,1)}, bf16[512,512]{1,0:T(8,128)(2,1)S(1)}, u32[]{:S(2)}, u32[]{:S(2)}) collective-permute-start(bf16[512,512]{1,0:T(8,128)(2,1)} %pad_maximum_fusion), channel_id=1, source_target_pairs={{0,8},{8,16},{16,24},{24,32},{32,40},{40,48},{48,56},{56,64},{64,7... | collective-permute-start | bytes 1572872 | tf_op jit(solution)/shard_map/ppermute | solution.py:370
  70.9 4.0 %all-to-all-done.square_ref = f32[64,8,128]{2,1,0:T(8,128)S(1)} async-done(((f32[64,8,128]{2,1,0:T(8,128)}), f32[64,8,128]{2,1,0:T(8,128)S(1)}, u32[]{:S(2)}, u32[]{:S(2)}) %all-to-all-start) | async-done | bytes 262176 | tf_op jit(solution)/shard_map/all_to_all | solution.py:63
  76.0 1.8 %collective-permute-done.15.rest_3_ = bf16[384,512]{1,0:T(8,128)(2,1)} collective-permute-done((bf16[384,512]{1,0:T(8,128)(2,1)S(1)}, bf16[384,512]{1,0:T(8,128)(2,1)}, u32[]{:S(2)}, u32[]{:S(2)}) %collective-permute-start.15) | collective-permute-done | bytes 393248 | tf_op jit(solution)/shard_map/ppermute | solution.py:39
  77.7 7.7 %shard_map.97 = (f32[1536,512]{1,0:T(8,128)}, bf16[1536,512]{1,0:T(8,128)(2,1)S(1)}, bf16[768,256]{1,0:T(8,128)(2,1)S(1)}, bf16[768,256]{1,0:T(8,128)(2,1)S(1)},...) custom-call(s32[1]{0:T(128)} %bitcast.1.place_ref, s32[8]{0:T(128)S(1)} %broadcast_multiply_fusion.starts_ref, ...), custom_call_target="tpu_custom_call" | custom-call | tf_op jit(solution)/shard_map/pallas_call | solution.py:297
  87.4 3.6 %collective-permute-start.17 = (bf16[384,256]{1,0:T(8,128)(2,1)S(1)}, bf16[384,256]{1,0:T(8,128)(2,1)S(1)}, u32[]{:S(2)}, u32[]{:S(2)}) collective-permute-start(bf16[384,256]{1,0:T(8,128)(2,1)S(1)} %add_convert_fusion.1), channel_id=1, source_target_pairs={{0,16},{8,56},{16,0},{24,40},{32,48},{40,24},{48,32},{56,8},{1,17}... | collective-permute-start | bytes 589832 | tf_op jit(solution)/shard_map/ppermute | solution.py:39
  91.5 1.9 %collective-permute-start.22 = (bf16[256,512]{1,0:T(8,128)(2,1)S(1)}, bf16[256,512]{1,0:T(8,128)(2,1)S(1)}, u32[]{:S(2)}, u32[]{:S(2)}) collective-permute-start(bf16[256,512]{1,0:T(8,128)(2,1)S(1)} %get-tuple-element.76), channel_id=1, source_target_pairs={{0,8},{8,16},{16,24},{24,32},{32,40},{40,48},{48,56},{56,64},{64,7... | collective-permute-start | bytes 786440 | tf_op jit(solution)/shard_map/ppermute | solution.py:321
  94.2 1.5 collective-permute-start.18
  98.4 7.2 %collective-permute-start.23 = (bf16[192,256]{1,0:T(8,128)(2,1)S(1)}, bf16[192,256]{1,0:T(8,128)(2,1)S(1)}, u32[]{:S(2)}, u32[]{:S(2)}) collective-permute-start(bf16[192,256]{1,0:T(8,128)(2,1)S(1)} %add_convert_fusion.8), channel_id=1, source_target_pairs={{0,64},{8,200},{64,0},{72,136},{128,192},{136,72},{192,128},{200,8... | collective-permute-start | bytes 294920 | tf_op jit(solution)/shard_map/ppermute | solution.py:39
  105.6 2.3 %collective-permute-start.24 = (bf16[192,256]{1,0:T(8,128)(2,1)S(1)}, bf16[192,256]{1,0:T(8,128)(2,1)S(1)}, u32[]{:S(2)}, u32[]{:S(2)}) collective-permute-start(bf16[192,256]{1,0:T(8,128)(2,1)S(1)} %add_convert_fusion.6), channel_id=1, source_target_pairs={{0,64},{8,200},{64,0},{72,136},{128,192},{136,72},{192,128},{200,8... | collective-permute-start | bytes 294920 | tf_op jit(solution)/shard_map/ppermute | solution.py:39
  108.0 2.8 %shard_map.98.attn_ref = f32[768,512]{1,0:T(8,128)S(1)} custom-call(s32[3]{0:T(128)S(1)} %pad_add_fusion.meta_ref, bf16[768,512]{1,0:T(8,128)(2,1)S(1)} %copy-done.2, bf16[256,512]{1,0:T(8,128)(2,1)S(1)} %copy-done.6, bf16[512,512]{1,0:T(8,128)(2,1)S(1)} %collective-permute-done.11.halo_ref, bf16[768,512]{1,0:T(8,128)(2,1)S(1)} %copy-done.1, ...), custom_call_target="tpu_custom_call" | custom-call | tf_op jit(solution)/shard_map/pallas_call | solution.py:297
  111.7 2.4 %collective-permute-start.26 = (bf16[192,256]{1,0:T(8,128)(2,1)S(1)}, bf16[192,256]{1,0:T(8,128)(2,1)S(1)}, u32[]{:S(2)}, u32[]{:S(2)}) collective-permute-start(bf16[192,256]{1,0:T(8,128)(2,1)S(1)} %add_convert_fusion.4.refs_1_), channel_id=1, source_target_pairs={{0,192},{8,72},{64,128},{72,8},{128,64},{136,200},{192,0},{200,136... | collective-permute-start | bytes 294920 | tf_op jit(solution)/shard_map/ppermute | solution.py:39
  114.4 3.9 %shard_map.99 = bf16[768,512]{1,0:T(8,128)(2,1)} custom-call(s32[3]{0:T(128)S(1)} %pad_add_fusion.meta_ref, bf16[768,512]{1,0:T(8,128)(2,1)S(1)} %copy-done.2, f32[768,512]{1,0:T(8,128)S(1)} %shard_map.98.attn_ref, bf16[1536,512]{1,0:T(8,128)(2,1)S(1)} %copy-done.4, bf16[1536,512]{1,0:T(8,128)(2,1)S(1)} %get-tuple-element.67.late_ref), custom_call_target="tpu_custom_call" | custom-call | tf_op jit(solution)/shard_map/pallas_call | solution.py:297
  120.7 14.4 %all-to-all-start.1 = ((f32[64,8,128]{2,1,0:T(8,128)}), f32[64,8,128]{2,1,0:T(8,128)S(1)}, u32[]{:S(2)}, u32[]{:S(2)}) async-start(f32[64,8,128]{2,1,0:T(8,128)} %get-tuple-element.72), calls=%async_computation.1 | async-start | bytes 524288 | tf_op jit(solution)/shard_map/all_to_all | solution.py:63
  135.1 2.9 %collective-permute-start.28 = (bf16[384,512]{1,0:T(8,128)(2,1)S(1)}, bf16[384,512]{1,0:T(8,128)(2,1)S(1)}, u32[]{:S(2)}, u32[]{:S(2)}) collective-permute-start(bf16[384,512]{1,0:T(8,128)(2,1)S(1)} %constant_dynamic-update-slice_fusion.2.rest_0_), channel_id=1, source_target_pairs={{0,16},{8,56},{16,0},{24,40},{32,48},{40,24},{48,32},{56,8},{1,17}... | collective-permute-start | bytes 1179656 | tf_op jit(solution)/shard_map/ppermute | solution.py:39
  138.0 6.7 %all-to-all-done.1.square_ref = f32[64,8,128]{2,1,0:T(8,128)S(1)} async-done(((f32[64,8,128]{2,1,0:T(8,128)}), f32[64,8,128]{2,1,0:T(8,128)S(1)}, u32[]{:S(2)}, u32[]{:S(2)}) %all-to-all-start.1) | async-done | bytes 262176 | tf_op jit(solution)/shard_map/all_to_all | solution.py:63
  145.7 1.7 %collective-permute-done.30.rest_3_ = bf16[384,512]{1,0:T(8,128)(2,1)S(1)} collective-permute-done((bf16[384,512]{1,0:T(8,128)(2,1)S(1)}, bf16[384,512]{1,0:T(8,128)(2,1)S(1)}, u32[]{:S(2)}, u32[]{:S(2)}) %collective-permute-start.30) | collective-permute-done | bytes 393248 | tf_op jit(solution)/shard_map/ppermute | solution.py:39
  147.4 3.4 %shard_map.101 = f32[1536,512]{1,0:T(8,128)} custom-call(s32[8]{0:T(128)S(1)} %broadcast_multiply_fusion.starts_ref, f32[64,8,128]{2,1,0:T(8,128)S(1)} %all-to-all-done.1.square_ref, f32[1536,512]{1,0:T(8,128)} %get-tuple-element.74.w_hbm, bf16[384,512]{1,0:T(8,128)(2,1)S(1)} %constant_dynamic-update-slice_fusion.2.rest_0_, ...), custom_call_target="tpu_custom_call" | custom-call | tf_op jit(solution)/shard_map/pallas_call | solution.py:297
  (85 shorter events, 24.8 us)
Async XLA Ops:
  9.0 5.0 %collective-permute-start.1 = (bf16[768,256]{1,0:T(8,128)(2,1)}, bf16[768,256]{1,0:T(8,128)(2,1)}, u32[]{:S(2)}, u32[]{:S(2)}) collective-permute-start(bf16[768,256]{1,0:T(8,128)(2,1)} %get-tuple-element.40), channel_id=1, source_target_pairs={{0,8},{8,0},{1,9},{9,1},{2,10},{10,2},{3,11},{11,3},{4,12},{12,4},... | collective-permute-start | bytes 1179656 | tf_op jit(solution)/shard_map/ppermute | solution.py:39
  12.3 4.1 %collective-permute-start.4 = (bf16[768,256]{1,0:T(8,128)(2,1)}, bf16[768,256]{1,0:T(8,128)(2,1)}, u32[]{:S(2)}, u32[]{:S(2)}) collective-permute-start(bf16[768,256]{1,0:T(8,128)(2,1)} %get-tuple-element.42), channel_id=1, source_target_pairs={{0,8},{8,0},{1,9},{9,1},{2,10},{10,2},{3,11},{11,3},{4,12},{12,4},... | collective-permute-start | bytes 1179656 | tf_op jit(solution)/shard_map/ppermute | solution.py:39
  15.7 7.2 %collective-permute-start.2 = (bf16[384,256]{1,0:T(8,128)(2,1)}, bf16[384,256]{1,0:T(8,128)(2,1)}, u32[]{:S(2)}, u32[]{:S(2)}) collective-permute-start(bf16[384,256]{1,0:T(8,128)(2,1)} %add_convert_fusion.3), channel_id=1, source_target_pairs={{0,16},{8,56},{16,0},{24,40},{32,48},{40,24},{48,32},{56,8},{1,17}... | collective-permute-start | bytes 589832 | tf_op jit(solution)/shard_map/ppermute | solution.py:39
  18.1 6.2 %collective-permute-start.5 = (bf16[384,256]{1,0:T(8,128)(2,1)}, bf16[384,256]{1,0:T(8,128)(2,1)}, u32[]{:S(2)}, u32[]{:S(2)}) collective-permute-start(bf16[384,256]{1,0:T(8,128)(2,1)} %add_convert_fusion.2), channel_id=1, source_target_pairs={{0,16},{8,56},{16,0},{24,40},{32,48},{40,24},{48,32},{56,8},{1,17}... | collective-permute-start | bytes 589832 | tf_op jit(solution)/shard_map/ppermute | solution.py:39
  20.8 9.3 %collective-permute-start = (bf16[256,512]{1,0:T(8,128)(2,1)}, bf16[256,512]{1,0:T(8,128)(2,1)S(1)}, u32[]{:S(2)}, u32[]{:S(2)}) collective-permute-start(bf16[256,512]{1,0:T(8,128)(2,1)} %get-tuple-element.79), channel_id=1, source_target_pairs={{0,8},{8,16},{16,24},{24,32},{32,40},{40,48},{48,56},{56,64},{64,7... | collective-permute-start | bytes 786440 | tf_op jit(solution)/shard_map/ppermute | solution.py:322
  23.9 3.6 %collective-permute-start.3 = (bf16[192,256]{1,0:T(8,128)(2,1)S(1)}, bf16[192,256]{1,0:T(8,128)(2,1)S(1)}, u32[]{:S(2)}, u32[]{:S(2)}) collective-permute-start(bf16[192,256]{1,0:T(8,128)(2,1)S(1)} %add_convert_fusion.15), channel_id=1, source_target_pairs={{0,48},{8,24},{16,32},{24,8},{32,16},{40,56},{48,0},{56,40},{1,49}... | collective-permute-start | bytes 294920 | tf_op jit(solution)/shard_map/ppermute | solution.py:39
  25.3 3.8 %collective-permute-start.6 = (bf16[192,256]{1,0:T(8,128)(2,1)S(1)}, bf16[192,256]{1,0:T(8,128)(2,1)S(1)}, u32[]{:S(2)}, u32[]{:S(2)}) collective-permute-start(bf16[192,256]{1,0:T(8,128)(2,1)S(1)} %add_convert_fusion.13), channel_id=1, source_target_pairs={{0,48},{8,24},{16,32},{24,8},{32,16},{40,56},{48,0},{56,40},{1,49}... | collective-permute-start | bytes 294920 | tf_op jit(solution)/shard_map/ppermute | solution.py:39
  30.1 8.2 %collective-permute-start.7 = (bf16[192,256]{1,0:T(8,128)(2,1)S(1)}, bf16[192,256]{1,0:T(8,128)(2,1)S(1)}, u32[]{:S(2)}, u32[]{:S(2)}) collective-permute-start(bf16[192,256]{1,0:T(8,128)(2,1)S(1)} %add_convert_fusion.14), channel_id=1, source_target_pairs={{0,64},{8,200},{64,0},{72,136},{128,192},{136,72},{192,128},{200,8... | collective-permute-start | bytes 294920 | tf_op jit(solution)/shard_map/ppermute | solution.py:39
  36.3 5.8 %collective-permute-start.8 = (bf16[192,256]{1,0:T(8,128)(2,1)S(1)}, bf16[192,256]{1,0:T(8,128)(2,1)S(1)}, u32[]{:S(2)}, u32[]{:S(2)}) collective-permute-start(bf16[192,256]{1,0:T(8,128)(2,1)S(1)} %add_convert_fusion.12), channel_id=1, source_target_pairs={{0,64},{8,200},{64,0},{72,136},{128,192},{136,72},{192,128},{200,8... | collective-permute-start | bytes 294920 | tf_op jit(solution)/shard_map/ppermute | solution.py:39
  38.4 6.8 %collective-permute-start.9 = (bf16[192,256]{1,0:T(8,128)(2,1)S(1)}, bf16[192,256]{1,0:T(8,128)(2,1)S(1)}, u32[]{:S(2)}, u32[]{:S(2)}) collective-permute-start(bf16[192,256]{1,0:T(8,128)(2,1)S(1)} %add_convert_fusion.11.refs_0_), channel_id=1, source_target_pairs={{0,192},{8,72},{64,128},{72,8},{128,64},{136,200},{192,0},{200,136... | collective-permute-start | bytes 294920 | tf_op jit(solution)/shard_map/ppermute | solution.py:39
  42.1 4.6 %collective-permute-start.10 = (bf16[192,256]{1,0:T(8,128)(2,1)S(1)}, bf16[192,256]{1,0:T(8,128)(2,1)S(1)}, u32[]{:S(2)}, u32[]{:S(2)}) collective-permute-start(bf16[192,256]{1,0:T(8,128)(2,1)S(1)} %add_convert_fusion.10.refs_1_), channel_id=1, source_target_pairs={{0,192},{8,72},{64,128},{72,8},{128,64},{136,200},{192,0},{200,136... | collective-permute-start | bytes 294920 | tf_op jit(solution)/shard_map/ppermute | solution.py:39
  47.5 17.7 %collective-permute-start.12 = (bf16[192,512]{1,0:T(8,128)(2,1)S(1)}, bf16[192,512]{1,0:T(8,128)(2,1)S(1)}, u32[]{:S(2)}, u32[]{:S(2)}) collective-permute-start(bf16[192,512]{1,0:T(8,128)(2,1)S(1)} %get-tuple-element.47), channel_id=1, source_target_pairs={{0,48},{8,24},{16,32},{24,8},{32,16},{40,56},{48,0},{56,40},{1,49}... | collective-permute-start | bytes 589832 | tf_op jit(solution)/shard_map/ppermute | solution.py:39
  50.2 24.8 %all-to-all-start = ((f32[64,8,128]{2,1,0:T(8,128)}), f32[64,8,128]{2,1,0:T(8,128)S(1)}, u32[]{:S(2)}, u32[]{:S(2)}) async-start(f32[64,8,128]{2,1,0:T(8,128)} %get-tuple-element.48), calls=%async_computation | async-start | bytes 524288 | tf_op jit(solution)/shard_map/all_to_all | solution.py:63
  65.3 10.6 %collective-permute-start.13 = (bf16[384,512]{1,0:T(8,128)(2,1)S(1)}, bf16[384,512]{1,0:T(8,128)(2,1)S(1)}, u32[]{:S(2)}, u32[]{:S(2)}) collective-permute-start(bf16[384,512]{1,0:T(8,128)(2,1)S(1)} %constant_dynamic-update-slice_fusion.rest_0_), channel_id=1, source_target_pairs={{0,16},{8,56},{16,0},{24,40},{32,48},{40,24},{48,32},{56,8},{1,17}... | collective-permute-start | bytes 1179656 | tf_op jit(solution)/shard_map/ppermute | solution.py:39
  68.2 17.3 %collective-permute-start.11 = (bf16[512,512]{1,0:T(8,128)(2,1)}, bf16[512,512]{1,0:T(8,128)(2,1)S(1)}, u32[]{:S(2)}, u32[]{:S(2)}) collective-permute-start(bf16[512,512]{1,0:T(8,128)(2,1)} %pad_maximum_fusion), channel_id=1, source_target_pairs={{0,8},{8,16},{16,24},{24,32},{32,40},{40,48},{48,56},{56,64},{64,7... | collective-permute-start | bytes 1572872 | tf_op jit(solution)/shard_map/ppermute | solution.py:370
  70.1 5.9 %collective-permute-start.14 = (bf16[384,512]{1,0:T(8,128)(2,1)S(1)}, bf16[384,512]{1,0:T(8,128)(2,1)S(1)}, u32[]{:S(2)}, u32[]{:S(2)}) collective-permute-start(bf16[384,512]{1,0:T(8,128)(2,1)S(1)} %constant_dynamic-update-slice_fusion.rest_0_), channel_id=1, source_target_pairs={{0,8},{8,0},{1,9},{9,1},{2,10},{10,2},{3,11},{11,3},{4,12},{12,4},... | collective-permute-start | bytes 1179656 | tf_op jit(solution)/shard_map/ppermute | solution.py:39
  75.9 1.9 %collective-permute-start.15 = (bf16[384,512]{1,0:T(8,128)(2,1)S(1)}, bf16[384,512]{1,0:T(8,128)(2,1)}, u32[]{:S(2)}, u32[]{:S(2)}) collective-permute-start(bf16[384,512]{1,0:T(8,128)(2,1)S(1)} %collective-permute-done.13.rest_1_), channel_id=1, source_target_pairs={{0,8},{8,0},{1,9},{9,1},{2,10},{10,2},{3,11},{11,3},{4,12},{12,4},... | collective-permute-start | bytes 1179656 | tf_op jit(solution)/shard_map/ppermute | solution.py:39
  85.5 1.8 %collective-permute-start.16 = (bf16[768,256]{1,0:T(8,128)(2,1)S(1)}, bf16[768,256]{1,0:T(8,128)(2,1)S(1)}, u32[]{:S(2)}, u32[]{:S(2)}) collective-permute-start(bf16[768,256]{1,0:T(8,128)(2,1)S(1)} %get-tuple-element.56), channel_id=1, source_target_pairs={{0,8},{8,0},{1,9},{9,1},{2,10},{10,2},{3,11},{11,3},{4,12},{12,4},... | collective-permute-start | bytes 1179656 | tf_op jit(solution)/shard_map/ppermute | solution.py:39
  85.8 5.2 %collective-permute-start.19 = (bf16[768,256]{1,0:T(8,128)(2,1)S(1)}, bf16[768,256]{1,0:T(8,128)(2,1)S(1)}, u32[]{:S(2)}, u32[]{:S(2)}) collective-permute-start(bf16[768,256]{1,0:T(8,128)(2,1)S(1)} %get-tuple-element.58), channel_id=1, source_target_pairs={{0,8},{8,0},{1,9},{9,1},{2,10},{10,2},{3,11},{11,3},{4,12},{12,4},... | collective-permute-start | bytes 1179656 | tf_op jit(solution)/shard_map/ppermute | solution.py:39
  87.4 6.7 %collective-permute-start.17 = (bf16[384,256]{1,0:T(8,128)(2,1)S(1)}, bf16[384,256]{1,0:T(8,128)(2,1)S(1)}, u32[]{:S(2)}, u32[]{:S(2)}) collective-permute-start(bf16[384,256]{1,0:T(8,128)(2,1)S(1)} %add_convert_fusion.1), channel_id=1, source_target_pairs={{0,16},{8,56},{16,0},{24,40},{32,48},{40,24},{48,32},{56,8},{1,17}... | collective-permute-start | bytes 589832 | tf_op jit(solution)/shard_map/ppermute | solution.py:39
  91.0 5.8 %collective-permute-start.20 = (bf16[384,256]{1,0:T(8,128)(2,1)S(1)}, bf16[384,256]{1,0:T(8,128)(2,1)S(1)}, u32[]{:S(2)}, u32[]{:S(2)}) collective-permute-start(bf16[384,256]{1,0:T(8,128)(2,1)S(1)} %add_convert_fusion), channel_id=1, source_target_pairs={{0,16},{8,56},{16,0},{24,40},{32,48},{40,24},{48,32},{56,8},{1,17}... | collective-permute-start | bytes 589832 | tf_op jit(solution)/shard_map/ppermute | solution.py:39
  91.5 16.5 %collective-permute-start.22 = (bf16[256,512]{1,0:T(8,128)(2,1)S(1)}, bf16[256,512]{1,0:T(8,128)(2,1)S(1)}, u32[]{:S(2)}, u32[]{:S(2)}) collective-permute-start(bf16[256,512]{1,0:T(8,128)(2,1)S(1)} %get-tuple-element.76), channel_id=1, source_target_pairs={{0,8},{8,16},{16,24},{24,32},{32,40},{40,48},{48,56},{56,64},{64,7... | collective-permute-start | bytes 786440 | tf_op jit(solution)/shard_map/ppermute | solution.py:321
  94.2 4.1 %collective-permute-start.18 = (bf16[192,256]{1,0:T(8,128)(2,1)S(1)}, bf16[192,256]{1,0:T(8,128)(2,1)S(1)}, u32[]{:S(2)}, u32[]{:S(2)}) collective-permute-start(bf16[192,256]{1,0:T(8,128)(2,1)S(1)} %add_convert_fusion.9), channel_id=1, source_target_pairs={{0,48},{8,24},{16,32},{24,8},{32,16},{40,56},{48,0},{56,40},{1,49}... | collective-permute-start | bytes 294920 | tf_op jit(solution)/shard_map/ppermute | solution.py:39
  96.9 8.6 %collective-permute-start.21 = (bf16[192,256]{1,0:T(8,128)(2,1)S(1)}, bf16[192,256]{1,0:T(8,128)(2,1)S(1)}, u32[]{:S(2)}, u32[]{:S(2)}) collective-permute-start(bf16[192,256]{1,0:T(8,128)(2,1)S(1)} %add_convert_fusion.7), channel_id=1, source_target_pairs={{0,48},{8,24},{16,32},{24,8},{32,16},{40,56},{48,0},{56,40},{1,49}... | collective-permute-start | bytes 294920 | tf_op jit(solution)/shard_map/ppermute | solution.py:39
  98.4 12.4 %collective-permute-start.23 = (bf16[192,256]{1,0:T(8,128)(2,1)S(1)}, bf16[192,256]{1,0:T(8,128)(2,1)S(1)}, u32[]{:S(2)}, u32[]{:S(2)}) collective-permute-start(bf16[192,256]{1,0:T(8,128)(2,1)S(1)} %add_convert_fusion.8), channel_id=1, source_target_pairs={{0,64},{8,200},{64,0},{72,136},{128,192},{136,72},{192,128},{200,8... | collective-permute-start | bytes 294920 | tf_op jit(solution)/shard_map/ppermute | solution.py:39
  105.6 6.1 %collective-permute-start.24 = (bf16[192,256]{1,0:T(8,128)(2,1)S(1)}, bf16[192,256]{1,0:T(8,128)(2,1)S(1)}, u32[]{:S(2)}, u32[]{:S(2)}) collective-permute-start(bf16[192,256]{1,0:T(8,128)(2,1)S(1)} %add_convert_fusion.6), channel_id=1, source_target_pairs={{0,64},{8,200},{64,0},{72,136},{128,192},{136,72},{192,128},{200,8... | collective-permute-start | bytes 294920 | tf_op jit(solution)/shard_map/ppermute | solution.py:39
  111.7 6.6 %collective-permute-start.26 = (bf16[192,256]{1,0:T(8,128)(2,1)S(1)}, bf16[192,256]{1,0:T(8,128)(2,1)S(1)}, u32[]{:S(2)}, u32[]{:S(2)}) collective-permute-start(bf16[192,256]{1,0:T(8,128)(2,1)S(1)} %add_convert_fusion.4.refs_1_), channel_id=1, source_target_pairs={{0,192},{8,72},{64,128},{72,8},{128,64},{136,200},{192,0},{200,136... | collective-permute-start | bytes 294920 | tf_op jit(solution)/shard_map/ppermute | solution.py:39
  114.1 4.7 %collective-permute-start.25 = (bf16[192,256]{1,0:T(8,128)(2,1)S(1)}, bf16[192,256]{1,0:T(8,128)(2,1)S(1)}, u32[]{:S(2)}, u32[]{:S(2)}) collective-permute-start(bf16[192,256]{1,0:T(8,128)(2,1)S(1)} %add_convert_fusion.5.refs_0_), channel_id=1, source_target_pairs={{0,192},{8,72},{64,128},{72,8},{128,64},{136,200},{192,0},{200,136... | collective-permute-start | bytes 294920 | tf_op jit(solution)/shard_map/ppermute | solution.py:39
  119.7 15.4 %collective-permute-start.27 = (bf16[192,512]{1,0:T(8,128)(2,1)S(1)}, bf16[192,512]{1,0:T(8,128)(2,1)S(1)}, u32[]{:S(2)}, u32[]{:S(2)}) collective-permute-start(bf16[192,512]{1,0:T(8,128)(2,1)S(1)} %get-tuple-element.71), channel_id=1, source_target_pairs={{0,48},{8,24},{16,32},{24,8},{32,16},{40,56},{48,0},{56,40},{1,49}... | collective-permute-start | bytes 589832 | tf_op jit(solution)/shard_map/ppermute | solution.py:39
  120.7 24.1 %all-to-all-start.1 = ((f32[64,8,128]{2,1,0:T(8,128)}), f32[64,8,128]{2,1,0:T(8,128)S(1)}, u32[]{:S(2)}, u32[]{:S(2)}) async-start(f32[64,8,128]{2,1,0:T(8,128)} %get-tuple-element.72), calls=%async_computation.1 | async-start | bytes 524288 | tf_op jit(solution)/shard_map/all_to_all | solution.py:63
  135.1 10.6 %collective-permute-start.28 = (bf16[384,512]{1,0:T(8,128)(2,1)S(1)}, bf16[384,512]{1,0:T(8,128)(2,1)S(1)}, u32[]{:S(2)}, u32[]{:S(2)}) collective-permute-start(bf16[384,512]{1,0:T(8,128)(2,1)S(1)} %constant_dynamic-update-slice_fusion.2.rest_0_), channel_id=1, source_target_pairs={{0,16},{8,56},{16,0},{24,40},{32,48},{40,24},{48,32},{56,8},{1,17}... | collective-permute-start | bytes 1179656 | tf_op jit(solution)/shard_map/ppermute | solution.py:39
  138.0 7.7 %collective-permute-start.29 = (bf16[384,512]{1,0:T(8,128)(2,1)S(1)}, bf16[384,512]{1,0:T(8,128)(2,1)S(1)}, u32[]{:S(2)}, u32[]{:S(2)}) collective-permute-start(bf16[384,512]{1,0:T(8,128)(2,1)S(1)} %constant_dynamic-update-slice_fusion.2.rest_0_), channel_id=1, source_target_pairs={{0,8},{8,0},{1,9},{9,1},{2,10},{10,2},{3,11},{11,3},{4,12},{12,4},... | collective-permute-start | bytes 1179656 | tf_op jit(solution)/shard_map/ppermute | solution.py:39
  (9 other events, 173.8 us)

commit v5 on v3

--- a/solution.py
+++ b/solution.py
@@ -18,7 +18,7 @@
 TILE = 256
 CHUNKS = 2
 SHARES = 64
-EARLY = 256
+EARLY = 128
 
 fast_rate = 0.01
 epsilon = 1e-06
@@ -161,7 +161,7 @@
         outs[CHUNKS + c][...] = grad_ref[pl.ds(pl.multiple_of(place * half, half), half)]
 
 
-def first_kernel(place_ref, keys_hbm, targets_hbm, rate_ref, w_hbm, wb_hbm, *rest):
+def first_kernel(place_ref, keys_hbm, targets_hbm, values_hbm, rate_ref, w_hbm, wb_hbm, mid_hbm, late_hbm, *rest):
     outs, (grad_ref, keys_ref, targets_ref, w_ref, wb_ref, sem) = rest[: 2 * CHUNKS], rest[2 * CHUNKS :]
     thirds = [pl.ds(i * HD, HD) for i in range(3)]
     copies = fetch(
@@ -169,6 +169,15 @@
         [w_ref.at[t] for t in thirds] + [keys_ref, targets_ref],
         sem,
     )
+    tail = keys_hbm.shape[0] - WIN
+    tails = [
+        (keys_hbm.at[pl.ds(tail, WIN)], mid_hbm.at[pl.ds(0, WIN)]),
+        (values_hbm.at[pl.ds(tail, EARLY)], mid_hbm.at[pl.ds(WIN, EARLY)]),
+        (values_hbm.at[pl.ds(tail + EARLY, WIN - EARLY)], late_hbm),
+    ]
+    moves = [pltpu.make_async_copy(a, b, sem.at[6 + i]) for i, (a, b) in enumerate(tails)]
+    for move in moves:
+        move.start()
     for copy, third in zip(copies, thirds):
         copy.wait()
         wb_ref[third] = w_ref[third].astype(bf16)
@@ -178,6 +187,8 @@
     copies[4].wait()
     grads(place_ref[0], keys_ref, targets_ref, rate_ref, wb_ref, grad_ref, outs)
     leave.wait()
+    for move in moves:
+        move.wait()
 
 
 def piece_rows(starts_ref):
@@ -219,9 +230,11 @@
         copy.wait()
 
 
-def last_kernel(starts_ref, square_ref, w_ref, *rest):
-    pieces, (out_ref, new_ref, sem) = rest[:4], rest[4:]
-    for copy in renew(starts_ref, square_ref, w_ref, pieces, new_ref, out_ref, sem):
+def last_kernel(starts_ref, square_ref, w_hbm, *rest):
+    pieces, (out_ref, new_ref, sem, w_ref, fetched) = rest[:4], rest[4:]
+    spans = piece_rows(starts_ref)
+    arrive = fetch([w_hbm.at[at] for at in spans], [w_ref.at[at] for at in spans], fetched)
+    for copy in renew(starts_ref, square_ref, w_ref, pieces, new_ref, out_ref, sem, None, arrive):
         copy.wait()
 
 
@@ -311,9 +324,6 @@
     anchor = lax.axis_index(SEQ) * local
     count = lax.axis_size(SEQ)
     onward = [(i, i + 1) for i in range(count - 1)]
-    tail = local - WIN
-    halo_v = lax.ppermute(values[tail + EARLY :], SEQ, onward)
-    with_gather = jnp.concatenate([keys[tail:], values[tail : tail + EARLY]], axis=0)
     positions = anchor + jnp.arange(local, dtype=jnp.int32)[:, None]
     first_block = (positions < split[0]).astype(f32)
     rate_zero = token_rate * first_block
@@ -329,15 +339,16 @@
 
     fetched = [pltpu.VMEM((local, HD), bf16)] * 2
 
-    wb_zero, *halved = call(
+    wb_zero, with_gather, late, *halved = call(
         first_kernel,
-        [SMEM_SPEC, HBM_SPEC, HBM_SPEC, VMEM_SPEC, HBM_SPEC],
-        [pltpu.HBM((ROWS, HID), bf16)] + wide,
-        (core, in_hbm(keys), in_hbm(targets), rate_zero, in_hbm(weights_zero)),
+        [SMEM_SPEC, HBM_SPEC, HBM_SPEC, HBM_SPEC, VMEM_SPEC, HBM_SPEC],
+        [pltpu.HBM((ROWS, HID), bf16), pltpu.HBM((WIN + EARLY, HD), bf16), pltpu.HBM((WIN - EARLY, HD), bf16)] + wide,
+        (core, in_hbm(keys), in_hbm(targets), in_hbm(values), rate_zero, in_hbm(weights_zero)),
         24,
-        [grad] + fetched + [pltpu.VMEM((ROWS, HID), f32), pltpu.VMEM((ROWS, HID), bf16), pltpu.SemaphoreType.DMA((6,))],
-        [HBM_SPEC] + [VMEM_SPEC] * (2 * CHUNKS),
-    )
+        [grad] + fetched + [pltpu.VMEM((ROWS, HID), f32), pltpu.VMEM((ROWS, HID), bf16), pltpu.SemaphoreType.DMA((9,))],
+        [HBM_SPEC] * 3 + [VMEM_SPEC] * (2 * CHUNKS),
+    )
+    halo_v = lax.ppermute(late, SEQ, onward)
 
     def finished(mine, other, later):
         total, square = call(
@@ -397,11 +408,11 @@
     square, pieces, _ = finished(*reduced(halved[:CHUNKS], halved[CHUNKS:], attend, apply), None)
     weights_two = call(
         last_kernel,
-        [SMEM_SPEC] + [VMEM_SPEC] * 6,
+        [SMEM_SPEC, VMEM_SPEC, HBM_SPEC] + [VMEM_SPEC] * 4,
         array((ROWS, HID), f32),
-        (starts, square, weights_one, *pieces),
+        (starts, square, in_hbm(weights_one), *pieces),
         20,
-        renewal,
+        renewal + [pltpu.VMEM((ROWS, HID), f32), pltpu.SemaphoreType.DMA((8,))],
         ANY_SPEC,
     )
     return (kept["outputs"], weights_two.reshape(1, 3, HD, HID))

time: 150 us -> 170 us (1.13)
  Pallas kernels: 26.8 us -> 52.1 us
  waiting for transfers between devices: 27.3 us -> 37.4 us
  other arithmetic: 8.74 us -> 0.79 us
  local copies, waits for them, and re-layouts: 4.99 us -> 1.03 us
  starting transfers between devices: 79.5 us -> 76 us
    pallas_call x7, Pallas kernels: 26.8 us -> 52.1 us  [call(): pl.pallas_call(kernel, out_shape=outs, in_specs=specs, out_specs=jax.tree...]
    ppermute x28, waiting for transfers between devices: 19.6 us -> 26.7 us  [exchange(): lax.ppermute(value, mesh_axes, [(i, partner(i)) for i in range(count)])]
    ppermute x28, starting transfers between devices: 49.1 us -> 43.9 us  [exchange(): lax.ppermute(value, mesh_axes, [(i, partner(i)) for i in range(count)])]
    convert_element_type x4, other arithmetic: 3.4 us -> 0.17 us  [reduced(): two(c, (1 - first) * half, half).astype(bf16)]
    all_to_all x2, waiting for transfers between devices: 7.69 us -> 10.8 us  [spread(): return lax.all_to_all(squares, ('x', 'core', 'head'), 0, 0, tiled=True)]
    convert_element_type x4, other arithmetic: 2.1 us -> 0.2 us  [reduced(): mine = [m.astype(bf16) for m in mine]]
    convert_element_type x4, other arithmetic: 2.03 us -> 0.14 us  [reduced(): (two(c, first * half + away, rows) + rows_of(got_x[c], away, rows).astype...]
  transfers between devices with their start and end apart: 32 -> 32, of which waited for: 16 -> 17; matrix products, arithmetic and copies ran while one was open for 8% -> 0% of each run, Pallas kernels for 10% -> 8%
where the time goes in v5:
time: 170 us
  starting transfers between devices  76 us (45%)
  Pallas kernels  52.1 us (31%)
  waiting for transfers between devices  37.4 us (22%)
  between operations  2.46 us (1%)
    pallas_call x7, Pallas kernels, call(): pl.pallas_call(kernel, out_shape=outs, in_specs=specs, out_specs=jax.tree...  52.1 us
    ppermute x28, starting transfers between devices, exchange(): lax.ppermute(value, mesh_axes, [(i, partner(i)) for i in range(count)])  43.9 us
    all_to_all x2, starting transfers between devices, spread(): return lax.all_to_all(squares, ('x', 'core', 'head'), 0, 0, tiled=True)  28.2 us
    ppermute x28, waiting for transfers between devices, exchange(): lax.ppermute(value, mesh_axes, [(i, partner(i)) for i in range(count)])  26.7 us
    all_to_all x2, waiting for transfers between devices, spread(): return lax.all_to_all(squares, ('x', 'core', 'head'), 0, 0, tiled=True)  10.8 us
  transfers between devices with their start and end apart: 32, of which 17 were waited for; matrix products, arithmetic and copies ran while one was open for 0% of the time, Pallas kernels for 8%

profile of v5, /device:TPU:1, one launch (start us, length us, event | category | flops | bytes accessed | tf_op | source)
XLA Modules:
  0.0 169.8 jit_solution(16112480322618497497)
XLA Ops:
  2.3 33.0 %shard_map.95 = (bf16[1536,512]{1,0:T(8,128)(2,1)}, bf16[640,512]{1,0:T(8,128)(2,1)}, bf16[384,512]{1,0:T(8,128)(2,1)}, bf16[768,256]{1,0:T(8,128)(2,1)S(1)}, bf...) custom-call(s32[1]{0:T(128)} %bitcast.1.place_ref, bf16[768,512]{1,0:T(8,128)(2,1)} %k_ref.1, ...), custom_call_target="tpu_custom_call" | custom-call | tf_op jit(solution)/shard_map/pallas_call | solution.py:304
  35.2 3.3 %collective-permute-start = (bf16[768,256]{1,0:T(8,128)(2,1)S(1)}, bf16[768,256]{1,0:T(8,128)(2,1)S(1)}, u32[]{:S(2)}, u32[]{:S(2)}) collective-permute-start(bf16[768,256]{1,0:T(8,128)(2,1)S(1)} %get-tuple-element.39), channel_id=1, source_target_pairs={{0,8},{8,0},{1,9},{9,1},{2,10},{10,2},{3,11},{11,3},{4,12},{12,4},... | collective-permute-start | bytes 1179656 | tf_op jit(solution)/shard_map/ppermute | solution.py:39
  40.8 2.0 %collective-permute-start.5 = (bf16[384,256]{1,0:T(8,128)(2,1)S(1)}, bf16[384,256]{1,0:T(8,128)(2,1)S(1)}, u32[]{:S(2)}, u32[]{:S(2)}) collective-permute-start(bf16[384,256]{1,0:T(8,128)(2,1)S(1)} %add_convert_fusion.2), channel_id=1, source_target_pairs={{0,16},{8,56},{16,0},{24,40},{32,48},{40,24},{48,32},{56,8},{1,17}... | collective-permute-start | bytes 589832 | tf_op jit(solution)/shard_map/ppermute | solution.py:39
  42.9 2.9 %collective-permute-done.1 = bf16[384,256]{1,0:T(8,128)(2,1)S(1)} collective-permute-done((bf16[384,256]{1,0:T(8,128)(2,1)S(1)}, bf16[384,256]{1,0:T(8,128)(2,1)S(1)}, u32[]{:S(2)}, u32[]{:S(2)}) %collective-permute-start.1) | collective-permute-done | bytes 196640 | tf_op jit(solution)/shard_map/ppermute | solution.py:39
  45.9 2.0 %collective-permute-done.5 = bf16[384,256]{1,0:T(8,128)(2,1)S(1)} collective-permute-done((bf16[384,256]{1,0:T(8,128)(2,1)S(1)}, bf16[384,256]{1,0:T(8,128)(2,1)S(1)}, u32[]{:S(2)}, u32[]{:S(2)}) %collective-permute-start.5) | collective-permute-done | bytes 196640 | tf_op jit(solution)/shard_map/ppermute | solution.py:39
  48.0 1.3 collective-permute-done.2
  49.4 4.4 %collective-permute-start.3 = (bf16[192,256]{1,0:T(8,128)(2,1)S(1)}, bf16[192,256]{1,0:T(8,128)(2,1)S(1)}, u32[]{:S(2)}, u32[]{:S(2)}) collective-permute-start(bf16[192,256]{1,0:T(8,128)(2,1)S(1)} %add_convert_fusion.14), channel_id=1, source_target_pairs={{0,64},{8,200},{64,0},{72,136},{128,192},{136,72},{192,128},{200,8... | collective-permute-start | bytes 294920 | tf_op jit(solution)/shard_map/ppermute | solution.py:39
  53.8 2.6 %collective-permute-start.7 = (bf16[192,256]{1,0:T(8,128)(2,1)S(1)}, bf16[192,256]{1,0:T(8,128)(2,1)S(1)}, u32[]{:S(2)}, u32[]{:S(2)}) collective-permute-start(bf16[192,256]{1,0:T(8,128)(2,1)S(1)} %add_convert_fusion.11), channel_id=1, source_target_pairs={{0,64},{8,200},{64,0},{72,136},{128,192},{136,72},{192,128},{200,8... | collective-permute-start | bytes 294920 | tf_op jit(solution)/shard_map/ppermute | solution.py:39
  56.4 1.7 %collective-permute-start.8 = (bf16[192,256]{1,0:T(8,128)(2,1)S(1)}, bf16[192,256]{1,0:T(8,128)(2,1)S(1)}, u32[]{:S(2)}, u32[]{:S(2)}) collective-permute-start(bf16[192,256]{1,0:T(8,128)(2,1)S(1)} %add_convert_fusion.13.refs_0_), channel_id=1, source_target_pairs={{0,192},{8,72},{64,128},{72,8},{128,64},{136,200},{192,0},{200,136... | collective-permute-start | bytes 294920 | tf_op jit(solution)/shard_map/ppermute | solution.py:39
  58.2 1.4 collective-permute-done.7
  59.6 2.3 %collective-permute-start.9 = (bf16[192,256]{1,0:T(8,128)(2,1)S(1)}, bf16[192,256]{1,0:T(8,128)(2,1)S(1)}, u32[]{:S(2)}, u32[]{:S(2)}) collective-permute-start(bf16[192,256]{1,0:T(8,128)(2,1)S(1)} %add_convert_fusion.10.refs_1_), channel_id=1, source_target_pairs={{0,192},{8,72},{64,128},{72,8},{128,64},{136,200},{192,0},{200,136... | collective-permute-start | bytes 294920 | tf_op jit(solution)/shard_map/ppermute | solution.py:39
  62.5 2.0 %collective-permute-done.9.refs_3_ = bf16[192,256]{1,0:T(8,128)(2,1)S(1)} collective-permute-done((bf16[192,256]{1,0:T(8,128)(2,1)S(1)}, bf16[192,256]{1,0:T(8,128)(2,1)S(1)}, u32[]{:S(2)}, u32[]{:S(2)}) %collective-permute-start.9) | collective-permute-done | bytes 98336 | tf_op jit(solution)/shard_map/ppermute | solution.py:39
  66.5 15.1 %all-to-all-start = ((f32[64,8,128]{2,1,0:T(8,128)}), f32[64,8,128]{2,1,0:T(8,128)S(1)}, u32[]{:S(2)}, u32[]{:S(2)}) async-start(f32[64,8,128]{2,1,0:T(8,128)} %get-tuple-element.46), calls=%async_computation | async-start | bytes 524288 | tf_op jit(solution)/shard_map/all_to_all | solution.py:63
  81.6 2.9 %collective-permute-start.12 = (bf16[384,512]{1,0:T(8,128)(2,1)S(1)}, bf16[384,512]{1,0:T(8,128)(2,1)S(1)}, u32[]{:S(2)}, u32[]{:S(2)}) collective-permute-start(bf16[384,512]{1,0:T(8,128)(2,1)S(1)} %constant_dynamic-update-slice_fusion.rest_0_), channel_id=1, source_target_pairs={{0,16},{8,56},{16,0},{24,40},{32,48},{40,24},{48,32},{56,8},{1,17}... | collective-permute-start | bytes 1179656 | tf_op jit(solution)/shard_map/ppermute | solution.py:39
  84.5 1.9 %collective-permute-start.10 = (bf16[640,512]{1,0:T(8,128)(2,1)}, bf16[640,512]{1,0:T(8,128)(2,1)S(1)}, u32[]{:S(2)}, u32[]{:S(2)}) collective-permute-start(bf16[640,512]{1,0:T(8,128)(2,1)} %get-tuple-element.44), channel_id=1, source_target_pairs={{0,8},{8,16},{16,24},{24,32},{32,40},{40,48},{48,56},{56,64},{64,7... | collective-permute-start | bytes 1966088 | tf_op jit(solution)/shard_map/ppermute | solution.py:370
  87.2 4.0 %all-to-all-done.square_ref = f32[64,8,128]{2,1,0:T(8,128)S(1)} async-done(((f32[64,8,128]{2,1,0:T(8,128)}), f32[64,8,128]{2,1,0:T(8,128)S(1)}, u32[]{:S(2)}, u32[]{:S(2)}) %all-to-all-start) | async-done | bytes 262176 | tf_op jit(solution)/shard_map/all_to_all | solution.py:63
  92.3 1.6 collective-permute-done.14.rest_3_
  93.9 7.3 %shard_map.97 = (f32[1536,512]{1,0:T(8,128)}, bf16[1536,512]{1,0:T(8,128)(2,1)S(1)}, bf16[768,256]{1,0:T(8,128)(2,1)S(1)}, bf16[768,256]{1,0:T(8,128)(2,1)S(1)},...) custom-call(s32[1]{0:T(128)} %bitcast.1.place_ref, s32[8]{0:T(128)S(1)} %broadcast_multiply_fusion.starts_ref, ...), custom_call_target="tpu_custom_call" | custom-call | tf_op jit(solution)/shard_map/pallas_call | solution.py:304
  103.1 3.6 %collective-permute-start.16 = (bf16[384,256]{1,0:T(8,128)(2,1)S(1)}, bf16[384,256]{1,0:T(8,128)(2,1)S(1)}, u32[]{:S(2)}, u32[]{:S(2)}) collective-permute-start(bf16[384,256]{1,0:T(8,128)(2,1)S(1)} %add_convert_fusion.1), channel_id=1, source_target_pairs={{0,16},{8,56},{16,0},{24,40},{32,48},{40,24},{48,32},{56,8},{1,17}... | collective-permute-start | bytes 589832 | tf_op jit(solution)/shard_map/ppermute | solution.py:39
  107.2 1.9 %collective-permute-start.21 = (bf16[384,512]{1,0:T(8,128)(2,1)S(1)}, bf16[384,512]{1,0:T(8,128)(2,1)S(1)}, u32[]{:S(2)}, u32[]{:S(2)}) collective-permute-start(bf16[384,512]{1,0:T(8,128)(2,1)S(1)} %copy-done.4), channel_id=1, source_target_pairs={{0,8},{8,16},{16,24},{24,32},{32,40},{40,48},{48,56},{56,64},{64,7... | collective-permute-start | bytes 1179656 | tf_op jit(solution)/shard_map/ppermute | solution.py:351
  109.8 1.5 collective-permute-start.17
  112.7 2.7 %collective-permute-done.17 = bf16[192,256]{1,0:T(8,128)(2,1)S(1)} collective-permute-done((bf16[192,256]{1,0:T(8,128)(2,1)S(1)}, bf16[192,256]{1,0:T(8,128)(2,1)S(1)}, u32[]{:S(2)}, u32[]{:S(2)}) %collective-permute-start.17) | collective-permute-done | bytes 98336 | tf_op jit(solution)/shard_map/ppermute | solution.py:39
  115.5 8.9 %collective-permute-start.22 = (bf16[192,256]{1,0:T(8,128)(2,1)S(1)}, bf16[192,256]{1,0:T(8,128)(2,1)S(1)}, u32[]{:S(2)}, u32[]{:S(2)}) collective-permute-start(bf16[192,256]{1,0:T(8,128)(2,1)S(1)} %add_convert_fusion.8), channel_id=1, source_target_pairs={{0,64},{8,200},{64,0},{72,136},{128,192},{136,72},{192,128},{200,8... | collective-permute-start | bytes 294920 | tf_op jit(solution)/shard_map/ppermute | solution.py:39
  125.7 2.8 %shard_map.98.attn_ref = f32[768,512]{1,0:T(8,128)S(1)} custom-call(s32[3]{0:T(128)S(1)} %pad_add_fusion.meta_ref, bf16[768,512]{1,0:T(8,128)(2,1)S(1)} %copy-done.2, bf16[640,512]{1,0:T(8,128)(2,1)S(1)} %collective-permute-done.10.halo_ref, bf16[768,512]{1,0:T(8,128)(2,1)S(1)} %copy-done, bf16[384,512]{1,0:T(8,128)(2,1)S(1)} %collective-permute-done.21.late_v_ref, ...), custom_call_target="tpu_custom_call" | custom-call | tf_op jit(solution)/shard_map/pallas_call | solution.py:304
  128.5 4.8 %collective-permute-done.23 = bf16[192,256]{1,0:T(8,128)(2,1)S(1)} collective-permute-done((bf16[192,256]{1,0:T(8,128)(2,1)S(1)}, bf16[192,256]{1,0:T(8,128)(2,1)S(1)}, u32[]{:S(2)}, u32[]{:S(2)}) %collective-permute-start.23) | collective-permute-done | bytes 98336 | tf_op jit(solution)/shard_map/ppermute | solution.py:39
  133.4 2.4 %collective-permute-start.24 = (bf16[192,256]{1,0:T(8,128)(2,1)S(1)}, bf16[192,256]{1,0:T(8,128)(2,1)S(1)}, u32[]{:S(2)}, u32[]{:S(2)}) collective-permute-start(bf16[192,256]{1,0:T(8,128)(2,1)S(1)} %add_convert_fusion.5.refs_0_), channel_id=1, source_target_pairs={{0,192},{8,72},{64,128},{72,8},{128,64},{136,200},{192,0},{200,136... | collective-permute-start | bytes 294920 | tf_op jit(solution)/shard_map/ppermute | solution.py:39
  135.8 3.9 %shard_map.99 = bf16[768,512]{1,0:T(8,128)(2,1)} custom-call(s32[3]{0:T(128)S(1)} %pad_add_fusion.meta_ref, bf16[768,512]{1,0:T(8,128)(2,1)S(1)} %copy-done.2, f32[768,512]{1,0:T(8,128)S(1)} %shard_map.98.attn_ref, bf16[1536,512]{1,0:T(8,128)(2,1)S(1)} %copy-done.3, bf16[1536,512]{1,0:T(8,128)(2,1)S(1)} %get-tuple-element.65.late_ref), custom_call_target="tpu_custom_call" | custom-call | tf_op jit(solution)/shard_map/pallas_call | solution.py:304
  140.8 13.1 %all-to-all-start.1 = ((f32[64,8,128]{2,1,0:T(8,128)}), f32[64,8,128]{2,1,0:T(8,128)S(1)}, u32[]{:S(2)}, u32[]{:S(2)}) async-start(f32[64,8,128]{2,1,0:T(8,128)} %get-tuple-element.70), calls=%async_computation.1 | async-start | bytes 524288 | tf_op jit(solution)/shard_map/all_to_all | solution.py:63
  153.9 2.9 %collective-permute-start.27 = (bf16[384,512]{1,0:T(8,128)(2,1)S(1)}, bf16[384,512]{1,0:T(8,128)(2,1)S(1)}, u32[]{:S(2)}, u32[]{:S(2)}) collective-permute-start(bf16[384,512]{1,0:T(8,128)(2,1)S(1)} %constant_dynamic-update-slice_fusion.2.rest_0_), channel_id=1, source_target_pairs={{0,16},{8,56},{16,0},{24,40},{32,48},{40,24},{48,32},{56,8},{1,17}... | collective-permute-start | bytes 1179656 | tf_op jit(solution)/shard_map/ppermute | solution.py:39
  156.9 6.7 %all-to-all-done.1.square_ref = f32[64,8,128]{2,1,0:T(8,128)S(1)} async-done(((f32[64,8,128]{2,1,0:T(8,128)}), f32[64,8,128]{2,1,0:T(8,128)S(1)}, u32[]{:S(2)}, u32[]{:S(2)}) %all-to-all-start.1) | async-done | bytes 262176 | tf_op jit(solution)/shard_map/all_to_all | solution.py:63
  164.5 1.7 %collective-permute-done.29.rest_3_ = bf16[384,512]{1,0:T(8,128)(2,1)S(1)} collective-permute-done((bf16[384,512]{1,0:T(8,128)(2,1)S(1)}, bf16[384,512]{1,0:T(8,128)(2,1)S(1)}, u32[]{:S(2)}, u32[]{:S(2)}) %collective-permute-start.29) | collective-permute-done | bytes 393248 | tf_op jit(solution)/shard_map/ppermute | solution.py:39
  166.3 3.4 %shard_map.101 = f32[1536,512]{1,0:T(8,128)} custom-call(s32[8]{0:T(128)S(1)} %broadcast_multiply_fusion.starts_ref, f32[64,8,128]{2,1,0:T(8,128)S(1)} %all-to-all-done.1.square_ref, f32[1536,512]{1,0:T(8,128)} %get-tuple-element.72.w_hbm, bf16[384,512]{1,0:T(8,128)(2,1)S(1)} %constant_dynamic-update-slice_fusion.2.rest_0_, ...), custom_call_target="tpu_custom_call" | custom-call | tf_op jit(solution)/shard_map/pallas_call | solution.py:304
  (74 shorter events, 15.2 us)
Async XLA Ops:
  35.2 4.7 %collective-permute-start = (bf16[768,256]{1,0:T(8,128)(2,1)S(1)}, bf16[768,256]{1,0:T(8,128)(2,1)S(1)}, u32[]{:S(2)}, u32[]{:S(2)}) collective-permute-start(bf16[768,256]{1,0:T(8,128)(2,1)S(1)} %get-tuple-element.39), channel_id=1, source_target_pairs={{0,8},{8,0},{1,9},{9,1},{2,10},{10,2},{3,11},{11,3},{4,12},{12,4},... | collective-permute-start | bytes 1179656 | tf_op jit(solution)/shard_map/ppermute | solution.py:39
  38.6 2.2 %collective-permute-start.4 = (bf16[768,256]{1,0:T(8,128)(2,1)S(1)}, bf16[768,256]{1,0:T(8,128)(2,1)S(1)}, u32[]{:S(2)}, u32[]{:S(2)}) collective-permute-start(bf16[768,256]{1,0:T(8,128)(2,1)S(1)} %get-tuple-element.41), channel_id=1, source_target_pairs={{0,8},{8,0},{1,9},{9,1},{2,10},{10,2},{3,11},{11,3},{4,12},{12,4},... | collective-permute-start | bytes 1179656 | tf_op jit(solution)/shard_map/ppermute | solution.py:39
  40.0 5.8 %collective-permute-start.1 = (bf16[384,256]{1,0:T(8,128)(2,1)S(1)}, bf16[384,256]{1,0:T(8,128)(2,1)S(1)}, u32[]{:S(2)}, u32[]{:S(2)}) collective-permute-start(bf16[384,256]{1,0:T(8,128)(2,1)S(1)} %add_convert_fusion.3), channel_id=1, source_target_pairs={{0,16},{8,56},{16,0},{24,40},{32,48},{40,24},{48,32},{56,8},{1,17}... | collective-permute-start | bytes 589832 | tf_op jit(solution)/shard_map/ppermute | solution.py:39
  40.8 7.0 %collective-permute-start.5 = (bf16[384,256]{1,0:T(8,128)(2,1)S(1)}, bf16[384,256]{1,0:T(8,128)(2,1)S(1)}, u32[]{:S(2)}, u32[]{:S(2)}) collective-permute-start(bf16[384,256]{1,0:T(8,128)(2,1)S(1)} %add_convert_fusion.2), channel_id=1, source_target_pairs={{0,16},{8,56},{16,0},{24,40},{32,48},{40,24},{48,32},{56,8},{1,17}... | collective-permute-start | bytes 589832 | tf_op jit(solution)/shard_map/ppermute | solution.py:39
  45.8 3.6 %collective-permute-start.2 = (bf16[192,256]{1,0:T(8,128)(2,1)S(1)}, bf16[192,256]{1,0:T(8,128)(2,1)S(1)}, u32[]{:S(2)}, u32[]{:S(2)}) collective-permute-start(bf16[192,256]{1,0:T(8,128)(2,1)S(1)} %add_convert_fusion.15), channel_id=1, source_target_pairs={{0,48},{8,24},{16,32},{24,8},{32,16},{40,56},{48,0},{56,40},{1,49}... | collective-permute-start | bytes 294920 | tf_op jit(solution)/shard_map/ppermute | solution.py:39
  47.9 5.9 %collective-permute-start.6 = (bf16[192,256]{1,0:T(8,128)(2,1)S(1)}, bf16[192,256]{1,0:T(8,128)(2,1)S(1)}, u32[]{:S(2)}, u32[]{:S(2)}) collective-permute-start(bf16[192,256]{1,0:T(8,128)(2,1)S(1)} %add_convert_fusion.12), channel_id=1, source_target_pairs={{0,48},{8,24},{16,32},{24,8},{32,16},{40,56},{48,0},{56,40},{1,49}... | collective-permute-start | bytes 294920 | tf_op jit(solution)/shard_map/ppermute | solution.py:39
  49.4 7.0 %collective-permute-start.3 = (bf16[192,256]{1,0:T(8,128)(2,1)S(1)}, bf16[192,256]{1,0:T(8,128)(2,1)S(1)}, u32[]{:S(2)}, u32[]{:S(2)}) collective-permute-start(bf16[192,256]{1,0:T(8,128)(2,1)S(1)} %add_convert_fusion.14), channel_id=1, source_target_pairs={{0,64},{8,200},{64,0},{72,136},{128,192},{136,72},{192,128},{200,8... | collective-permute-start | bytes 294920 | tf_op jit(solution)/shard_map/ppermute | solution.py:39
  53.8 5.8 %collective-permute-start.7 = (bf16[192,256]{1,0:T(8,128)(2,1)S(1)}, bf16[192,256]{1,0:T(8,128)(2,1)S(1)}, u32[]{:S(2)}, u32[]{:S(2)}) collective-permute-start(bf16[192,256]{1,0:T(8,128)(2,1)S(1)} %add_convert_fusion.11), channel_id=1, source_target_pairs={{0,64},{8,200},{64,0},{72,136},{128,192},{136,72},{192,128},{200,8... | collective-permute-start | bytes 294920 | tf_op jit(solution)/shard_map/ppermute | solution.py:39
  56.4 6.1 %collective-permute-start.8 = (bf16[192,256]{1,0:T(8,128)(2,1)S(1)}, bf16[192,256]{1,0:T(8,128)(2,1)S(1)}, u32[]{:S(2)}, u32[]{:S(2)}) collective-permute-start(bf16[192,256]{1,0:T(8,128)(2,1)S(1)} %add_convert_fusion.13.refs_0_), channel_id=1, source_target_pairs={{0,192},{8,72},{64,128},{72,8},{128,64},{136,200},{192,0},{200,136... | collective-permute-start | bytes 294920 | tf_op jit(solution)/shard_map/ppermute | solution.py:39
  59.6 4.9 %collective-permute-start.9 = (bf16[192,256]{1,0:T(8,128)(2,1)S(1)}, bf16[192,256]{1,0:T(8,128)(2,1)S(1)}, u32[]{:S(2)}, u32[]{:S(2)}) collective-permute-start(bf16[192,256]{1,0:T(8,128)(2,1)S(1)} %add_convert_fusion.10.refs_1_), channel_id=1, source_target_pairs={{0,192},{8,72},{64,128},{72,8},{128,64},{136,200},{192,0},{200,136... | collective-permute-start | bytes 294920 | tf_op jit(solution)/shard_map/ppermute | solution.py:39
  65.5 16.1 %collective-permute-start.11 = (bf16[192,512]{1,0:T(8,128)(2,1)S(1)}, bf16[192,512]{1,0:T(8,128)(2,1)S(1)}, u32[]{:S(2)}, u32[]{:S(2)}) collective-permute-start(bf16[192,512]{1,0:T(8,128)(2,1)S(1)} %get-tuple-element.45), channel_id=1, source_target_pairs={{0,48},{8,24},{16,32},{24,8},{32,16},{40,56},{48,0},{56,40},{1,49}... | collective-permute-start | bytes 589832 | tf_op jit(solution)/shard_map/ppermute | solution.py:39
  66.5 24.8 %all-to-all-start = ((f32[64,8,128]{2,1,0:T(8,128)}), f32[64,8,128]{2,1,0:T(8,128)S(1)}, u32[]{:S(2)}, u32[]{:S(2)}) async-start(f32[64,8,128]{2,1,0:T(8,128)} %get-tuple-element.46), calls=%async_computation | async-start | bytes 524288 | tf_op jit(solution)/shard_map/all_to_all | solution.py:63
  81.6 10.6 %collective-permute-start.12 = (bf16[384,512]{1,0:T(8,128)(2,1)S(1)}, bf16[384,512]{1,0:T(8,128)(2,1)S(1)}, u32[]{:S(2)}, u32[]{:S(2)}) collective-permute-start(bf16[384,512]{1,0:T(8,128)(2,1)S(1)} %constant_dynamic-update-slice_fusion.rest_0_), channel_id=1, source_target_pairs={{0,16},{8,56},{16,0},{24,40},{32,48},{40,24},{48,32},{56,8},{1,17}... | collective-permute-start | bytes 1179656 | tf_op jit(solution)/shard_map/ppermute | solution.py:39
  84.5 16.7 %collective-permute-start.10 = (bf16[640,512]{1,0:T(8,128)(2,1)}, bf16[640,512]{1,0:T(8,128)(2,1)S(1)}, u32[]{:S(2)}, u32[]{:S(2)}) collective-permute-start(bf16[640,512]{1,0:T(8,128)(2,1)} %get-tuple-element.44), channel_id=1, source_target_pairs={{0,8},{8,16},{16,24},{24,32},{32,40},{40,48},{48,56},{56,64},{64,7... | collective-permute-start | bytes 1966088 | tf_op jit(solution)/shard_map/ppermute | solution.py:370
  86.4 5.9 %collective-permute-start.13 = (bf16[384,512]{1,0:T(8,128)(2,1)S(1)}, bf16[384,512]{1,0:T(8,128)(2,1)S(1)}, u32[]{:S(2)}, u32[]{:S(2)}) collective-permute-start(bf16[384,512]{1,0:T(8,128)(2,1)S(1)} %constant_dynamic-update-slice_fusion.rest_0_), channel_id=1, source_target_pairs={{0,8},{8,0},{1,9},{9,1},{2,10},{10,2},{3,11},{11,3},{4,12},{12,4},... | collective-permute-start | bytes 1179656 | tf_op jit(solution)/shard_map/ppermute | solution.py:39
  92.2 1.7 %collective-permute-start.14 = (bf16[384,512]{1,0:T(8,128)(2,1)S(1)}, bf16[384,512]{1,0:T(8,128)(2,1)S(1)}, u32[]{:S(2)}, u32[]{:S(2)}) collective-permute-start(bf16[384,512]{1,0:T(8,128)(2,1)S(1)} %collective-permute-done.12.rest_1_), channel_id=1, source_target_pairs={{0,8},{8,0},{1,9},{9,1},{2,10},{10,2},{3,11},{11,3},{4,12},{12,4},... | collective-permute-start | bytes 1179656 | tf_op jit(solution)/shard_map/ppermute | solution.py:39
  101.2 1.8 %collective-permute-start.15 = (bf16[768,256]{1,0:T(8,128)(2,1)S(1)}, bf16[768,256]{1,0:T(8,128)(2,1)S(1)}, u32[]{:S(2)}, u32[]{:S(2)}) collective-permute-start(bf16[768,256]{1,0:T(8,128)(2,1)S(1)} %get-tuple-element.54), channel_id=1, source_target_pairs={{0,8},{8,0},{1,9},{9,1},{2,10},{10,2},{3,11},{11,3},{4,12},{12,4},... | collective-permute-start | bytes 1179656 | tf_op jit(solution)/shard_map/ppermute | solution.py:39
  101.4 5.2 %collective-permute-start.18 = (bf16[768,256]{1,0:T(8,128)(2,1)S(1)}, bf16[768,256]{1,0:T(8,128)(2,1)S(1)}, u32[]{:S(2)}, u32[]{:S(2)}) collective-permute-start(bf16[768,256]{1,0:T(8,128)(2,1)S(1)} %get-tuple-element.56), channel_id=1, source_target_pairs={{0,8},{8,0},{1,9},{9,1},{2,10},{10,2},{3,11},{11,3},{4,12},{12,4},... | collective-permute-start | bytes 1179656 | tf_op jit(solution)/shard_map/ppermute | solution.py:39
  103.1 6.7 %collective-permute-start.16 = (bf16[384,256]{1,0:T(8,128)(2,1)S(1)}, bf16[384,256]{1,0:T(8,128)(2,1)S(1)}, u32[]{:S(2)}, u32[]{:S(2)}) collective-permute-start(bf16[384,256]{1,0:T(8,128)(2,1)S(1)} %add_convert_fusion.1), channel_id=1, source_target_pairs={{0,16},{8,56},{16,0},{24,40},{32,48},{40,24},{48,32},{56,8},{1,17}... | collective-permute-start | bytes 589832 | tf_op jit(solution)/shard_map/ppermute | solution.py:39
  106.7 5.8 %collective-permute-start.19 = (bf16[384,256]{1,0:T(8,128)(2,1)S(1)}, bf16[384,256]{1,0:T(8,128)(2,1)S(1)}, u32[]{:S(2)}, u32[]{:S(2)}) collective-permute-start(bf16[384,256]{1,0:T(8,128)(2,1)S(1)} %add_convert_fusion), channel_id=1, source_target_pairs={{0,16},{8,56},{16,0},{24,40},{32,48},{40,24},{48,32},{56,8},{1,17}... | collective-permute-start | bytes 589832 | tf_op jit(solution)/shard_map/ppermute | solution.py:39
  107.2 18.5 %collective-permute-start.21 = (bf16[384,512]{1,0:T(8,128)(2,1)S(1)}, bf16[384,512]{1,0:T(8,128)(2,1)S(1)}, u32[]{:S(2)}, u32[]{:S(2)}) collective-permute-start(bf16[384,512]{1,0:T(8,128)(2,1)S(1)} %copy-done.4), channel_id=1, source_target_pairs={{0,8},{8,16},{16,24},{24,32},{32,40},{40,48},{48,56},{56,64},{64,7... | collective-permute-start | bytes 1179656 | tf_op jit(solution)/shard_map/ppermute | solution.py:351
  109.8 5.5 %collective-permute-start.17 = (bf16[192,256]{1,0:T(8,128)(2,1)S(1)}, bf16[192,256]{1,0:T(8,128)(2,1)S(1)}, u32[]{:S(2)}, u32[]{:S(2)}) collective-permute-start(bf16[192,256]{1,0:T(8,128)(2,1)S(1)} %add_convert_fusion.9), channel_id=1, source_target_pairs={{0,48},{8,24},{16,32},{24,8},{32,16},{40,56},{48,0},{56,40},{1,49}... | collective-permute-start | bytes 294920 | tf_op jit(solution)/shard_map/ppermute | solution.py:39
  112.6 11.8 %collective-permute-start.20 = (bf16[192,256]{1,0:T(8,128)(2,1)S(1)}, bf16[192,256]{1,0:T(8,128)(2,1)S(1)}, u32[]{:S(2)}, u32[]{:S(2)}) collective-permute-start(bf16[192,256]{1,0:T(8,128)(2,1)S(1)} %add_convert_fusion.7), channel_id=1, source_target_pairs={{0,48},{8,24},{16,32},{24,8},{32,16},{40,56},{48,0},{56,40},{1,49}... | collective-permute-start | bytes 294920 | tf_op jit(solution)/shard_map/ppermute | solution.py:39
  115.5 13.0 %collective-permute-start.22 = (bf16[192,256]{1,0:T(8,128)(2,1)S(1)}, bf16[192,256]{1,0:T(8,128)(2,1)S(1)}, u32[]{:S(2)}, u32[]{:S(2)}) collective-permute-start(bf16[192,256]{1,0:T(8,128)(2,1)S(1)} %add_convert_fusion.8), channel_id=1, source_target_pairs={{0,64},{8,200},{64,0},{72,136},{128,192},{136,72},{192,128},{200,8... | collective-permute-start | bytes 294920 | tf_op jit(solution)/shard_map/ppermute | solution.py:39
  124.5 8.8 %collective-permute-start.23 = (bf16[192,256]{1,0:T(8,128)(2,1)S(1)}, bf16[192,256]{1,0:T(8,128)(2,1)S(1)}, u32[]{:S(2)}, u32[]{:S(2)}) collective-permute-start(bf16[192,256]{1,0:T(8,128)(2,1)S(1)} %add_convert_fusion.6), channel_id=1, source_target_pairs={{0,64},{8,200},{64,0},{72,136},{128,192},{136,72},{192,128},{200,8... | collective-permute-start | bytes 294920 | tf_op jit(solution)/shard_map/ppermute | solution.py:39
  133.3 6.4 %collective-permute-start.25 = (bf16[192,256]{1,0:T(8,128)(2,1)S(1)}, bf16[192,256]{1,0:T(8,128)(2,1)S(1)}, u32[]{:S(2)}, u32[]{:S(2)}) collective-permute-start(bf16[192,256]{1,0:T(8,128)(2,1)S(1)} %add_convert_fusion.4.refs_1_), channel_id=1, source_target_pairs={{0,192},{8,72},{64,128},{72,8},{128,64},{136,200},{192,0},{200,136... | collective-permute-start | bytes 294920 | tf_op jit(solution)/shard_map/ppermute | solution.py:39
  133.4 6.3 %collective-permute-start.24 = (bf16[192,256]{1,0:T(8,128)(2,1)S(1)}, bf16[192,256]{1,0:T(8,128)(2,1)S(1)}, u32[]{:S(2)}, u32[]{:S(2)}) collective-permute-start(bf16[192,256]{1,0:T(8,128)(2,1)S(1)} %add_convert_fusion.5.refs_0_), channel_id=1, source_target_pairs={{0,192},{8,72},{64,128},{72,8},{128,64},{136,200},{192,0},{200,136... | collective-permute-start | bytes 294920 | tf_op jit(solution)/shard_map/ppermute | solution.py:39
  140.6 13.3 %collective-permute-start.26 = (bf16[192,512]{1,0:T(8,128)(2,1)S(1)}, bf16[192,512]{1,0:T(8,128)(2,1)S(1)}, u32[]{:S(2)}, u32[]{:S(2)}) collective-permute-start(bf16[192,512]{1,0:T(8,128)(2,1)S(1)} %get-tuple-element.69), channel_id=1, source_target_pairs={{0,48},{8,24},{16,32},{24,8},{32,16},{40,56},{48,0},{56,40},{1,49}... | collective-permute-start | bytes 589832 | tf_op jit(solution)/shard_map/ppermute | solution.py:39
  140.8 22.9 %all-to-all-start.1 = ((f32[64,8,128]{2,1,0:T(8,128)}), f32[64,8,128]{2,1,0:T(8,128)S(1)}, u32[]{:S(2)}, u32[]{:S(2)}) async-start(f32[64,8,128]{2,1,0:T(8,128)} %get-tuple-element.70), calls=%async_computation.1 | async-start | bytes 524288 | tf_op jit(solution)/shard_map/all_to_all | solution.py:63
  153.9 10.6 %collective-permute-start.27 = (bf16[384,512]{1,0:T(8,128)(2,1)S(1)}, bf16[384,512]{1,0:T(8,128)(2,1)S(1)}, u32[]{:S(2)}, u32[]{:S(2)}) collective-permute-start(bf16[384,512]{1,0:T(8,128)(2,1)S(1)} %constant_dynamic-update-slice_fusion.2.rest_0_), channel_id=1, source_target_pairs={{0,16},{8,56},{16,0},{24,40},{32,48},{40,24},{48,32},{56,8},{1,17}... | collective-permute-start | bytes 1179656 | tf_op jit(solution)/shard_map/ppermute | solution.py:39
  156.9 7.7 %collective-permute-start.28 = (bf16[384,512]{1,0:T(8,128)(2,1)S(1)}, bf16[384,512]{1,0:T(8,128)(2,1)S(1)}, u32[]{:S(2)}, u32[]{:S(2)}) collective-permute-start(bf16[384,512]{1,0:T(8,128)(2,1)S(1)} %constant_dynamic-update-slice_fusion.2.rest_0_), channel_id=1, source_target_pairs={{0,8},{8,0},{1,9},{9,1},{2,10},{10,2},{3,11},{11,3},{4,12},{12,4},... | collective-permute-start | bytes 1179656 | tf_op jit(solution)/shard_map/ppermute | solution.py:39
  164.5 1.7 %collective-permute-start.29 = (bf16[384,512]{1,0:T(8,128)(2,1)S(1)}, bf16[384,512]{1,0:T(8,128)(2,1)S(1)}, u32[]{:S(2)}, u32[]{:S(2)}) collective-permute-start(bf16[384,512]{1,0:T(8,128)(2,1)S(1)} %collective-permute-done.27.rest_1_), channel_id=1, source_target_pairs={{0,8},{8,0},{1,9},{9,1},{2,10},{10,2},{3,11},{11,3},{4,12},{12,4},... | collective-permute-start | bytes 1179656 | tf_op jit(solution)/shard_map/ppermute | solution.py:39
  (5 other events, 107.3 us)

commit v6 on v5

--- a/solution.py
+++ b/solution.py
@@ -162,7 +162,7 @@
 
 
 def first_kernel(place_ref, keys_hbm, targets_hbm, values_hbm, rate_ref, w_hbm, wb_hbm, mid_hbm, late_hbm, *rest):
-    outs, (grad_ref, keys_ref, targets_ref, w_ref, wb_ref, sem) = rest[: 2 * CHUNKS], rest[2 * CHUNKS :]
+    outs, (grad_ref, keys_ref, targets_ref, w_ref, wb_ref, tail_ref, sem) = rest[: 2 * CHUNKS], rest[2 * CHUNKS :]
     thirds = [pl.ds(i * HD, HD) for i in range(3)]
     copies = fetch(
         [w_hbm.at[t] for t in thirds] + [keys_hbm, targets_hbm],
@@ -170,14 +170,14 @@
         sem,
     )
     tail = keys_hbm.shape[0] - WIN
+    tail_copy = pltpu.make_async_copy(values_hbm.at[pl.ds(tail, WIN)], tail_ref, sem.at[9])
+    tail_copy.start()
     tails = [
-        (keys_hbm.at[pl.ds(tail, WIN)], mid_hbm.at[pl.ds(0, WIN)]),
-        (values_hbm.at[pl.ds(tail, EARLY)], mid_hbm.at[pl.ds(WIN, EARLY)]),
-        (values_hbm.at[pl.ds(tail + EARLY, WIN - EARLY)], late_hbm),
+        (keys_ref.at[pl.ds(tail, WIN)], mid_hbm.at[pl.ds(0, WIN)]),
+        (tail_ref.at[pl.ds(0, EARLY)], mid_hbm.at[pl.ds(WIN, EARLY)]),
+        (tail_ref.at[pl.ds(EARLY, WIN - EARLY)], late_hbm),
     ]
     moves = [pltpu.make_async_copy(a, b, sem.at[6 + i]) for i, (a, b) in enumerate(tails)]
-    for move in moves:
-        move.start()
     for copy, third in zip(copies, thirds):
         copy.wait()
         wb_ref[third] = w_ref[third].astype(bf16)
@@ -185,6 +185,9 @@
     leave.start()
     copies[3].wait()
     copies[4].wait()
+    tail_copy.wait()
+    for move in moves:
+        move.start()
     grads(place_ref[0], keys_ref, targets_ref, rate_ref, wb_ref, grad_ref, outs)
     leave.wait()
     for move in moves:
@@ -345,7 +348,7 @@
         [pltpu.HBM((ROWS, HID), bf16), pltpu.HBM((WIN + EARLY, HD), bf16), pltpu.HBM((WIN - EARLY, HD), bf16)] + wide,
         (core, in_hbm(keys), in_hbm(targets), in_hbm(values), rate_zero, in_hbm(weights_zero)),
         24,
-        [grad] + fetched + [pltpu.VMEM((ROWS, HID), f32), pltpu.VMEM((ROWS, HID), bf16), pltpu.SemaphoreType.DMA((9,))],
+        [grad] + fetched + [pltpu.VMEM((ROWS, HID), f32), pltpu.VMEM((ROWS, HID), bf16), pltpu.VMEM((WIN, HD), bf16), pltpu.SemaphoreType.DMA((10,))],
         [HBM_SPEC] * 3 + [VMEM_SPEC] * (2 * CHUNKS),
     )
     halo_v = lax.ppermute(late, SEQ, onward)

time: 170 us -> 143 us (0.84)
  Pallas kernels: 52.1 us -> 25.1 us
    pallas_call x7, Pallas kernels: 52.1 us -> 25.1 us  [call(): pl.pallas_call(kernel, out_shape=outs, in_specs=specs, out_specs=jax.tree...]
  transfers between devices with their start and end apart: 32 -> 32, of which waited for: 17 -> 17; matrix products, arithmetic and copies ran while one was open for 0% -> 1% of each run, Pallas kernels for 8% -> 10%
where the time goes in v6:
time: 143 us
  starting transfers between devices  76 us (53%)
  waiting for transfers between devices  37.4 us (26%)
  Pallas kernels  25.1 us (18%)
  between operations  2.46 us (2%)
    ppermute x28, starting transfers between devices, exchange(): lax.ppermute(value, mesh_axes, [(i, partner(i)) for i in range(count)])  43.9 us
    all_to_all x2, starting transfers between devices, spread(): return lax.all_to_all(squares, ('x', 'core', 'head'), 0, 0, tiled=True)  28.3 us
    ppermute x28, waiting for transfers between devices, exchange(): lax.ppermute(value, mesh_axes, [(i, partner(i)) for i in range(count)])  26.7 us
    pallas_call x7, Pallas kernels, call(): pl.pallas_call(kernel, out_shape=outs, in_specs=specs, out_specs=jax.tree...  25.1 us
    all_to_all x2, waiting for transfers between devices, spread(): return lax.all_to_all(squares, ('x', 'core', 'head'), 0, 0, tiled=True)  10.8 us
  transfers between devices with their start and end apart: 32, of which 17 were waited for; matrix products, arithmetic and copies ran while one was open for 1% of the time, Pallas kernels for 10%

profile of v6, /device:TPU:1, one launch (start us, length us, event | category | flops | bytes accessed | tf_op | source)
XLA Modules:
  0.0 142.9 jit_solution(5875532212230290159)
XLA Ops:
  2.3 6.0 %shard_map.95 = (bf16[1536,512]{1,0:T(8,128)(2,1)}, bf16[640,512]{1,0:T(8,128)(2,1)}, bf16[384,512]{1,0:T(8,128)(2,1)}, bf16[768,256]{1,0:T(8,128)(2,1)S(1)}, bf...) custom-call(s32[1]{0:T(128)} %bitcast.1.place_ref, bf16[768,512]{1,0:T(8,128)(2,1)} %k_ref.1, ...), custom_call_target="tpu_custom_call" | custom-call | tf_op jit(solution)/shard_map/pallas_call | solution.py:307
  8.2 3.3 %collective-permute-start = (bf16[768,256]{1,0:T(8,128)(2,1)S(1)}, bf16[768,256]{1,0:T(8,128)(2,1)S(1)}, u32[]{:S(2)}, u32[]{:S(2)}) collective-permute-start(bf16[768,256]{1,0:T(8,128)(2,1)S(1)} %get-tuple-element.39), channel_id=1, source_target_pairs={{0,8},{8,0},{1,9},{9,1},{2,10},{10,2},{3,11},{11,3},{4,12},{12,4},... | collective-permute-start | bytes 1179656 | tf_op jit(solution)/shard_map/ppermute | solution.py:39
  13.8 2.0 %collective-permute-start.5 = (bf16[384,256]{1,0:T(8,128)(2,1)S(1)}, bf16[384,256]{1,0:T(8,128)(2,1)S(1)}, u32[]{:S(2)}, u32[]{:S(2)}) collective-permute-start(bf16[384,256]{1,0:T(8,128)(2,1)S(1)} %add_convert_fusion.2), channel_id=1, source_target_pairs={{0,16},{8,56},{16,0},{24,40},{32,48},{40,24},{48,32},{56,8},{1,17}... | collective-permute-start | bytes 589832 | tf_op jit(solution)/shard_map/ppermute | solution.py:39
  15.9 2.9 %collective-permute-done.1 = bf16[384,256]{1,0:T(8,128)(2,1)S(1)} collective-permute-done((bf16[384,256]{1,0:T(8,128)(2,1)S(1)}, bf16[384,256]{1,0:T(8,128)(2,1)S(1)}, u32[]{:S(2)}, u32[]{:S(2)}) %collective-permute-start.1) | collective-permute-done | bytes 196640 | tf_op jit(solution)/shard_map/ppermute | solution.py:39
  18.9 2.0 %collective-permute-done.5 = bf16[384,256]{1,0:T(8,128)(2,1)S(1)} collective-permute-done((bf16[384,256]{1,0:T(8,128)(2,1)S(1)}, bf16[384,256]{1,0:T(8,128)(2,1)S(1)}, u32[]{:S(2)}, u32[]{:S(2)}) %collective-permute-start.5) | collective-permute-done | bytes 196640 | tf_op jit(solution)/shard_map/ppermute | solution.py:39
  21.0 1.3 collective-permute-done.2
  22.4 4.4 %collective-permute-start.3 = (bf16[192,256]{1,0:T(8,128)(2,1)S(1)}, bf16[192,256]{1,0:T(8,128)(2,1)S(1)}, u32[]{:S(2)}, u32[]{:S(2)}) collective-permute-start(bf16[192,256]{1,0:T(8,128)(2,1)S(1)} %add_convert_fusion.14), channel_id=1, source_target_pairs={{0,64},{8,200},{64,0},{72,136},{128,192},{136,72},{192,128},{200,8... | collective-permute-start | bytes 294920 | tf_op jit(solution)/shard_map/ppermute | solution.py:39
  26.8 2.6 %collective-permute-start.7 = (bf16[192,256]{1,0:T(8,128)(2,1)S(1)}, bf16[192,256]{1,0:T(8,128)(2,1)S(1)}, u32[]{:S(2)}, u32[]{:S(2)}) collective-permute-start(bf16[192,256]{1,0:T(8,128)(2,1)S(1)} %add_convert_fusion.11), channel_id=1, source_target_pairs={{0,64},{8,200},{64,0},{72,136},{128,192},{136,72},{192,128},{200,8... | collective-permute-start | bytes 294920 | tf_op jit(solution)/shard_map/ppermute | solution.py:39
  29.4 1.7 %collective-permute-start.8 = (bf16[192,256]{1,0:T(8,128)(2,1)S(1)}, bf16[192,256]{1,0:T(8,128)(2,1)S(1)}, u32[]{:S(2)}, u32[]{:S(2)}) collective-permute-start(bf16[192,256]{1,0:T(8,128)(2,1)S(1)} %add_convert_fusion.13.refs_0_), channel_id=1, source_target_pairs={{0,192},{8,72},{64,128},{72,8},{128,64},{136,200},{192,0},{200,136... | collective-permute-start | bytes 294920 | tf_op jit(solution)/shard_map/ppermute | solution.py:39
  31.2 1.4 %collective-permute-done.7 = bf16[192,256]{1,0:T(8,128)(2,1)S(1)} collective-permute-done((bf16[192,256]{1,0:T(8,128)(2,1)S(1)}, bf16[192,256]{1,0:T(8,128)(2,1)S(1)}, u32[]{:S(2)}, u32[]{:S(2)}) %collective-permute-start.7) | collective-permute-done | bytes 98336 | tf_op jit(solution)/shard_map/ppermute | solution.py:39
  32.6 2.3 %collective-permute-start.9 = (bf16[192,256]{1,0:T(8,128)(2,1)S(1)}, bf16[192,256]{1,0:T(8,128)(2,1)S(1)}, u32[]{:S(2)}, u32[]{:S(2)}) collective-permute-start(bf16[192,256]{1,0:T(8,128)(2,1)S(1)} %add_convert_fusion.10.refs_1_), channel_id=1, source_target_pairs={{0,192},{8,72},{64,128},{72,8},{128,64},{136,200},{192,0},{200,136... | collective-permute-start | bytes 294920 | tf_op jit(solution)/shard_map/ppermute | solution.py:39
  35.5 2.0 %collective-permute-done.9.refs_3_ = bf16[192,256]{1,0:T(8,128)(2,1)S(1)} collective-permute-done((bf16[192,256]{1,0:T(8,128)(2,1)S(1)}, bf16[192,256]{1,0:T(8,128)(2,1)S(1)}, u32[]{:S(2)}, u32[]{:S(2)}) %collective-permute-start.9) | collective-permute-done | bytes 98336 | tf_op jit(solution)/shard_map/ppermute | solution.py:39
  39.5 15.1 %all-to-all-start = ((f32[64,8,128]{2,1,0:T(8,128)}), f32[64,8,128]{2,1,0:T(8,128)S(1)}, u32[]{:S(2)}, u32[]{:S(2)}) async-start(f32[64,8,128]{2,1,0:T(8,128)} %get-tuple-element.46), calls=%async_computation | async-start | bytes 524288 | tf_op jit(solution)/shard_map/all_to_all | solution.py:63
  54.6 2.9 %collective-permute-start.12 = (bf16[384,512]{1,0:T(8,128)(2,1)S(1)}, bf16[384,512]{1,0:T(8,128)(2,1)S(1)}, u32[]{:S(2)}, u32[]{:S(2)}) collective-permute-start(bf16[384,512]{1,0:T(8,128)(2,1)S(1)} %constant_dynamic-update-slice_fusion.rest_0_), channel_id=1, source_target_pairs={{0,16},{8,56},{16,0},{24,40},{32,48},{40,24},{48,32},{56,8},{1,17}... | collective-permute-start | bytes 1179656 | tf_op jit(solution)/shard_map/ppermute | solution.py:39
  57.5 1.9 %collective-permute-start.10 = (bf16[640,512]{1,0:T(8,128)(2,1)}, bf16[640,512]{1,0:T(8,128)(2,1)S(1)}, u32[]{:S(2)}, u32[]{:S(2)}) collective-permute-start(bf16[640,512]{1,0:T(8,128)(2,1)} %get-tuple-element.44), channel_id=1, source_target_pairs={{0,8},{8,16},{16,24},{24,32},{32,40},{40,48},{48,56},{56,64},{64,7... | collective-permute-start | bytes 1966088 | tf_op jit(solution)/shard_map/ppermute | solution.py:373
  60.2 4.0 %all-to-all-done.square_ref = f32[64,8,128]{2,1,0:T(8,128)S(1)} async-done(((f32[64,8,128]{2,1,0:T(8,128)}), f32[64,8,128]{2,1,0:T(8,128)S(1)}, u32[]{:S(2)}, u32[]{:S(2)}) %all-to-all-start) | async-done | bytes 262176 | tf_op jit(solution)/shard_map/all_to_all | solution.py:63
  65.3 1.6 %collective-permute-done.14.rest_3_ = bf16[384,512]{1,0:T(8,128)(2,1)S(1)} collective-permute-done((bf16[384,512]{1,0:T(8,128)(2,1)S(1)}, bf16[384,512]{1,0:T(8,128)(2,1)S(1)}, u32[]{:S(2)}, u32[]{:S(2)}) %collective-permute-start.14) | collective-permute-done | bytes 393248 | tf_op jit(solution)/shard_map/ppermute | solution.py:39
  66.9 7.3 %shard_map.97 = (f32[1536,512]{1,0:T(8,128)}, bf16[1536,512]{1,0:T(8,128)(2,1)S(1)}, bf16[768,256]{1,0:T(8,128)(2,1)S(1)}, bf16[768,256]{1,0:T(8,128)(2,1)S(1)},...) custom-call(s32[1]{0:T(128)} %bitcast.1.place_ref, s32[8]{0:T(128)S(1)} %broadcast_multiply_fusion.starts_ref, ...), custom_call_target="tpu_custom_call" | custom-call | tf_op jit(solution)/shard_map/pallas_call | solution.py:307
  76.1 3.6 %collective-permute-start.16 = (bf16[384,256]{1,0:T(8,128)(2,1)S(1)}, bf16[384,256]{1,0:T(8,128)(2,1)S(1)}, u32[]{:S(2)}, u32[]{:S(2)}) collective-permute-start(bf16[384,256]{1,0:T(8,128)(2,1)S(1)} %add_convert_fusion.1), channel_id=1, source_target_pairs={{0,16},{8,56},{16,0},{24,40},{32,48},{40,24},{48,32},{56,8},{1,17}... | collective-permute-start | bytes 589832 | tf_op jit(solution)/shard_map/ppermute | solution.py:39
  80.2 1.9 %collective-permute-start.21 = (bf16[384,512]{1,0:T(8,128)(2,1)S(1)}, bf16[384,512]{1,0:T(8,128)(2,1)S(1)}, u32[]{:S(2)}, u32[]{:S(2)}) collective-permute-start(bf16[384,512]{1,0:T(8,128)(2,1)S(1)} %copy-done.4), channel_id=1, source_target_pairs={{0,8},{8,16},{16,24},{24,32},{32,40},{40,48},{48,56},{56,64},{64,7... | collective-permute-start | bytes 1179656 | tf_op jit(solution)/shard_map/ppermute | solution.py:354
  82.9 1.5 %collective-permute-start.17 = (bf16[192,256]{1,0:T(8,128)(2,1)S(1)}, bf16[192,256]{1,0:T(8,128)(2,1)S(1)}, u32[]{:S(2)}, u32[]{:S(2)}) collective-permute-start(bf16[192,256]{1,0:T(8,128)(2,1)S(1)} %add_convert_fusion.9), channel_id=1, source_target_pairs={{0,48},{8,24},{16,32},{24,8},{32,16},{40,56},{48,0},{56,40},{1,49}... | collective-permute-start | bytes 294920 | tf_op jit(solution)/shard_map/ppermute | solution.py:39
  85.7 2.7 %collective-permute-done.17 = bf16[192,256]{1,0:T(8,128)(2,1)S(1)} collective-permute-done((bf16[192,256]{1,0:T(8,128)(2,1)S(1)}, bf16[192,256]{1,0:T(8,128)(2,1)S(1)}, u32[]{:S(2)}, u32[]{:S(2)}) %collective-permute-start.17) | collective-permute-done | bytes 98336 | tf_op jit(solution)/shard_map/ppermute | solution.py:39
  88.5 8.9 %collective-permute-start.22 = (bf16[192,256]{1,0:T(8,128)(2,1)S(1)}, bf16[192,256]{1,0:T(8,128)(2,1)S(1)}, u32[]{:S(2)}, u32[]{:S(2)}) collective-permute-start(bf16[192,256]{1,0:T(8,128)(2,1)S(1)} %add_convert_fusion.8), channel_id=1, source_target_pairs={{0,64},{8,200},{64,0},{72,136},{128,192},{136,72},{192,128},{200,8... | collective-permute-start | bytes 294920 | tf_op jit(solution)/shard_map/ppermute | solution.py:39
  98.7 2.8 %shard_map.98.attn_ref = f32[768,512]{1,0:T(8,128)S(1)} custom-call(s32[3]{0:T(128)S(1)} %pad_add_fusion.meta_ref, bf16[768,512]{1,0:T(8,128)(2,1)S(1)} %copy-done.2, bf16[640,512]{1,0:T(8,128)(2,1)S(1)} %collective-permute-done.10.halo_ref, bf16[768,512]{1,0:T(8,128)(2,1)S(1)} %copy-done, bf16[384,512]{1,0:T(8,128)(2,1)S(1)} %collective-permute-done.21.late_v_ref, ...), custom_call_target="tpu_custom_call" | custom-call | tf_op jit(solution)/shard_map/pallas_call | solution.py:307
  101.5 4.8 %collective-permute-done.23 = bf16[192,256]{1,0:T(8,128)(2,1)S(1)} collective-permute-done((bf16[192,256]{1,0:T(8,128)(2,1)S(1)}, bf16[192,256]{1,0:T(8,128)(2,1)S(1)}, u32[]{:S(2)}, u32[]{:S(2)}) %collective-permute-start.23) | collective-permute-done | bytes 98336 | tf_op jit(solution)/shard_map/ppermute | solution.py:39
  106.4 2.4 %collective-permute-start.24 = (bf16[192,256]{1,0:T(8,128)(2,1)S(1)}, bf16[192,256]{1,0:T(8,128)(2,1)S(1)}, u32[]{:S(2)}, u32[]{:S(2)}) collective-permute-start(bf16[192,256]{1,0:T(8,128)(2,1)S(1)} %add_convert_fusion.5.refs_0_), channel_id=1, source_target_pairs={{0,192},{8,72},{64,128},{72,8},{128,64},{136,200},{192,0},{200,136... | collective-permute-start | bytes 294920 | tf_op jit(solution)/shard_map/ppermute | solution.py:39
  108.8 3.9 %shard_map.99 = bf16[768,512]{1,0:T(8,128)(2,1)} custom-call(s32[3]{0:T(128)S(1)} %pad_add_fusion.meta_ref, bf16[768,512]{1,0:T(8,128)(2,1)S(1)} %copy-done.2, f32[768,512]{1,0:T(8,128)S(1)} %shard_map.98.attn_ref, bf16[1536,512]{1,0:T(8,128)(2,1)S(1)} %copy-done.3, bf16[1536,512]{1,0:T(8,128)(2,1)S(1)} %get-tuple-element.65.late_ref), custom_call_target="tpu_custom_call" | custom-call | tf_op jit(solution)/shard_map/pallas_call | solution.py:307
  113.8 13.2 %all-to-all-start.1 = ((f32[64,8,128]{2,1,0:T(8,128)}), f32[64,8,128]{2,1,0:T(8,128)S(1)}, u32[]{:S(2)}, u32[]{:S(2)}) async-start(f32[64,8,128]{2,1,0:T(8,128)} %get-tuple-element.70), calls=%async_computation.1 | async-start | bytes 524288 | tf_op jit(solution)/shard_map/all_to_all | solution.py:63
  127.0 2.9 %collective-permute-start.27 = (bf16[384,512]{1,0:T(8,128)(2,1)S(1)}, bf16[384,512]{1,0:T(8,128)(2,1)S(1)}, u32[]{:S(2)}, u32[]{:S(2)}) collective-permute-start(bf16[384,512]{1,0:T(8,128)(2,1)S(1)} %constant_dynamic-update-slice_fusion.2.rest_0_), channel_id=1, source_target_pairs={{0,16},{8,56},{16,0},{24,40},{32,48},{40,24},{48,32},{56,8},{1,17}... | collective-permute-start | bytes 1179656 | tf_op jit(solution)/shard_map/ppermute | solution.py:39
  129.9 6.7 %all-to-all-done.1.square_ref = f32[64,8,128]{2,1,0:T(8,128)S(1)} async-done(((f32[64,8,128]{2,1,0:T(8,128)}), f32[64,8,128]{2,1,0:T(8,128)S(1)}, u32[]{:S(2)}, u32[]{:S(2)}) %all-to-all-start.1) | async-done | bytes 262176 | tf_op jit(solution)/shard_map/all_to_all | solution.py:63
  137.6 1.7 %collective-permute-done.29.rest_3_ = bf16[384,512]{1,0:T(8,128)(2,1)S(1)} collective-permute-done((bf16[384,512]{1,0:T(8,128)(2,1)S(1)}, bf16[384,512]{1,0:T(8,128)(2,1)S(1)}, u32[]{:S(2)}, u32[]{:S(2)}) %collective-permute-start.29) | collective-permute-done | bytes 393248 | tf_op jit(solution)/shard_map/ppermute | solution.py:39
  139.3 3.4 %shard_map.101 = f32[1536,512]{1,0:T(8,128)} custom-call(s32[8]{0:T(128)S(1)} %broadcast_multiply_fusion.starts_ref, f32[64,8,128]{2,1,0:T(8,128)S(1)} %all-to-all-done.1.square_ref, f32[1536,512]{1,0:T(8,128)} %get-tuple-element.72.w_hbm, bf16[384,512]{1,0:T(8,128)(2,1)S(1)} %constant_dynamic-update-slice_fusion.2.rest_0_, ...), custom_call_target="tpu_custom_call" | custom-call | tf_op jit(solution)/shard_map/pallas_call | solution.py:307
  (74 shorter events, 15.2 us)
Async XLA Ops:
  8.2 4.7 %collective-permute-start = (bf16[768,256]{1,0:T(8,128)(2,1)S(1)}, bf16[768,256]{1,0:T(8,128)(2,1)S(1)}, u32[]{:S(2)}, u32[]{:S(2)}) collective-permute-start(bf16[768,256]{1,0:T(8,128)(2,1)S(1)} %get-tuple-element.39), channel_id=1, source_target_pairs={{0,8},{8,0},{1,9},{9,1},{2,10},{10,2},{3,11},{11,3},{4,12},{12,4},... | collective-permute-start | bytes 1179656 | tf_op jit(solution)/shard_map/ppermute | solution.py:39
  11.6 2.2 %collective-permute-start.4 = (bf16[768,256]{1,0:T(8,128)(2,1)S(1)}, bf16[768,256]{1,0:T(8,128)(2,1)S(1)}, u32[]{:S(2)}, u32[]{:S(2)}) collective-permute-start(bf16[768,256]{1,0:T(8,128)(2,1)S(1)} %get-tuple-element.41), channel_id=1, source_target_pairs={{0,8},{8,0},{1,9},{9,1},{2,10},{10,2},{3,11},{11,3},{4,12},{12,4},... | collective-permute-start | bytes 1179656 | tf_op jit(solution)/shard_map/ppermute | solution.py:39
  13.0 5.8 %collective-permute-start.1 = (bf16[384,256]{1,0:T(8,128)(2,1)S(1)}, bf16[384,256]{1,0:T(8,128)(2,1)S(1)}, u32[]{:S(2)}, u32[]{:S(2)}) collective-permute-start(bf16[384,256]{1,0:T(8,128)(2,1)S(1)} %add_convert_fusion.3), channel_id=1, source_target_pairs={{0,16},{8,56},{16,0},{24,40},{32,48},{40,24},{48,32},{56,8},{1,17}... | collective-permute-start | bytes 589832 | tf_op jit(solution)/shard_map/ppermute | solution.py:39
  13.8 7.0 %collective-permute-start.5 = (bf16[384,256]{1,0:T(8,128)(2,1)S(1)}, bf16[384,256]{1,0:T(8,128)(2,1)S(1)}, u32[]{:S(2)}, u32[]{:S(2)}) collective-permute-start(bf16[384,256]{1,0:T(8,128)(2,1)S(1)} %add_convert_fusion.2), channel_id=1, source_target_pairs={{0,16},{8,56},{16,0},{24,40},{32,48},{40,24},{48,32},{56,8},{1,17}... | collective-permute-start | bytes 589832 | tf_op jit(solution)/shard_map/ppermute | solution.py:39
  18.8 3.6 %collective-permute-start.2 = (bf16[192,256]{1,0:T(8,128)(2,1)S(1)}, bf16[192,256]{1,0:T(8,128)(2,1)S(1)}, u32[]{:S(2)}, u32[]{:S(2)}) collective-permute-start(bf16[192,256]{1,0:T(8,128)(2,1)S(1)} %add_convert_fusion.15), channel_id=1, source_target_pairs={{0,48},{8,24},{16,32},{24,8},{32,16},{40,56},{48,0},{56,40},{1,49}... | collective-permute-start | bytes 294920 | tf_op jit(solution)/shard_map/ppermute | solution.py:39
  20.9 5.9 %collective-permute-start.6 = (bf16[192,256]{1,0:T(8,128)(2,1)S(1)}, bf16[192,256]{1,0:T(8,128)(2,1)S(1)}, u32[]{:S(2)}, u32[]{:S(2)}) collective-permute-start(bf16[192,256]{1,0:T(8,128)(2,1)S(1)} %add_convert_fusion.12), channel_id=1, source_target_pairs={{0,48},{8,24},{16,32},{24,8},{32,16},{40,56},{48,0},{56,40},{1,49}... | collective-permute-start | bytes 294920 | tf_op jit(solution)/shard_map/ppermute | solution.py:39
  22.4 7.0 %collective-permute-start.3 = (bf16[192,256]{1,0:T(8,128)(2,1)S(1)}, bf16[192,256]{1,0:T(8,128)(2,1)S(1)}, u32[]{:S(2)}, u32[]{:S(2)}) collective-permute-start(bf16[192,256]{1,0:T(8,128)(2,1)S(1)} %add_convert_fusion.14), channel_id=1, source_target_pairs={{0,64},{8,200},{64,0},{72,136},{128,192},{136,72},{192,128},{200,8... | collective-permute-start | bytes 294920 | tf_op jit(solution)/shard_map/ppermute | solution.py:39
  26.8 5.8 %collective-permute-start.7 = (bf16[192,256]{1,0:T(8,128)(2,1)S(1)}, bf16[192,256]{1,0:T(8,128)(2,1)S(1)}, u32[]{:S(2)}, u32[]{:S(2)}) collective-permute-start(bf16[192,256]{1,0:T(8,128)(2,1)S(1)} %add_convert_fusion.11), channel_id=1, source_target_pairs={{0,64},{8,200},{64,0},{72,136},{128,192},{136,72},{192,128},{200,8... | collective-permute-start | bytes 294920 | tf_op jit(solution)/shard_map/ppermute | solution.py:39
  29.4 6.1 %collective-permute-start.8 = (bf16[192,256]{1,0:T(8,128)(2,1)S(1)}, bf16[192,256]{1,0:T(8,128)(2,1)S(1)}, u32[]{:S(2)}, u32[]{:S(2)}) collective-permute-start(bf16[192,256]{1,0:T(8,128)(2,1)S(1)} %add_convert_fusion.13.refs_0_), channel_id=1, source_target_pairs={{0,192},{8,72},{64,128},{72,8},{128,64},{136,200},{192,0},{200,136... | collective-permute-start | bytes 294920 | tf_op jit(solution)/shard_map/ppermute | solution.py:39
  32.6 4.9 %collective-permute-start.9 = (bf16[192,256]{1,0:T(8,128)(2,1)S(1)}, bf16[192,256]{1,0:T(8,128)(2,1)S(1)}, u32[]{:S(2)}, u32[]{:S(2)}) collective-permute-start(bf16[192,256]{1,0:T(8,128)(2,1)S(1)} %add_convert_fusion.10.refs_1_), channel_id=1, source_target_pairs={{0,192},{8,72},{64,128},{72,8},{128,64},{136,200},{192,0},{200,136... | collective-permute-start | bytes 294920 | tf_op jit(solution)/shard_map/ppermute | solution.py:39
  38.5 16.1 %collective-permute-start.11 = (bf16[192,512]{1,0:T(8,128)(2,1)S(1)}, bf16[192,512]{1,0:T(8,128)(2,1)S(1)}, u32[]{:S(2)}, u32[]{:S(2)}) collective-permute-start(bf16[192,512]{1,0:T(8,128)(2,1)S(1)} %get-tuple-element.45), channel_id=1, source_target_pairs={{0,48},{8,24},{16,32},{24,8},{32,16},{40,56},{48,0},{56,40},{1,49}... | collective-permute-start | bytes 589832 | tf_op jit(solution)/shard_map/ppermute | solution.py:39
  39.5 24.8 %all-to-all-start = ((f32[64,8,128]{2,1,0:T(8,128)}), f32[64,8,128]{2,1,0:T(8,128)S(1)}, u32[]{:S(2)}, u32[]{:S(2)}) async-start(f32[64,8,128]{2,1,0:T(8,128)} %get-tuple-element.46), calls=%async_computation | async-start | bytes 524288 | tf_op jit(solution)/shard_map/all_to_all | solution.py:63
  54.6 10.6 %collective-permute-start.12 = (bf16[384,512]{1,0:T(8,128)(2,1)S(1)}, bf16[384,512]{1,0:T(8,128)(2,1)S(1)}, u32[]{:S(2)}, u32[]{:S(2)}) collective-permute-start(bf16[384,512]{1,0:T(8,128)(2,1)S(1)} %constant_dynamic-update-slice_fusion.rest_0_), channel_id=1, source_target_pairs={{0,16},{8,56},{16,0},{24,40},{32,48},{40,24},{48,32},{56,8},{1,17}... | collective-permute-start | bytes 1179656 | tf_op jit(solution)/shard_map/ppermute | solution.py:39
  57.5 16.7 %collective-permute-start.10 = (bf16[640,512]{1,0:T(8,128)(2,1)}, bf16[640,512]{1,0:T(8,128)(2,1)S(1)}, u32[]{:S(2)}, u32[]{:S(2)}) collective-permute-start(bf16[640,512]{1,0:T(8,128)(2,1)} %get-tuple-element.44), channel_id=1, source_target_pairs={{0,8},{8,16},{16,24},{24,32},{32,40},{40,48},{48,56},{56,64},{64,7... | collective-permute-start | bytes 1966088 | tf_op jit(solution)/shard_map/ppermute | solution.py:373
  59.4 5.9 %collective-permute-start.13 = (bf16[384,512]{1,0:T(8,128)(2,1)S(1)}, bf16[384,512]{1,0:T(8,128)(2,1)S(1)}, u32[]{:S(2)}, u32[]{:S(2)}) collective-permute-start(bf16[384,512]{1,0:T(8,128)(2,1)S(1)} %constant_dynamic-update-slice_fusion.rest_0_), channel_id=1, source_target_pairs={{0,8},{8,0},{1,9},{9,1},{2,10},{10,2},{3,11},{11,3},{4,12},{12,4},... | collective-permute-start | bytes 1179656 | tf_op jit(solution)/shard_map/ppermute | solution.py:39
  65.2 1.7 %collective-permute-start.14 = (bf16[384,512]{1,0:T(8,128)(2,1)S(1)}, bf16[384,512]{1,0:T(8,128)(2,1)S(1)}, u32[]{:S(2)}, u32[]{:S(2)}) collective-permute-start(bf16[384,512]{1,0:T(8,128)(2,1)S(1)} %collective-permute-done.12.rest_1_), channel_id=1, source_target_pairs={{0,8},{8,0},{1,9},{9,1},{2,10},{10,2},{3,11},{11,3},{4,12},{12,4},... | collective-permute-start | bytes 1179656 | tf_op jit(solution)/shard_map/ppermute | solution.py:39
  74.2 1.8 %collective-permute-start.15 = (bf16[768,256]{1,0:T(8,128)(2,1)S(1)}, bf16[768,256]{1,0:T(8,128)(2,1)S(1)}, u32[]{:S(2)}, u32[]{:S(2)}) collective-permute-start(bf16[768,256]{1,0:T(8,128)(2,1)S(1)} %get-tuple-element.54), channel_id=1, source_target_pairs={{0,8},{8,0},{1,9},{9,1},{2,10},{10,2},{3,11},{11,3},{4,12},{12,4},... | collective-permute-start | bytes 1179656 | tf_op jit(solution)/shard_map/ppermute | solution.py:39
  74.5 5.2 %collective-permute-start.18 = (bf16[768,256]{1,0:T(8,128)(2,1)S(1)}, bf16[768,256]{1,0:T(8,128)(2,1)S(1)}, u32[]{:S(2)}, u32[]{:S(2)}) collective-permute-start(bf16[768,256]{1,0:T(8,128)(2,1)S(1)} %get-tuple-element.56), channel_id=1, source_target_pairs={{0,8},{8,0},{1,9},{9,1},{2,10},{10,2},{3,11},{11,3},{4,12},{12,4},... | collective-permute-start | bytes 1179656 | tf_op jit(solution)/shard_map/ppermute | solution.py:39
  76.1 6.7 %collective-permute-start.16 = (bf16[384,256]{1,0:T(8,128)(2,1)S(1)}, bf16[384,256]{1,0:T(8,128)(2,1)S(1)}, u32[]{:S(2)}, u32[]{:S(2)}) collective-permute-start(bf16[384,256]{1,0:T(8,128)(2,1)S(1)} %add_convert_fusion.1), channel_id=1, source_target_pairs={{0,16},{8,56},{16,0},{24,40},{32,48},{40,24},{48,32},{56,8},{1,17}... | collective-permute-start | bytes 589832 | tf_op jit(solution)/shard_map/ppermute | solution.py:39
  79.7 5.8 %collective-permute-start.19 = (bf16[384,256]{1,0:T(8,128)(2,1)S(1)}, bf16[384,256]{1,0:T(8,128)(2,1)S(1)}, u32[]{:S(2)}, u32[]{:S(2)}) collective-permute-start(bf16[384,256]{1,0:T(8,128)(2,1)S(1)} %add_convert_fusion), channel_id=1, source_target_pairs={{0,16},{8,56},{16,0},{24,40},{32,48},{40,24},{48,32},{56,8},{1,17}... | collective-permute-start | bytes 589832 | tf_op jit(solution)/shard_map/ppermute | solution.py:39
  80.2 18.5 %collective-permute-start.21 = (bf16[384,512]{1,0:T(8,128)(2,1)S(1)}, bf16[384,512]{1,0:T(8,128)(2,1)S(1)}, u32[]{:S(2)}, u32[]{:S(2)}) collective-permute-start(bf16[384,512]{1,0:T(8,128)(2,1)S(1)} %copy-done.4), channel_id=1, source_target_pairs={{0,8},{8,16},{16,24},{24,32},{32,40},{40,48},{48,56},{56,64},{64,7... | collective-permute-start | bytes 1179656 | tf_op jit(solution)/shard_map/ppermute | solution.py:354
  82.9 5.5 %collective-permute-start.17 = (bf16[192,256]{1,0:T(8,128)(2,1)S(1)}, bf16[192,256]{1,0:T(8,128)(2,1)S(1)}, u32[]{:S(2)}, u32[]{:S(2)}) collective-permute-start(bf16[192,256]{1,0:T(8,128)(2,1)S(1)} %add_convert_fusion.9), channel_id=1, source_target_pairs={{0,48},{8,24},{16,32},{24,8},{32,16},{40,56},{48,0},{56,40},{1,49}... | collective-permute-start | bytes 294920 | tf_op jit(solution)/shard_map/ppermute | solution.py:39
  85.6 11.8 %collective-permute-start.20 = (bf16[192,256]{1,0:T(8,128)(2,1)S(1)}, bf16[192,256]{1,0:T(8,128)(2,1)S(1)}, u32[]{:S(2)}, u32[]{:S(2)}) collective-permute-start(bf16[192,256]{1,0:T(8,128)(2,1)S(1)} %add_convert_fusion.7), channel_id=1, source_target_pairs={{0,48},{8,24},{16,32},{24,8},{32,16},{40,56},{48,0},{56,40},{1,49}... | collective-permute-start | bytes 294920 | tf_op jit(solution)/shard_map/ppermute | solution.py:39
  88.5 13.0 %collective-permute-start.22 = (bf16[192,256]{1,0:T(8,128)(2,1)S(1)}, bf16[192,256]{1,0:T(8,128)(2,1)S(1)}, u32[]{:S(2)}, u32[]{:S(2)}) collective-permute-start(bf16[192,256]{1,0:T(8,128)(2,1)S(1)} %add_convert_fusion.8), channel_id=1, source_target_pairs={{0,64},{8,200},{64,0},{72,136},{128,192},{136,72},{192,128},{200,8... | collective-permute-start | bytes 294920 | tf_op jit(solution)/shard_map/ppermute | solution.py:39
  97.5 8.8 %collective-permute-start.23 = (bf16[192,256]{1,0:T(8,128)(2,1)S(1)}, bf16[192,256]{1,0:T(8,128)(2,1)S(1)}, u32[]{:S(2)}, u32[]{:S(2)}) collective-permute-start(bf16[192,256]{1,0:T(8,128)(2,1)S(1)} %add_convert_fusion.6), channel_id=1, source_target_pairs={{0,64},{8,200},{64,0},{72,136},{128,192},{136,72},{192,128},{200,8... | collective-permute-start | bytes 294920 | tf_op jit(solution)/shard_map/ppermute | solution.py:39
  106.3 6.4 %collective-permute-start.25 = (bf16[192,256]{1,0:T(8,128)(2,1)S(1)}, bf16[192,256]{1,0:T(8,128)(2,1)S(1)}, u32[]{:S(2)}, u32[]{:S(2)}) collective-permute-start(bf16[192,256]{1,0:T(8,128)(2,1)S(1)} %add_convert_fusion.4.refs_1_), channel_id=1, source_target_pairs={{0,192},{8,72},{64,128},{72,8},{128,64},{136,200},{192,0},{200,136... | collective-permute-start | bytes 294920 | tf_op jit(solution)/shard_map/ppermute | solution.py:39
  106.4 6.3 %collective-permute-start.24 = (bf16[192,256]{1,0:T(8,128)(2,1)S(1)}, bf16[192,256]{1,0:T(8,128)(2,1)S(1)}, u32[]{:S(2)}, u32[]{:S(2)}) collective-permute-start(bf16[192,256]{1,0:T(8,128)(2,1)S(1)} %add_convert_fusion.5.refs_0_), channel_id=1, source_target_pairs={{0,192},{8,72},{64,128},{72,8},{128,64},{136,200},{192,0},{200,136... | collective-permute-start | bytes 294920 | tf_op jit(solution)/shard_map/ppermute | solution.py:39
  113.7 13.3 %collective-permute-start.26 = (bf16[192,512]{1,0:T(8,128)(2,1)S(1)}, bf16[192,512]{1,0:T(8,128)(2,1)S(1)}, u32[]{:S(2)}, u32[]{:S(2)}) collective-permute-start(bf16[192,512]{1,0:T(8,128)(2,1)S(1)} %get-tuple-element.69), channel_id=1, source_target_pairs={{0,48},{8,24},{16,32},{24,8},{32,16},{40,56},{48,0},{56,40},{1,49}... | collective-permute-start | bytes 589832 | tf_op jit(solution)/shard_map/ppermute | solution.py:39
  113.8 22.9 %all-to-all-start.1 = ((f32[64,8,128]{2,1,0:T(8,128)}), f32[64,8,128]{2,1,0:T(8,128)S(1)}, u32[]{:S(2)}, u32[]{:S(2)}) async-start(f32[64,8,128]{2,1,0:T(8,128)} %get-tuple-element.70), calls=%async_computation.1 | async-start | bytes 524288 | tf_op jit(solution)/shard_map/all_to_all | solution.py:63
  127.0 10.6 %collective-permute-start.27 = (bf16[384,512]{1,0:T(8,128)(2,1)S(1)}, bf16[384,512]{1,0:T(8,128)(2,1)S(1)}, u32[]{:S(2)}, u32[]{:S(2)}) collective-permute-start(bf16[384,512]{1,0:T(8,128)(2,1)S(1)} %constant_dynamic-update-slice_fusion.2.rest_0_), channel_id=1, source_target_pairs={{0,16},{8,56},{16,0},{24,40},{32,48},{40,24},{48,32},{56,8},{1,17}... | collective-permute-start | bytes 1179656 | tf_op jit(solution)/shard_map/ppermute | solution.py:39
  129.9 7.7 %collective-permute-start.28 = (bf16[384,512]{1,0:T(8,128)(2,1)S(1)}, bf16[384,512]{1,0:T(8,128)(2,1)S(1)}, u32[]{:S(2)}, u32[]{:S(2)}) collective-permute-start(bf16[384,512]{1,0:T(8,128)(2,1)S(1)} %constant_dynamic-update-slice_fusion.2.rest_0_), channel_id=1, source_target_pairs={{0,8},{8,0},{1,9},{9,1},{2,10},{10,2},{3,11},{11,3},{4,12},{12,4},... | collective-permute-start | bytes 1179656 | tf_op jit(solution)/shard_map/ppermute | solution.py:39
  137.6 1.7 %collective-permute-start.29 = (bf16[384,512]{1,0:T(8,128)(2,1)S(1)}, bf16[384,512]{1,0:T(8,128)(2,1)S(1)}, u32[]{:S(2)}, u32[]{:S(2)}) collective-permute-start(bf16[384,512]{1,0:T(8,128)(2,1)S(1)} %collective-permute-done.27.rest_1_), channel_id=1, source_target_pairs={{0,8},{8,0},{1,9},{9,1},{2,10},{10,2},{3,11},{11,3},{4,12},{12,4},... | collective-permute-start | bytes 1179656 | tf_op jit(solution)/shard_map/ppermute | solution.py:39
  (5 other events, 107.2 us)

commit v7 on v6

--- a/solution.py
+++ b/solution.py
@@ -18,7 +18,7 @@
 TILE = 256
 CHUNKS = 2
 SHARES = 64
-EARLY = 128
+EARLY = 32
 
 fast_rate = 0.01
 epsilon = 1e-06

time: 143 us -> 143 us (level)
  no operation moved by 1% of the time
where the time goes in v7:
time: 143 us
  starting transfers between devices  74.8 us (52%)
  waiting for transfers between devices  38.4 us (27%)
  Pallas kernels  25.1 us (18%)
  between operations  2.46 us (2%)
    ppermute x28, starting transfers between devices, exchange(): lax.ppermute(value, mesh_axes, [(i, partner(i)) for i in range(count)])  42.7 us
    all_to_all x2, starting transfers between devices, spread(): return lax.all_to_all(squares, ('x', 'core', 'head'), 0, 0, tiled=True)  28.3 us
    ppermute x28, waiting for transfers between devices, exchange(): lax.ppermute(value, mesh_axes, [(i, partner(i)) for i in range(count)])  27.6 us
    pallas_call x7, Pallas kernels, call(): pl.pallas_call(kernel, out_shape=outs, in_specs=specs, out_specs=jax.tree...  25.1 us
    all_to_all x2, waiting for transfers between devices, spread(): return lax.all_to_all(squares, ('x', 'core', 'head'), 0, 0, tiled=True)  10.8 us
  transfers between devices with their start and end apart: 32, of which 17 were waited for; matrix products, arithmetic and copies ran while one was open for 1% of the time, Pallas kernels for 10%

profile of v7, /device:TPU:1, one launch (start us, length us, event | category | flops | bytes accessed | tf_op | source)
XLA Modules:
  0.0 142.6 jit_solution(8639218752717354195)
XLA Ops:
  2.3 6.0 %shard_map.95 = (bf16[1536,512]{1,0:T(8,128)(2,1)}, bf16[544,512]{1,0:T(8,128)(2,1)}, bf16[480,512]{1,0:T(8,128)(2,1)}, bf16[768,256]{1,0:T(8,128)(2,1)S(1)}, bf...) custom-call(s32[1]{0:T(128)} %bitcast.1.place_ref, bf16[768,512]{1,0:T(8,128)(2,1)} %k_ref.1, ...), custom_call_target="tpu_custom_call" | custom-call | tf_op jit(solution)/shard_map/pallas_call | solution.py:307
  8.2 3.3 %collective-permute-start = (bf16[768,256]{1,0:T(8,128)(2,1)S(1)}, bf16[768,256]{1,0:T(8,128)(2,1)S(1)}, u32[]{:S(2)}, u32[]{:S(2)}) collective-permute-start(bf16[768,256]{1,0:T(8,128)(2,1)S(1)} %get-tuple-element.39), channel_id=1, source_target_pairs={{0,8},{8,0},{1,9},{9,1},{2,10},{10,2},{3,11},{11,3},{4,12},{12,4},... | collective-permute-start | bytes 1179656 | tf_op jit(solution)/shard_map/ppermute | solution.py:39
  13.8 2.0 %collective-permute-start.5 = (bf16[384,256]{1,0:T(8,128)(2,1)S(1)}, bf16[384,256]{1,0:T(8,128)(2,1)S(1)}, u32[]{:S(2)}, u32[]{:S(2)}) collective-permute-start(bf16[384,256]{1,0:T(8,128)(2,1)S(1)} %add_convert_fusion.2), channel_id=1, source_target_pairs={{0,16},{8,56},{16,0},{24,40},{32,48},{40,24},{48,32},{56,8},{1,17}... | collective-permute-start | bytes 589832 | tf_op jit(solution)/shard_map/ppermute | solution.py:39
  15.9 2.9 %collective-permute-done.1 = bf16[384,256]{1,0:T(8,128)(2,1)S(1)} collective-permute-done((bf16[384,256]{1,0:T(8,128)(2,1)S(1)}, bf16[384,256]{1,0:T(8,128)(2,1)S(1)}, u32[]{:S(2)}, u32[]{:S(2)}) %collective-permute-start.1) | collective-permute-done | bytes 196640 | tf_op jit(solution)/shard_map/ppermute | solution.py:39
  18.9 2.0 %collective-permute-done.5 = bf16[384,256]{1,0:T(8,128)(2,1)S(1)} collective-permute-done((bf16[384,256]{1,0:T(8,128)(2,1)S(1)}, bf16[384,256]{1,0:T(8,128)(2,1)S(1)}, u32[]{:S(2)}, u32[]{:S(2)}) %collective-permute-start.5) | collective-permute-done | bytes 196640 | tf_op jit(solution)/shard_map/ppermute | solution.py:39
  21.0 1.3 collective-permute-done.2
  22.4 4.4 %collective-permute-start.3 = (bf16[192,256]{1,0:T(8,128)(2,1)S(1)}, bf16[192,256]{1,0:T(8,128)(2,1)S(1)}, u32[]{:S(2)}, u32[]{:S(2)}) collective-permute-start(bf16[192,256]{1,0:T(8,128)(2,1)S(1)} %add_convert_fusion.14), channel_id=1, source_target_pairs={{0,64},{8,200},{64,0},{72,136},{128,192},{136,72},{192,128},{200,8... | collective-permute-start | bytes 294920 | tf_op jit(solution)/shard_map/ppermute | solution.py:39
  26.8 2.6 %collective-permute-start.7 = (bf16[192,256]{1,0:T(8,128)(2,1)S(1)}, bf16[192,256]{1,0:T(8,128)(2,1)S(1)}, u32[]{:S(2)}, u32[]{:S(2)}) collective-permute-start(bf16[192,256]{1,0:T(8,128)(2,1)S(1)} %add_convert_fusion.11), channel_id=1, source_target_pairs={{0,64},{8,200},{64,0},{72,136},{128,192},{136,72},{192,128},{200,8... | collective-permute-start | bytes 294920 | tf_op jit(solution)/shard_map/ppermute | solution.py:39
  29.4 1.7 %collective-permute-start.8 = (bf16[192,256]{1,0:T(8,128)(2,1)S(1)}, bf16[192,256]{1,0:T(8,128)(2,1)S(1)}, u32[]{:S(2)}, u32[]{:S(2)}) collective-permute-start(bf16[192,256]{1,0:T(8,128)(2,1)S(1)} %add_convert_fusion.13.refs_0_), channel_id=1, source_target_pairs={{0,192},{8,72},{64,128},{72,8},{128,64},{136,200},{192,0},{200,136... | collective-permute-start | bytes 294920 | tf_op jit(solution)/shard_map/ppermute | solution.py:39
  31.2 1.4 %collective-permute-done.7 = bf16[192,256]{1,0:T(8,128)(2,1)S(1)} collective-permute-done((bf16[192,256]{1,0:T(8,128)(2,1)S(1)}, bf16[192,256]{1,0:T(8,128)(2,1)S(1)}, u32[]{:S(2)}, u32[]{:S(2)}) %collective-permute-start.7) | collective-permute-done | bytes 98336 | tf_op jit(solution)/shard_map/ppermute | solution.py:39
  32.6 2.3 %collective-permute-start.9 = (bf16[192,256]{1,0:T(8,128)(2,1)S(1)}, bf16[192,256]{1,0:T(8,128)(2,1)S(1)}, u32[]{:S(2)}, u32[]{:S(2)}) collective-permute-start(bf16[192,256]{1,0:T(8,128)(2,1)S(1)} %add_convert_fusion.10.refs_1_), channel_id=1, source_target_pairs={{0,192},{8,72},{64,128},{72,8},{128,64},{136,200},{192,0},{200,136... | collective-permute-start | bytes 294920 | tf_op jit(solution)/shard_map/ppermute | solution.py:39
  35.5 2.0 %collective-permute-done.9.refs_3_ = bf16[192,256]{1,0:T(8,128)(2,1)S(1)} collective-permute-done((bf16[192,256]{1,0:T(8,128)(2,1)S(1)}, bf16[192,256]{1,0:T(8,128)(2,1)S(1)}, u32[]{:S(2)}, u32[]{:S(2)}) %collective-permute-start.9) | collective-permute-done | bytes 98336 | tf_op jit(solution)/shard_map/ppermute | solution.py:39
  39.5 15.1 %all-to-all-start = ((f32[64,8,128]{2,1,0:T(8,128)}), f32[64,8,128]{2,1,0:T(8,128)S(1)}, u32[]{:S(2)}, u32[]{:S(2)}) async-start(f32[64,8,128]{2,1,0:T(8,128)} %get-tuple-element.46), calls=%async_computation | async-start | bytes 524288 | tf_op jit(solution)/shard_map/all_to_all | solution.py:63
  54.6 2.9 %collective-permute-start.12 = (bf16[384,512]{1,0:T(8,128)(2,1)S(1)}, bf16[384,512]{1,0:T(8,128)(2,1)S(1)}, u32[]{:S(2)}, u32[]{:S(2)}) collective-permute-start(bf16[384,512]{1,0:T(8,128)(2,1)S(1)} %constant_dynamic-update-slice_fusion.rest_0_), channel_id=1, source_target_pairs={{0,16},{8,56},{16,0},{24,40},{32,48},{40,24},{48,32},{56,8},{1,17}... | collective-permute-start | bytes 1179656 | tf_op jit(solution)/shard_map/ppermute | solution.py:39
  57.5 1.9 %collective-permute-start.10 = (bf16[544,512]{1,0:T(8,128)(2,1)}, bf16[544,512]{1,0:T(8,128)(2,1)S(1)}, u32[]{:S(2)}, u32[]{:S(2)}) collective-permute-start(bf16[544,512]{1,0:T(8,128)(2,1)} %get-tuple-element.44), channel_id=1, source_target_pairs={{0,8},{8,16},{16,24},{24,32},{32,40},{40,48},{48,56},{56,64},{64,7... | collective-permute-start | bytes 1671176 | tf_op jit(solution)/shard_map/ppermute | solution.py:373
  60.2 4.0 %all-to-all-done.square_ref = f32[64,8,128]{2,1,0:T(8,128)S(1)} async-done(((f32[64,8,128]{2,1,0:T(8,128)}), f32[64,8,128]{2,1,0:T(8,128)S(1)}, u32[]{:S(2)}, u32[]{:S(2)}) %all-to-all-start) | async-done | bytes 262176 | tf_op jit(solution)/shard_map/all_to_all | solution.py:63
  65.3 1.6 %collective-permute-done.14.rest_3_ = bf16[384,512]{1,0:T(8,128)(2,1)S(1)} collective-permute-done((bf16[384,512]{1,0:T(8,128)(2,1)S(1)}, bf16[384,512]{1,0:T(8,128)(2,1)S(1)}, u32[]{:S(2)}, u32[]{:S(2)}) %collective-permute-start.14) | collective-permute-done | bytes 393248 | tf_op jit(solution)/shard_map/ppermute | solution.py:39
  66.9 7.3 %shard_map.97 = (f32[1536,512]{1,0:T(8,128)}, bf16[1536,512]{1,0:T(8,128)(2,1)S(1)}, bf16[768,256]{1,0:T(8,128)(2,1)S(1)}, bf16[768,256]{1,0:T(8,128)(2,1)S(1)},...) custom-call(s32[1]{0:T(128)} %bitcast.1.place_ref, s32[8]{0:T(128)S(1)} %broadcast_multiply_fusion.starts_ref, ...), custom_call_target="tpu_custom_call" | custom-call | tf_op jit(solution)/shard_map/pallas_call | solution.py:307
  76.1 3.6 %collective-permute-start.16 = (bf16[384,256]{1,0:T(8,128)(2,1)S(1)}, bf16[384,256]{1,0:T(8,128)(2,1)S(1)}, u32[]{:S(2)}, u32[]{:S(2)}) collective-permute-start(bf16[384,256]{1,0:T(8,128)(2,1)S(1)} %add_convert_fusion.1), channel_id=1, source_target_pairs={{0,16},{8,56},{16,0},{24,40},{32,48},{40,24},{48,32},{56,8},{1,17}... | collective-permute-start | bytes 589832 | tf_op jit(solution)/shard_map/ppermute | solution.py:39
  80.2 1.9 %collective-permute-start.21 = (bf16[480,512]{1,0:T(8,128)(2,1)S(1)}, bf16[480,512]{1,0:T(8,128)(2,1)S(1)}, u32[]{:S(2)}, u32[]{:S(2)}) collective-permute-start(bf16[480,512]{1,0:T(8,128)(2,1)S(1)} %copy-done.4), channel_id=1, source_target_pairs={{0,8},{8,16},{16,24},{24,32},{32,40},{40,48},{48,56},{56,64},{64,7... | collective-permute-start | bytes 1474568 | tf_op jit(solution)/shard_map/ppermute | solution.py:354
  82.9 1.5 %collective-permute-start.17 = (bf16[192,256]{1,0:T(8,128)(2,1)S(1)}, bf16[192,256]{1,0:T(8,128)(2,1)S(1)}, u32[]{:S(2)}, u32[]{:S(2)}) collective-permute-start(bf16[192,256]{1,0:T(8,128)(2,1)S(1)} %add_convert_fusion.9), channel_id=1, source_target_pairs={{0,48},{8,24},{16,32},{24,8},{32,16},{40,56},{48,0},{56,40},{1,49}... | collective-permute-start | bytes 294920 | tf_op jit(solution)/shard_map/ppermute | solution.py:39
  85.7 3.8 %collective-permute-done.17 = bf16[192,256]{1,0:T(8,128)(2,1)S(1)} collective-permute-done((bf16[192,256]{1,0:T(8,128)(2,1)S(1)}, bf16[192,256]{1,0:T(8,128)(2,1)S(1)}, u32[]{:S(2)}, u32[]{:S(2)}) %collective-permute-start.17) | collective-permute-done | bytes 98336 | tf_op jit(solution)/shard_map/ppermute | solution.py:39
  89.5 7.9 %collective-permute-start.22 = (bf16[192,256]{1,0:T(8,128)(2,1)S(1)}, bf16[192,256]{1,0:T(8,128)(2,1)S(1)}, u32[]{:S(2)}, u32[]{:S(2)}) collective-permute-start(bf16[192,256]{1,0:T(8,128)(2,1)S(1)} %add_convert_fusion.8), channel_id=1, source_target_pairs={{0,64},{8,200},{64,0},{72,136},{128,192},{136,72},{192,128},{200,8... | collective-permute-start | bytes 294920 | tf_op jit(solution)/shard_map/ppermute | solution.py:39
  98.5 2.8 %shard_map.98.attn_ref = f32[768,512]{1,0:T(8,128)S(1)} custom-call(s32[3]{0:T(128)S(1)} %pad_add_fusion.meta_ref, bf16[768,512]{1,0:T(8,128)(2,1)S(1)} %copy-done.2, bf16[544,512]{1,0:T(8,128)(2,1)S(1)} %collective-permute-done.10.halo_ref, bf16[768,512]{1,0:T(8,128)(2,1)S(1)} %copy-done, bf16[480,512]{1,0:T(8,128)(2,1)S(1)} %collective-permute-done.21.late_v_ref, ...), custom_call_target="tpu_custom_call" | custom-call | tf_op jit(solution)/shard_map/pallas_call | solution.py:307
  101.3 4.6 %collective-permute-done.23 = bf16[192,256]{1,0:T(8,128)(2,1)S(1)} collective-permute-done((bf16[192,256]{1,0:T(8,128)(2,1)S(1)}, bf16[192,256]{1,0:T(8,128)(2,1)S(1)}, u32[]{:S(2)}, u32[]{:S(2)}) %collective-permute-start.23) | collective-permute-done | bytes 98336 | tf_op jit(solution)/shard_map/ppermute | solution.py:39
  106.1 2.4 %collective-permute-start.24 = (bf16[192,256]{1,0:T(8,128)(2,1)S(1)}, bf16[192,256]{1,0:T(8,128)(2,1)S(1)}, u32[]{:S(2)}, u32[]{:S(2)}) collective-permute-start(bf16[192,256]{1,0:T(8,128)(2,1)S(1)} %add_convert_fusion.5.refs_0_), channel_id=1, source_target_pairs={{0,192},{8,72},{64,128},{72,8},{128,64},{136,200},{192,0},{200,136... | collective-permute-start | bytes 294920 | tf_op jit(solution)/shard_map/ppermute | solution.py:39
  108.5 3.9 %shard_map.99 = bf16[768,512]{1,0:T(8,128)(2,1)} custom-call(s32[3]{0:T(128)S(1)} %pad_add_fusion.meta_ref, bf16[768,512]{1,0:T(8,128)(2,1)S(1)} %copy-done.2, f32[768,512]{1,0:T(8,128)S(1)} %shard_map.98.attn_ref, bf16[1536,512]{1,0:T(8,128)(2,1)S(1)} %copy-done.3, bf16[1536,512]{1,0:T(8,128)(2,1)S(1)} %get-tuple-element.65.late_ref), custom_call_target="tpu_custom_call" | custom-call | tf_op jit(solution)/shard_map/pallas_call | solution.py:307
  113.4 13.3 %all-to-all-start.1 = ((f32[64,8,128]{2,1,0:T(8,128)}), f32[64,8,128]{2,1,0:T(8,128)S(1)}, u32[]{:S(2)}, u32[]{:S(2)}) async-start(f32[64,8,128]{2,1,0:T(8,128)} %get-tuple-element.70), calls=%async_computation.1 | async-start | bytes 524288 | tf_op jit(solution)/shard_map/all_to_all | solution.py:63
  126.8 2.9 %collective-permute-start.27 = (bf16[384,512]{1,0:T(8,128)(2,1)S(1)}, bf16[384,512]{1,0:T(8,128)(2,1)S(1)}, u32[]{:S(2)}, u32[]{:S(2)}) collective-permute-start(bf16[384,512]{1,0:T(8,128)(2,1)S(1)} %constant_dynamic-update-slice_fusion.2.rest_0_), channel_id=1, source_target_pairs={{0,16},{8,56},{16,0},{24,40},{32,48},{40,24},{48,32},{56,8},{1,17}... | collective-permute-start | bytes 1179656 | tf_op jit(solution)/shard_map/ppermute | solution.py:39
  129.7 6.7 %all-to-all-done.1.square_ref = f32[64,8,128]{2,1,0:T(8,128)S(1)} async-done(((f32[64,8,128]{2,1,0:T(8,128)}), f32[64,8,128]{2,1,0:T(8,128)S(1)}, u32[]{:S(2)}, u32[]{:S(2)}) %all-to-all-start.1) | async-done | bytes 262176 | tf_op jit(solution)/shard_map/all_to_all | solution.py:63
  137.3 1.7 %collective-permute-done.29.rest_3_ = bf16[384,512]{1,0:T(8,128)(2,1)S(1)} collective-permute-done((bf16[384,512]{1,0:T(8,128)(2,1)S(1)}, bf16[384,512]{1,0:T(8,128)(2,1)S(1)}, u32[]{:S(2)}, u32[]{:S(2)}) %collective-permute-start.29) | collective-permute-done | bytes 393248 | tf_op jit(solution)/shard_map/ppermute | solution.py:39
  139.1 3.4 %shard_map.101 = f32[1536,512]{1,0:T(8,128)} custom-call(s32[8]{0:T(128)S(1)} %broadcast_multiply_fusion.starts_ref, f32[64,8,128]{2,1,0:T(8,128)S(1)} %all-to-all-done.1.square_ref, f32[1536,512]{1,0:T(8,128)} %get-tuple-element.72.w_hbm, bf16[384,512]{1,0:T(8,128)(2,1)S(1)} %constant_dynamic-update-slice_fusion.2.rest_0_, ...), custom_call_target="tpu_custom_call" | custom-call | tf_op jit(solution)/shard_map/pallas_call | solution.py:307
  (74 shorter events, 15.0 us)
Async XLA Ops:
  8.2 4.7 %collective-permute-start = (bf16[768,256]{1,0:T(8,128)(2,1)S(1)}, bf16[768,256]{1,0:T(8,128)(2,1)S(1)}, u32[]{:S(2)}, u32[]{:S(2)}) collective-permute-start(bf16[768,256]{1,0:T(8,128)(2,1)S(1)} %get-tuple-element.39), channel_id=1, source_target_pairs={{0,8},{8,0},{1,9},{9,1},{2,10},{10,2},{3,11},{11,3},{4,12},{12,4},... | collective-permute-start | bytes 1179656 | tf_op jit(solution)/shard_map/ppermute | solution.py:39
  11.6 2.2 %collective-permute-start.4 = (bf16[768,256]{1,0:T(8,128)(2,1)S(1)}, bf16[768,256]{1,0:T(8,128)(2,1)S(1)}, u32[]{:S(2)}, u32[]{:S(2)}) collective-permute-start(bf16[768,256]{1,0:T(8,128)(2,1)S(1)} %get-tuple-element.41), channel_id=1, source_target_pairs={{0,8},{8,0},{1,9},{9,1},{2,10},{10,2},{3,11},{11,3},{4,12},{12,4},... | collective-permute-start | bytes 1179656 | tf_op jit(solution)/shard_map/ppermute | solution.py:39
  13.0 5.8 %collective-permute-start.1 = (bf16[384,256]{1,0:T(8,128)(2,1)S(1)}, bf16[384,256]{1,0:T(8,128)(2,1)S(1)}, u32[]{:S(2)}, u32[]{:S(2)}) collective-permute-start(bf16[384,256]{1,0:T(8,128)(2,1)S(1)} %add_convert_fusion.3), channel_id=1, source_target_pairs={{0,16},{8,56},{16,0},{24,40},{32,48},{40,24},{48,32},{56,8},{1,17}... | collective-permute-start | bytes 589832 | tf_op jit(solution)/shard_map/ppermute | solution.py:39
  13.8 7.0 %collective-permute-start.5 = (bf16[384,256]{1,0:T(8,128)(2,1)S(1)}, bf16[384,256]{1,0:T(8,128)(2,1)S(1)}, u32[]{:S(2)}, u32[]{:S(2)}) collective-permute-start(bf16[384,256]{1,0:T(8,128)(2,1)S(1)} %add_convert_fusion.2), channel_id=1, source_target_pairs={{0,16},{8,56},{16,0},{24,40},{32,48},{40,24},{48,32},{56,8},{1,17}... | collective-permute-start | bytes 589832 | tf_op jit(solution)/shard_map/ppermute | solution.py:39
  18.8 3.6 %collective-permute-start.2 = (bf16[192,256]{1,0:T(8,128)(2,1)S(1)}, bf16[192,256]{1,0:T(8,128)(2,1)S(1)}, u32[]{:S(2)}, u32[]{:S(2)}) collective-permute-start(bf16[192,256]{1,0:T(8,128)(2,1)S(1)} %add_convert_fusion.15), channel_id=1, source_target_pairs={{0,48},{8,24},{16,32},{24,8},{32,16},{40,56},{48,0},{56,40},{1,49}... | collective-permute-start | bytes 294920 | tf_op jit(solution)/shard_map/ppermute | solution.py:39
  20.9 5.9 %collective-permute-start.6 = (bf16[192,256]{1,0:T(8,128)(2,1)S(1)}, bf16[192,256]{1,0:T(8,128)(2,1)S(1)}, u32[]{:S(2)}, u32[]{:S(2)}) collective-permute-start(bf16[192,256]{1,0:T(8,128)(2,1)S(1)} %add_convert_fusion.12), channel_id=1, source_target_pairs={{0,48},{8,24},{16,32},{24,8},{32,16},{40,56},{48,0},{56,40},{1,49}... | collective-permute-start | bytes 294920 | tf_op jit(solution)/shard_map/ppermute | solution.py:39
  22.4 7.0 %collective-permute-start.3 = (bf16[192,256]{1,0:T(8,128)(2,1)S(1)}, bf16[192,256]{1,0:T(8,128)(2,1)S(1)}, u32[]{:S(2)}, u32[]{:S(2)}) collective-permute-start(bf16[192,256]{1,0:T(8,128)(2,1)S(1)} %add_convert_fusion.14), channel_id=1, source_target_pairs={{0,64},{8,200},{64,0},{72,136},{128,192},{136,72},{192,128},{200,8... | collective-permute-start | bytes 294920 | tf_op jit(solution)/shard_map/ppermute | solution.py:39
  26.8 5.8 %collective-permute-start.7 = (bf16[192,256]{1,0:T(8,128)(2,1)S(1)}, bf16[192,256]{1,0:T(8,128)(2,1)S(1)}, u32[]{:S(2)}, u32[]{:S(2)}) collective-permute-start(bf16[192,256]{1,0:T(8,128)(2,1)S(1)} %add_convert_fusion.11), channel_id=1, source_target_pairs={{0,64},{8,200},{64,0},{72,136},{128,192},{136,72},{192,128},{200,8... | collective-permute-start | bytes 294920 | tf_op jit(solution)/shard_map/ppermute | solution.py:39
  29.4 6.1 %collective-permute-start.8 = (bf16[192,256]{1,0:T(8,128)(2,1)S(1)}, bf16[192,256]{1,0:T(8,128)(2,1)S(1)}, u32[]{:S(2)}, u32[]{:S(2)}) collective-permute-start(bf16[192,256]{1,0:T(8,128)(2,1)S(1)} %add_convert_fusion.13.refs_0_), channel_id=1, source_target_pairs={{0,192},{8,72},{64,128},{72,8},{128,64},{136,200},{192,0},{200,136... | collective-permute-start | bytes 294920 | tf_op jit(solution)/shard_map/ppermute | solution.py:39
  32.6 4.9 %collective-permute-start.9 = (bf16[192,256]{1,0:T(8,128)(2,1)S(1)}, bf16[192,256]{1,0:T(8,128)(2,1)S(1)}, u32[]{:S(2)}, u32[]{:S(2)}) collective-permute-start(bf16[192,256]{1,0:T(8,128)(2,1)S(1)} %add_convert_fusion.10.refs_1_), channel_id=1, source_target_pairs={{0,192},{8,72},{64,128},{72,8},{128,64},{136,200},{192,0},{200,136... | collective-permute-start | bytes 294920 | tf_op jit(solution)/shard_map/ppermute | solution.py:39
  38.5 16.1 %collective-permute-start.11 = (bf16[192,512]{1,0:T(8,128)(2,1)S(1)}, bf16[192,512]{1,0:T(8,128)(2,1)S(1)}, u32[]{:S(2)}, u32[]{:S(2)}) collective-permute-start(bf16[192,512]{1,0:T(8,128)(2,1)S(1)} %get-tuple-element.45), channel_id=1, source_target_pairs={{0,48},{8,24},{16,32},{24,8},{32,16},{40,56},{48,0},{56,40},{1,49}... | collective-permute-start | bytes 589832 | tf_op jit(solution)/shard_map/ppermute | solution.py:39
  39.5 24.8 %all-to-all-start = ((f32[64,8,128]{2,1,0:T(8,128)}), f32[64,8,128]{2,1,0:T(8,128)S(1)}, u32[]{:S(2)}, u32[]{:S(2)}) async-start(f32[64,8,128]{2,1,0:T(8,128)} %get-tuple-element.46), calls=%async_computation | async-start | bytes 524288 | tf_op jit(solution)/shard_map/all_to_all | solution.py:63
  54.6 10.6 %collective-permute-start.12 = (bf16[384,512]{1,0:T(8,128)(2,1)S(1)}, bf16[384,512]{1,0:T(8,128)(2,1)S(1)}, u32[]{:S(2)}, u32[]{:S(2)}) collective-permute-start(bf16[384,512]{1,0:T(8,128)(2,1)S(1)} %constant_dynamic-update-slice_fusion.rest_0_), channel_id=1, source_target_pairs={{0,16},{8,56},{16,0},{24,40},{32,48},{40,24},{48,32},{56,8},{1,17}... | collective-permute-start | bytes 1179656 | tf_op jit(solution)/shard_map/ppermute | solution.py:39
  57.5 16.7 %collective-permute-start.10 = (bf16[544,512]{1,0:T(8,128)(2,1)}, bf16[544,512]{1,0:T(8,128)(2,1)S(1)}, u32[]{:S(2)}, u32[]{:S(2)}) collective-permute-start(bf16[544,512]{1,0:T(8,128)(2,1)} %get-tuple-element.44), channel_id=1, source_target_pairs={{0,8},{8,16},{16,24},{24,32},{32,40},{40,48},{48,56},{56,64},{64,7... | collective-permute-start | bytes 1671176 | tf_op jit(solution)/shard_map/ppermute | solution.py:373
  59.4 5.9 %collective-permute-start.13 = (bf16[384,512]{1,0:T(8,128)(2,1)S(1)}, bf16[384,512]{1,0:T(8,128)(2,1)S(1)}, u32[]{:S(2)}, u32[]{:S(2)}) collective-permute-start(bf16[384,512]{1,0:T(8,128)(2,1)S(1)} %constant_dynamic-update-slice_fusion.rest_0_), channel_id=1, source_target_pairs={{0,8},{8,0},{1,9},{9,1},{2,10},{10,2},{3,11},{11,3},{4,12},{12,4},... | collective-permute-start | bytes 1179656 | tf_op jit(solution)/shard_map/ppermute | solution.py:39
  65.2 1.7 %collective-permute-start.14 = (bf16[384,512]{1,0:T(8,128)(2,1)S(1)}, bf16[384,512]{1,0:T(8,128)(2,1)S(1)}, u32[]{:S(2)}, u32[]{:S(2)}) collective-permute-start(bf16[384,512]{1,0:T(8,128)(2,1)S(1)} %collective-permute-done.12.rest_1_), channel_id=1, source_target_pairs={{0,8},{8,0},{1,9},{9,1},{2,10},{10,2},{3,11},{11,3},{4,12},{12,4},... | collective-permute-start | bytes 1179656 | tf_op jit(solution)/shard_map/ppermute | solution.py:39
  74.2 1.8 %collective-permute-start.15 = (bf16[768,256]{1,0:T(8,128)(2,1)S(1)}, bf16[768,256]{1,0:T(8,128)(2,1)S(1)}, u32[]{:S(2)}, u32[]{:S(2)}) collective-permute-start(bf16[768,256]{1,0:T(8,128)(2,1)S(1)} %get-tuple-element.54), channel_id=1, source_target_pairs={{0,8},{8,0},{1,9},{9,1},{2,10},{10,2},{3,11},{11,3},{4,12},{12,4},... | collective-permute-start | bytes 1179656 | tf_op jit(solution)/shard_map/ppermute | solution.py:39
  74.5 5.2 %collective-permute-start.18 = (bf16[768,256]{1,0:T(8,128)(2,1)S(1)}, bf16[768,256]{1,0:T(8,128)(2,1)S(1)}, u32[]{:S(2)}, u32[]{:S(2)}) collective-permute-start(bf16[768,256]{1,0:T(8,128)(2,1)S(1)} %get-tuple-element.56), channel_id=1, source_target_pairs={{0,8},{8,0},{1,9},{9,1},{2,10},{10,2},{3,11},{11,3},{4,12},{12,4},... | collective-permute-start | bytes 1179656 | tf_op jit(solution)/shard_map/ppermute | solution.py:39
  76.1 6.7 %collective-permute-start.16 = (bf16[384,256]{1,0:T(8,128)(2,1)S(1)}, bf16[384,256]{1,0:T(8,128)(2,1)S(1)}, u32[]{:S(2)}, u32[]{:S(2)}) collective-permute-start(bf16[384,256]{1,0:T(8,128)(2,1)S(1)} %add_convert_fusion.1), channel_id=1, source_target_pairs={{0,16},{8,56},{16,0},{24,40},{32,48},{40,24},{48,32},{56,8},{1,17}... | collective-permute-start | bytes 589832 | tf_op jit(solution)/shard_map/ppermute | solution.py:39
  79.7 5.8 %collective-permute-start.19 = (bf16[384,256]{1,0:T(8,128)(2,1)S(1)}, bf16[384,256]{1,0:T(8,128)(2,1)S(1)}, u32[]{:S(2)}, u32[]{:S(2)}) collective-permute-start(bf16[384,256]{1,0:T(8,128)(2,1)S(1)} %add_convert_fusion), channel_id=1, source_target_pairs={{0,16},{8,56},{16,0},{24,40},{32,48},{40,24},{48,32},{56,8},{1,17}... | collective-permute-start | bytes 589832 | tf_op jit(solution)/shard_map/ppermute | solution.py:39
  80.2 18.3 %collective-permute-start.21 = (bf16[480,512]{1,0:T(8,128)(2,1)S(1)}, bf16[480,512]{1,0:T(8,128)(2,1)S(1)}, u32[]{:S(2)}, u32[]{:S(2)}) collective-permute-start(bf16[480,512]{1,0:T(8,128)(2,1)S(1)} %copy-done.4), channel_id=1, source_target_pairs={{0,8},{8,16},{16,24},{24,32},{32,40},{40,48},{48,56},{56,64},{64,7... | collective-permute-start | bytes 1474568 | tf_op jit(solution)/shard_map/ppermute | solution.py:354
  82.9 6.6 %collective-permute-start.17 = (bf16[192,256]{1,0:T(8,128)(2,1)S(1)}, bf16[192,256]{1,0:T(8,128)(2,1)S(1)}, u32[]{:S(2)}, u32[]{:S(2)}) collective-permute-start(bf16[192,256]{1,0:T(8,128)(2,1)S(1)} %add_convert_fusion.9), channel_id=1, source_target_pairs={{0,48},{8,24},{16,32},{24,8},{32,16},{40,56},{48,0},{56,40},{1,49}... | collective-permute-start | bytes 294920 | tf_op jit(solution)/shard_map/ppermute | solution.py:39
  85.6 11.8 %collective-permute-start.20 = (bf16[192,256]{1,0:T(8,128)(2,1)S(1)}, bf16[192,256]{1,0:T(8,128)(2,1)S(1)}, u32[]{:S(2)}, u32[]{:S(2)}) collective-permute-start(bf16[192,256]{1,0:T(8,128)(2,1)S(1)} %add_convert_fusion.7), channel_id=1, source_target_pairs={{0,48},{8,24},{16,32},{24,8},{32,16},{40,56},{48,0},{56,40},{1,49}... | collective-permute-start | bytes 294920 | tf_op jit(solution)/shard_map/ppermute | solution.py:39
  89.5 11.8 %collective-permute-start.22 = (bf16[192,256]{1,0:T(8,128)(2,1)S(1)}, bf16[192,256]{1,0:T(8,128)(2,1)S(1)}, u32[]{:S(2)}, u32[]{:S(2)}) collective-permute-start(bf16[192,256]{1,0:T(8,128)(2,1)S(1)} %add_convert_fusion.8), channel_id=1, source_target_pairs={{0,64},{8,200},{64,0},{72,136},{128,192},{136,72},{192,128},{200,8... | collective-permute-start | bytes 294920 | tf_op jit(solution)/shard_map/ppermute | solution.py:39
  97.5 8.5 %collective-permute-start.23 = (bf16[192,256]{1,0:T(8,128)(2,1)S(1)}, bf16[192,256]{1,0:T(8,128)(2,1)S(1)}, u32[]{:S(2)}, u32[]{:S(2)}) collective-permute-start(bf16[192,256]{1,0:T(8,128)(2,1)S(1)} %add_convert_fusion.6), channel_id=1, source_target_pairs={{0,64},{8,200},{64,0},{72,136},{128,192},{136,72},{192,128},{200,8... | collective-permute-start | bytes 294920 | tf_op jit(solution)/shard_map/ppermute | solution.py:39
  106.0 6.4 %collective-permute-start.25 = (bf16[192,256]{1,0:T(8,128)(2,1)S(1)}, bf16[192,256]{1,0:T(8,128)(2,1)S(1)}, u32[]{:S(2)}, u32[]{:S(2)}) collective-permute-start(bf16[192,256]{1,0:T(8,128)(2,1)S(1)} %add_convert_fusion.4.refs_1_), channel_id=1, source_target_pairs={{0,192},{8,72},{64,128},{72,8},{128,64},{136,200},{192,0},{200,136... | collective-permute-start | bytes 294920 | tf_op jit(solution)/shard_map/ppermute | solution.py:39
  106.1 6.3 %collective-permute-start.24 = (bf16[192,256]{1,0:T(8,128)(2,1)S(1)}, bf16[192,256]{1,0:T(8,128)(2,1)S(1)}, u32[]{:S(2)}, u32[]{:S(2)}) collective-permute-start(bf16[192,256]{1,0:T(8,128)(2,1)S(1)} %add_convert_fusion.5.refs_0_), channel_id=1, source_target_pairs={{0,192},{8,72},{64,128},{72,8},{128,64},{136,200},{192,0},{200,136... | collective-permute-start | bytes 294920 | tf_op jit(solution)/shard_map/ppermute | solution.py:39
  113.3 13.4 %collective-permute-start.26 = (bf16[192,512]{1,0:T(8,128)(2,1)S(1)}, bf16[192,512]{1,0:T(8,128)(2,1)S(1)}, u32[]{:S(2)}, u32[]{:S(2)}) collective-permute-start(bf16[192,512]{1,0:T(8,128)(2,1)S(1)} %get-tuple-element.69), channel_id=1, source_target_pairs={{0,48},{8,24},{16,32},{24,8},{32,16},{40,56},{48,0},{56,40},{1,49}... | collective-permute-start | bytes 589832 | tf_op jit(solution)/shard_map/ppermute | solution.py:39
  113.4 23.0 %all-to-all-start.1 = ((f32[64,8,128]{2,1,0:T(8,128)}), f32[64,8,128]{2,1,0:T(8,128)S(1)}, u32[]{:S(2)}, u32[]{:S(2)}) async-start(f32[64,8,128]{2,1,0:T(8,128)} %get-tuple-element.70), calls=%async_computation.1 | async-start | bytes 524288 | tf_op jit(solution)/shard_map/all_to_all | solution.py:63
  126.8 10.6 %collective-permute-start.27 = (bf16[384,512]{1,0:T(8,128)(2,1)S(1)}, bf16[384,512]{1,0:T(8,128)(2,1)S(1)}, u32[]{:S(2)}, u32[]{:S(2)}) collective-permute-start(bf16[384,512]{1,0:T(8,128)(2,1)S(1)} %constant_dynamic-update-slice_fusion.2.rest_0_), channel_id=1, source_target_pairs={{0,16},{8,56},{16,0},{24,40},{32,48},{40,24},{48,32},{56,8},{1,17}... | collective-permute-start | bytes 1179656 | tf_op jit(solution)/shard_map/ppermute | solution.py:39
  129.7 7.7 %collective-permute-start.28 = (bf16[384,512]{1,0:T(8,128)(2,1)S(1)}, bf16[384,512]{1,0:T(8,128)(2,1)S(1)}, u32[]{:S(2)}, u32[]{:S(2)}) collective-permute-start(bf16[384,512]{1,0:T(8,128)(2,1)S(1)} %constant_dynamic-update-slice_fusion.2.rest_0_), channel_id=1, source_target_pairs={{0,8},{8,0},{1,9},{9,1},{2,10},{10,2},{3,11},{11,3},{4,12},{12,4},... | collective-permute-start | bytes 1179656 | tf_op jit(solution)/shard_map/ppermute | solution.py:39
  137.3 1.7 %collective-permute-start.29 = (bf16[384,512]{1,0:T(8,128)(2,1)S(1)}, bf16[384,512]{1,0:T(8,128)(2,1)S(1)}, u32[]{:S(2)}, u32[]{:S(2)}) collective-permute-start(bf16[384,512]{1,0:T(8,128)(2,1)S(1)} %collective-permute-done.27.rest_1_), channel_id=1, source_target_pairs={{0,8},{8,0},{1,9},{9,1},{2,10},{10,2},{3,11},{11,3},{4,12},{12,4},... | collective-permute-start | bytes 1179656 | tf_op jit(solution)/shard_map/ppermute | solution.py:39
  (5 other events, 105.3 us)
